TPU v7x, 32 devices: a whole 2x2x4 slice. The times are simulated.
32 devices in a mesh: rep: 2 (over x), shard: 4 (over z), seq: 4 (over y, core).
Axes of the slice: x: 2, y: 2, z: 4, core: 2. Of those that a mesh axis runs over, the one named last changes fastest.
Arguments:
- x_img: bfloat16 [16, 896, 1536], P(('rep', 'shard'), 'seq'), may hold values from -6 to 6
- x_txt: bfloat16 [16, 128, 1536], P(('rep', 'shard'), 'seq'), may hold values from -6 to 6
- cond: bfloat16 [16, 1536], P('rep'), may hold values from -6 to 6
- counts: int32 [8], P(('rep', 'shard')), may hold values from 1 to 2, as said below
- ct_img: bfloat16 [16, 896, 1536], P(('rep', 'shard'), 'seq'), may hold values from -6 to 6
- ct_txt: bfloat16 [16, 128, 1536], P(('rep', 'shard'), 'seq'), may hold values from -6 to 6
- ada_w: bfloat16 [2, 1536, 9216], P(None, ('shard', 'seq')), may hold values from -0.15625 to 0.15625
- ada_b: bfloat16 [2, 9216], P(None, ('shard', 'seq')), may hold values from -4 to 4
- qkv_w: bfloat16 [2, 1536, 4608], P(None, ('shard', 'seq')), may hold values from -0.15625 to 0.15625
- qv_b: bfloat16 [2, 3072], P(None, ('shard', 'seq')), may hold values from -1.5 to 1.5
- proj_w: bfloat16 [2, 1536, 1536], P(None, ('shard', 'seq')), may hold values from -1.5 to 1.5
- proj_b: bfloat16 [2, 1536], P(None, ('shard', 'seq')), may hold values from -1.5 to 1.5
- fc1_w: bfloat16 [2, 1536, 6144], P(None, ('shard', 'seq')), may hold values from -0.15625 to 0.15625
- fc1_b: bfloat16 [2, 6144], P(None, ('shard', 'seq')), may hold values from -1.5 to 1.5
- fc2_w: bfloat16 [2, 6144, 1536], P(None, ('shard', 'seq')), may hold values from -0.078125 to 0.078125
- fc2_b: bfloat16 [2, 1536], P(None, ('shard', 'seq')), may hold values from -1.5 to 1.5
Outputs:
- y_img: bfloat16 [16, 896, 1536], P(('rep', 'shard'), 'seq')
- y_txt: bfloat16 [16, 128, 1536], P(('rep', 'shard'), 'seq')
- dx_img: float32 [16, 896, 1536], P(('rep', 'shard'), 'seq')
- dx_txt: float32 [16, 128, 1536], P(('rep', 'shard'), 'seq')
- d_cond: float32 [16, 1536], P('rep')
- g_ada_w: float32 [2, 1536, 9216], P(None, ('shard', 'seq'))
- g_ada_b: float32 [2, 9216], P(None, ('shard', 'seq'))
- g_qkv_w: float32 [2, 1536, 4608], P(None, ('shard', 'seq'))
- g_qv_b: float32 [2, 3072], P(None, ('shard', 'seq'))
- g_proj_w: float32 [2, 1536, 1536], P(None, ('shard', 'seq'))
- g_proj_b: float32 [2, 1536], P(None, ('shard', 'seq'))
- g_fc1_w: float32 [2, 1536, 6144], P(None, ('shard', 'seq'))
- g_fc1_b: float32 [2, 6144], P(None, ('shard', 'seq'))
- g_fc2_w: float32 [2, 6144, 1536], P(None, ('shard', 'seq'))
- g_fc2_b: float32 [2, 1536], P(None, ('shard', 'seq'))
Inputs may be any that keep to these rules, and one draw needn't show every extreme that they name: `counts`: each of the 8 groups has between 1 and 2 live sequences; some group is full and some has one.
All inputs are finite; a program needn't handle non-finite values.
Results may differ from a plain program's by a relative error of at most 0.0165.
The roundings to bfloat16 on the way count: a program that leaves them out, or rounds other values in their place, can miss the bound.
Values may be sent and summed in bfloat16 or wider, within the bound.
No kernel may reach another device: no remote copies, remote signals or barrier semaphores. Data moves between devices by JAX's collectives and lax.ppermute only.
A program may use at most 640 MiB of HBM per device.

v0:
```python
from functools import partial

import jax
import jax.numpy as jnp
from jax import lax
from jax.sharding import PartitionSpec as P

HD = 64


def normalize(values):
    centre = jnp.mean(values, axis=-1, keepdims=True)
    offset = values - centre
    spread = jnp.mean(offset * offset, axis=-1, keepdims=True)
    return offset * lax.rsqrt(spread + 1e-06)


def gelu_tanh(values):
    return jax.nn.gelu(values, approximate=True)


def attend_forward(packed, score_scale):
    query_heads = packed[:, 0]
    key_heads = packed[:, 1]
    value_heads = packed[:, 2]
    raw_scores = (
        jnp.einsum("qhd,khd->hqk", query_heads, key_heads, preferred_element_type=jnp.float32)
        * score_scale
    )
    row_max = jnp.max(raw_scores, axis=-1, keepdims=True)
    row_total = jnp.sum(jnp.exp(raw_scores - row_max), axis=-1, keepdims=True)
    log_total = row_max + jnp.log(row_total)
    weights = jnp.exp(raw_scores - log_total).astype(jnp.bfloat16)
    mixed_out = jnp.einsum("hqk,khd->qhd", weights, value_heads, preferred_element_type=jnp.float32)
    return (mixed_out.astype(jnp.bfloat16), log_total[:, :, 0])


def attend_backward(items, score_scale):
    packed, log_total, grad_mixed = items
    query_heads = packed[:, 0]
    key_heads = packed[:, 1]
    value_heads = packed[:, 2]
    raw_scores = (
        jnp.einsum("qhd,khd->hqk", query_heads, key_heads, preferred_element_type=jnp.float32)
        * score_scale
    )
    shifted = raw_scores - log_total[:, :, None]
    weights = jnp.exp(shifted).astype(jnp.bfloat16)
    grad_value = jnp.einsum("hqk,qhd->khd", weights, grad_mixed, preferred_element_type=jnp.float32)
    grad_prob = jnp.einsum(
        "qhd,khd->hqk", grad_mixed, value_heads, preferred_element_type=jnp.float32
    )
    row_delta = jnp.sum(jnp.exp(shifted) * grad_prob, axis=-1, keepdims=True)
    grad_raw = (jnp.exp(shifted) * (grad_prob - row_delta) * score_scale).astype(jnp.bfloat16)
    grad_query = jnp.einsum("hqk,khd->qhd", grad_raw, key_heads, preferred_element_type=jnp.float32)
    grad_key = jnp.einsum("hqk,qhd->khd", grad_raw, query_heads, preferred_element_type=jnp.float32)
    return jnp.stack([grad_query, grad_key, grad_value], axis=1).astype(jnp.bfloat16)


def outer_sum(left, right):
    return jnp.einsum("ctd,cte->de", left, right, preferred_element_type=jnp.float32)


def column_total(values):
    return jnp.sum(values.astype(jnp.float32), axis=(0, 1))


def on_device(
    x_img,
    x_txt,
    cond,
    counts,
    ct_img,
    ct_txt,
    ada_w,
    ada_b,
    qkv_w,
    qv_b,
    proj_w,
    proj_b,
    fc1_w,
    fc1_b,
    fc2_w,
    fc2_b,
):
    slot_count = x_img.shape[0]
    model_width = x_img.shape[2]
    text_rows = x_txt.shape[1]
    seq_count = lax.axis_size("seq")
    shard_id = lax.axis_index("shard")
    owner_id = shard_id * seq_count + lax.axis_index("seq")
    own_rows = ada_w.shape[1]
    bias_cols = ada_b.shape[1]
    rep_rows = cond.shape[0]
    score_scale = HD ** (-0.5)
    live_mask = (jnp.arange(slot_count, dtype=jnp.int32) < counts[0]).astype(jnp.float32)[
        :, None, None
    ]
    cond_value = cond.astype(jnp.float32)
    silu_cond = jax.nn.silu(cond_value).astype(jnp.bfloat16)
    silu_own = lax.dynamic_slice_in_dim(silu_cond, owner_id * own_rows, own_rows, 1)
    partial_mod = jnp.einsum("sd,jdm->jsm", silu_own, ada_w, preferred_element_type=jnp.float32)
    bias_full = lax.dynamic_update_slice_in_dim(
        jnp.zeros((2, 6 * model_width), jnp.float32),
        ada_b.astype(jnp.float32),
        owner_id * bias_cols,
        1,
    )
    mod_rep = lax.psum(partial_mod + bias_full[:, None, :], ("shard", "seq"))
    modulation = lax.dynamic_slice_in_dim(mod_rep, shard_id * slot_count, slot_count, 1).reshape(
        2, slot_count, 6, model_width
    )
    qkv_full, qv_full, proj_full, projb_full, up_full, upb_full, down_full, downb_full = (
        lax.all_gather(qkv_w, ("shard", "seq"), axis=1, tiled=True),
        lax.all_gather(qv_b, ("shard", "seq"), axis=1, tiled=True),
        lax.all_gather(proj_w, ("shard", "seq"), axis=1, tiled=True),
        lax.all_gather(proj_b, ("shard", "seq"), axis=1, tiled=True),
        lax.all_gather(fc1_w, ("shard", "seq"), axis=1, tiled=True),
        lax.all_gather(fc1_b, ("shard", "seq"), axis=1, tiled=True),
        lax.all_gather(fc2_w, ("shard", "seq"), axis=1, tiled=True),
        lax.all_gather(fc2_b, ("shard", "seq"), axis=1, tiled=True),
    )
    inputs = (x_img.astype(jnp.float32), x_txt.astype(jnp.float32))
    normed_list = []
    hidden_list = []
    qkv_list = []
    for stream in range(2):
        stream_mod = modulation[stream]
        normed = normalize(inputs[stream])
        hidden = (normed * (1.0 + stream_mod[:, 1:2]) + stream_mod[:, 0:1]).astype(jnp.bfloat16)
        qkv_bias = jnp.concatenate(
            [
                qv_full[stream, :model_width],
                jnp.zeros((model_width,), qv_full.dtype),
                qv_full[stream, model_width:],
            ]
        ).astype(jnp.float32)
        projected = (
            jnp.einsum("ctd,de->cte", hidden, qkv_full[stream], preferred_element_type=jnp.float32)
            + qkv_bias
        )
        normed_list.append(normed)
        hidden_list.append(hidden)
        qkv_list.append(projected.astype(jnp.bfloat16))
    joint_tokens = jnp.concatenate([qkv_list[1], qkv_list[0]], axis=1)
    local_tokens = joint_tokens.shape[1]
    group_cols = model_width // seq_count
    head_count = group_cols // HD
    heads_layout = lax.all_to_all(
        joint_tokens.reshape(slot_count, local_tokens, 3, seq_count, group_cols),
        "seq",
        split_axis=3,
        concat_axis=1,
        tiled=True,
    )
    full_tokens = heads_layout.shape[1]
    heads_packed = heads_layout.reshape(slot_count, full_tokens, 3, head_count, HD)
    mixed_heads, log_totals = lax.map(
        partial(attend_forward, score_scale=score_scale), heads_packed
    )
    back_tokens = lax.all_to_all(
        mixed_heads.reshape(slot_count, full_tokens, group_cols),
        "seq",
        split_axis=1,
        concat_axis=2,
        tiled=True,
    )
    attn_parts = (back_tokens[:, text_rows:], back_tokens[:, :text_rows])
    out_list = []
    after_list = []
    normed_two_list = []
    hidden_two_list = []
    pre_list = []
    act_list = []
    mlp_list = []
    results = []
    for stream in range(2):
        stream_mod = modulation[stream]
        attn_out = jnp.einsum(
            "ctd,de->cte", attn_parts[stream], proj_full[stream], preferred_element_type=jnp.float32
        ) + projb_full[stream].astype(jnp.float32)
        after_attn = inputs[stream] + stream_mod[:, 2:3] * attn_out
        normed_two = normalize(after_attn)
        hidden_two = (normed_two * (1.0 + stream_mod[:, 4:5]) + stream_mod[:, 3:4]).astype(
            jnp.bfloat16
        )
        pre_act = jnp.einsum(
            "ctd,df->ctf", hidden_two, up_full[stream], preferred_element_type=jnp.float32
        ) + upb_full[stream].astype(jnp.float32)
        activated = gelu_tanh(pre_act).astype(jnp.bfloat16)
        mlp_out = jnp.einsum(
            "ctf,fd->ctd", activated, down_full[stream], preferred_element_type=jnp.float32
        ) + downb_full[stream].astype(jnp.float32)
        results.append(
            ((after_attn + stream_mod[:, 5:6] * mlp_out) * live_mask).astype(jnp.bfloat16)
        )
        out_list.append(attn_out)
        after_list.append(after_attn)
        normed_two_list.append(normed_two)
        hidden_two_list.append(hidden_two)
        pre_list.append(pre_act)
        act_list.append(activated)
        mlp_list.append(mlp_out)
    up_used, down_used = (
        lax.all_gather(fc1_w, ("shard", "seq"), axis=1, tiled=True),
        lax.all_gather(fc2_w, ("shard", "seq"), axis=1, tiled=True),
    )
    cotangents = (ct_img, ct_txt)
    grad_mlp_list = []
    grad_pre_list = []
    grad_after_list = []
    late_mods = []
    for stream in range(2):
        stream_mod = modulation[stream]
        grad_y = cotangents[stream].astype(jnp.float32) * live_mask
        grad_mlp = (stream_mod[:, 5:6] * grad_y).astype(jnp.bfloat16)
        grad_gate_two = jnp.sum(mlp_list[stream] * grad_y, axis=1)
        grad_act = jnp.einsum(
            "ctd,fd->ctf", grad_mlp, down_used[stream], preferred_element_type=jnp.float32
        )
        grad_pre = jax.vjp(gelu_tanh, pre_list[stream])[1](grad_act)[0].astype(jnp.bfloat16)
        grad_hidden_two = jnp.einsum(
            "ctf,df->ctd", grad_pre, up_used[stream], preferred_element_type=jnp.float32
        )
        grad_shift_two = jnp.sum(grad_hidden_two, axis=1)
        grad_scale_two = jnp.sum(grad_hidden_two * normed_two_list[stream], axis=1)
        grad_after = (
            grad_y
            + jax.vjp(normalize, after_list[stream])[1](
                grad_hidden_two * (1.0 + stream_mod[:, 4:5])
            )[0]
        )
        grad_after_list.append(grad_after)
        grad_mlp_list.append(grad_mlp)
        grad_pre_list.append(grad_pre)
        late_mods.append((grad_shift_two, grad_scale_two, grad_gate_two))
    grad_down_all = jnp.stack([outer_sum(act_list[j], grad_mlp_list[j]) for j in range(2)])
    grad_downb_all = jnp.stack([column_total(grad_mlp_list[j]) for j in range(2)])
    grad_up_all = jnp.stack([outer_sum(hidden_two_list[j], grad_pre_list[j]) for j in range(2)])
    grad_upb_all = jnp.stack([column_total(grad_pre_list[j]) for j in range(2)])
    mlp_shards = (
        lax.psum_scatter(
            grad_up_all.astype(jnp.bfloat16), ("shard", "seq"), scatter_dimension=1, tiled=True
        ).astype(jnp.float32),
        lax.psum_scatter(
            grad_upb_all.astype(jnp.bfloat16), ("shard", "seq"), scatter_dimension=1, tiled=True
        ).astype(jnp.float32),
        lax.psum_scatter(
            grad_down_all.astype(jnp.bfloat16), ("shard", "seq"), scatter_dimension=1, tiled=True
        ).astype(jnp.float32),
        lax.psum_scatter(
            grad_downb_all.astype(jnp.bfloat16), ("shard", "seq"), scatter_dimension=1, tiled=True
        ).astype(jnp.float32),
    )
    qkv_back, proj_back = (
        lax.all_gather(qkv_w, ("shard", "seq"), axis=1, tiled=True),
        lax.all_gather(proj_w, ("shard", "seq"), axis=1, tiled=True),
    )
    grad_out_list = []
    gate_one_list = []
    grad_attn_list = []
    for stream in range(2):
        stream_mod = modulation[stream]
        grad_out = (stream_mod[:, 2:3] * grad_after_list[stream]).astype(jnp.bfloat16)
        gate_one_list.append(jnp.sum(out_list[stream] * grad_after_list[stream], axis=1))
        grad_out_list.append(grad_out)
        grad_attn_list.append(
            jnp.einsum(
                "cte,de->ctd", grad_out, proj_back[stream], preferred_element_type=jnp.float32
            ).astype(jnp.bfloat16)
        )
    grad_proj_all = jnp.stack([outer_sum(attn_parts[j], grad_out_list[j]) for j in range(2)])
    grad_projb_all = jnp.stack([column_total(grad_out_list[j]) for j in range(2)])
    grad_joint = jnp.concatenate([grad_attn_list[1], grad_attn_list[0]], axis=1)
    grad_heads = lax.all_to_all(grad_joint, "seq", split_axis=2, concat_axis=1, tiled=True).reshape(
        slot_count, full_tokens, head_count, HD
    )
    head_grads = lax.map(
        partial(attend_backward, score_scale=score_scale), (heads_packed, log_totals, grad_heads)
    )
    grad_qkv_joint = lax.all_to_all(
        head_grads.reshape(slot_count, full_tokens, 3, 1, group_cols),
        "seq",
        split_axis=1,
        concat_axis=3,
        tiled=True,
    ).reshape(slot_count, local_tokens, 3 * model_width)
    grad_parts = (grad_qkv_joint[:, text_rows:], grad_qkv_joint[:, :text_rows])
    grads_qvb = []
    input_grads = []
    dmod_streams = []
    for stream in range(2):
        stream_mod = modulation[stream]
        grad_qkv = grad_parts[stream]
        column_sums = column_total(grad_qkv)
        grads_qvb.append(
            jnp.concatenate([column_sums[:model_width], column_sums[2 * model_width :]])
        )
        grad_hidden = jnp.einsum(
            "cte,de->ctd", grad_qkv, qkv_back[stream], preferred_element_type=jnp.float32
        )
        grad_shift_one = jnp.sum(grad_hidden, axis=1)
        grad_scale_one = jnp.sum(grad_hidden * normed_list[stream], axis=1)
        input_grads.append(
            grad_after_list[stream]
            + jax.vjp(normalize, inputs[stream])[1](grad_hidden * (1.0 + stream_mod[:, 1:2]))[0]
        )
        grad_shift_two, grad_scale_two, grad_gate_two = late_mods[stream]
        stacked_mod = jnp.stack(
            [
                grad_shift_one,
                grad_scale_one,
                gate_one_list[stream],
                grad_shift_two,
                grad_scale_two,
                grad_gate_two,
            ],
            axis=1,
        )
        dmod_streams.append(stacked_mod.reshape(slot_count, 6 * model_width))
    grad_qkv_all = jnp.stack([outer_sum(hidden_list[j], grad_parts[j]) for j in range(2)])
    attn_shards = (
        lax.psum_scatter(
            grad_qkv_all.astype(jnp.bfloat16), ("shard", "seq"), scatter_dimension=1, tiled=True
        ).astype(jnp.float32),
        lax.psum_scatter(
            jnp.stack(grads_qvb).astype(jnp.bfloat16),
            ("shard", "seq"),
            scatter_dimension=1,
            tiled=True,
        ).astype(jnp.float32),
        lax.psum_scatter(
            grad_proj_all.astype(jnp.bfloat16), ("shard", "seq"), scatter_dimension=1, tiled=True
        ).astype(jnp.float32),
        lax.psum_scatter(
            grad_projb_all.astype(jnp.bfloat16), ("shard", "seq"), scatter_dimension=1, tiled=True
        ).astype(jnp.float32),
    )
    dmod_place = lax.dynamic_update_slice_in_dim(
        jnp.zeros((2, rep_rows, 6 * model_width), jnp.float32),
        jnp.stack(dmod_streams),
        shard_id * slot_count,
        1,
    )
    dmod_rep = lax.psum(dmod_place.astype(jnp.bfloat16), ("shard", "seq"))
    dsilu_part = jnp.einsum("jsm,jdm->sd", dmod_rep, ada_w, preferred_element_type=jnp.float32)
    dsilu = lax.all_gather(dsilu_part, ("shard", "seq"), axis=1, tiled=True)
    d_cond = jax.vjp(jax.nn.silu, cond_value)[1](dsilu)[0]
    silu_all, dmod_all = (
        lax.all_gather(silu_cond, "rep", axis=0, tiled=True),
        lax.all_gather(dmod_rep, "rep", axis=1, tiled=True),
    )
    silu_cols = lax.dynamic_slice_in_dim(silu_all, owner_id * own_rows, own_rows, 1)
    grad_ada_w = jnp.einsum("sd,jsm->jdm", silu_cols, dmod_all, preferred_element_type=jnp.float32)
    grad_ada_b = lax.dynamic_slice_in_dim(
        jnp.sum(dmod_all.astype(jnp.float32), axis=1), owner_id * bias_cols, bias_cols, 1
    )
    summed = (
        lax.psum(attn_shards[0].astype(jnp.bfloat16), "rep").astype(jnp.float32),
        lax.psum(attn_shards[1].astype(jnp.bfloat16), "rep").astype(jnp.float32),
        lax.psum(attn_shards[2].astype(jnp.bfloat16), "rep").astype(jnp.float32),
        lax.psum(attn_shards[3].astype(jnp.bfloat16), "rep").astype(jnp.float32),
        lax.psum(mlp_shards[0].astype(jnp.bfloat16), "rep").astype(jnp.float32),
        lax.psum(mlp_shards[1].astype(jnp.bfloat16), "rep").astype(jnp.float32),
        lax.psum(mlp_shards[2].astype(jnp.bfloat16), "rep").astype(jnp.float32),
        lax.psum(mlp_shards[3].astype(jnp.bfloat16), "rep").astype(jnp.float32),
    )
    return (
        results[0],
        results[1],
        input_grads[0],
        input_grads[1],
        d_cond,
        grad_ada_w,
        grad_ada_b,
        summed[0],
        summed[1],
        summed[2],
        summed[3],
        summed[4],
        summed[5],
        summed[6],
        summed[7],
    )


def solution(mesh):
    placed = (
        P(("rep", "shard"), "seq", None),
        P(("rep", "shard"), "seq", None),
        P("rep", None),
        P(("rep", "shard")),
        P(("rep", "shard"), "seq", None),
        P(("rep", "shard"), "seq", None),
        P(None, ("shard", "seq"), None),
        P(None, ("shard", "seq")),
        P(None, ("shard", "seq"), None),
        P(None, ("shard", "seq")),
        P(None, ("shard", "seq"), None),
        P(None, ("shard", "seq")),
        P(None, ("shard", "seq"), None),
        P(None, ("shard", "seq")),
        P(None, ("shard", "seq"), None),
        P(None, ("shard", "seq")),
    )
    return jax.shard_map(
        on_device,
        mesh=mesh,
        in_specs=placed,
        out_specs=(
            P(("rep", "shard"), "seq", None),
            P(("rep", "shard"), "seq", None),
            P(("rep", "shard"), "seq", None),
            P(("rep", "shard"), "seq", None),
            P("rep", None),
            P(None, ("shard", "seq"), None),
            P(None, ("shard", "seq")),
            P(None, ("shard", "seq"), None),
            P(None, ("shard", "seq")),
            P(None, ("shard", "seq"), None),
            P(None, ("shard", "seq")),
            P(None, ("shard", "seq"), None),
            P(None, ("shard", "seq")),
            P(None, ("shard", "seq"), None),
            P(None, ("shard", "seq")),
        ),
        check_vma=False,
    )
```

profile of v0, /device:TPU:0, one launch (start us, length us, event | category | flops | bytes accessed | tf_op | source)
XLA Modules:
  0.0 2838.1 jit_solution(15658694298256778596)
XLA Ops:
  16.7 23.1 all-gather
  48.0 60.4 %all-reduce.6.cloned.1.call-done = f32[2,8,9216]{2,1,0:T(8,128)} async-done(((f32[2,8,9216]{2,1,0:T(8,128)}), f32[2,8,9216]{2,1,0:T(8,128)}) %all-reduce.6.cloned.1.call-update) | async-done | bytes 589840 | tf_op jit(solution)/shard_map/psum | solution.py:109
  119.0 133.3 %all-gather.9.cloned.1.call-done = bf16[2,1536,4608]{2,1,0:T(8,128)(2,1)} async-done(((bf16[2,96,4608]{2,1,0:T(8,128)(2,1)}), bf16[2,1536,4608]{2,1,0:T(8,128)(2,1)}) %all-gather.9.cloned.1.call-update) | async-done | bytes 28311568 | tf_op jit(solution)/shard_map/all_gather | solution.py:114
  291.9 91.0 %all_gather.42 = bf16[2,6144]{1,0:T(2,128)(2,1)S(1)} all-gather(bf16[2,384]{1,0:T(2,128)(2,1)S(1)} %copy-done.84), channel_id=1, replica_groups=mesh['rep'=2,'shard'=4,'seq'=4] {'shard','seq'}, dimensions={1}, use_global_device_ids=true | all-gather | bytes 26112 | tf_op jit(solution)/shard_map/all_gather | solution.py:119
  400.8 73.1 %while.22 = (s32[]{:T(128)}, bf16[2,1024,6,64]{1,3,2,0:T(8,128)(2,1)}, f32[2,6,1024]{2,1,0:T(8,128)}, bf16[2,1024,3,6,64]{1,4,3,2,0:T(8,128)(2,1)}, s32[]{:T(128)}) while((s32[]{:T(128)}, bf16[2,1024,6,64]{1,3,2,0:T(8,128)(2,1)}, f32[2,6,1024]{2,1,0:T(8,128)}, bf16[2,1024,3,6,64]{1,4,3,2,0:T(8,128)(2,1)}, s32[]{:T(128)}) %tuple.99), condition=%wide.region_8.9_spmd, body=%wide.region_5.8_spmd.sunk | while | flops 1661331456 | bytes 96575672 | solution.py:158
  483.8 47.0 %all-gather.1 = bf16[16,96,2]{1,2,0:T(2,128)(2,1)S(1)} all-gather(bf16[1,96,2]{1,2,0:T(2,128)(2,1)S(1)} %bitcast.392), channel_id=1, replica_groups=mesh['rep'=2,'shard'=4,'seq'=4] {'shard','seq'}, dimensions={0}, use_global_device_ids=true | all-gather | bytes 6528 | tf_op jit(solution)/shard_map/all_gather | solution.py:117
  530.9 19.1 all-gather.2
  588.3 166.0 %all-gather.15.cloned.1.call-done = bf16[2,6144,1536]{2,1,0:T(8,128)(2,1)} async-done(((bf16[2,384,1536]{2,1,0:T(8,128)(2,1)}), bf16[2,6144,1536]{2,1,0:T(8,128)(2,1)}) %all-gather.15.cloned.1.call-update) | async-done | bytes 37748752 | tf_op jit(solution)/shard_map/all_gather | solution.py:120
  809.7 21.0 fusion.175
  846.7 27.6 multiply_reduce_fusion.2
  925.9 244.2 %while.23 = (s32[]{:T(128)}, bf16[2,1024,3,6,64]{1,4,3,2,0:T(8,128)(2,1)}, bf16[2,1024,3,6,64]{1,4,3,2,0:T(8,128)(2,1)}, f32[2,6,1024]{2,1,0:T(8,128)}, bf16[2,1024,6,64]{1,3,2,0:T(8,128)(2,1)}, /*index=5*/s32[]{:T(128)}) while((s32[]{:T(128)}, bf16[2,1024,3,6,64]{1,4,3,2,0:T(8,128)(2,1)}, bf16[2,1024,3,6,64]{1,4,3,2,0:T(8,128)(2,1)}, ...), condition=%wide.region_19.20_spmd, body=%wide.region_17.19_spmd.sunk | while | flops 4166924288 | bytes 310264960 | solution.py:278
  952.3 39.8 %fusion.209 = bf16[1,1024,1,6,64]{1,4,3,2,0:T(8,128)(2,1)} fusion(f32[6,1024,1024]{1,2,0:T(8,128)} %fusion.207, f32[6,1024,1024]{1,2,0:T(8,128)} %fusion.205, f32[6,1024]{1,0:T(8,128)} %dynamic-slice_bitcast_fusion.8, bf16[1024,3,6,64]{0,3,2,1:T(8,128)(2,1)} %copy-done.1), kind=kOutput, calls=%fused_computation.33.clone.1 | convolution fusion | flops 862329856 | bytes 102301696 | tf_op jit(solution)/shard_map/while/body/eval_jaxpr/hqk,khd->qhd/dot_general | solution.py:55
  992.1 40.6 %fusion.208 = bf16[1,1024,1,6,64]{1,4,3,2,0:T(8,128)(2,1)} fusion(f32[6,1024,1024]{1,2,0:T(8,128)} %fusion.207, f32[6,1024,1024]{1,2,0:T(8,128)} %fusion.205, f32[6,1024]{1,0:T(8,128)} %dynamic-slice_bitcast_fusion.8, bf16[1024,3,6,64]{0,3,2,1:T(8,128)(2,1)} %copy-done.1), kind=kOutput, calls=%fused_computation.32.clone.1 | convolution fusion | flops 862329856 | bytes 102301696 | tf_op jit(solution)/shard_map/while/body/eval_jaxpr/hqk,qhd->khd/dot_general | solution.py:56
  1072.5 39.9 %fusion.209 = bf16[1,1024,1,6,64]{1,4,3,2,0:T(8,128)(2,1)} fusion(f32[6,1024,1024]{1,2,0:T(8,128)} %fusion.207, f32[6,1024,1024]{1,2,0:T(8,128)} %fusion.205, f32[6,1024]{1,0:T(8,128)} %dynamic-slice_bitcast_fusion.8, bf16[1024,3,6,64]{0,3,2,1:T(8,128)(2,1)} %copy-done.1), kind=kOutput, calls=%fused_computation.33.clone.1 | convolution fusion | flops 862329856 | bytes 102301696 | tf_op jit(solution)/shard_map/while/body/eval_jaxpr/hqk,khd->qhd/dot_general | solution.py:55
  1112.3 40.6 %fusion.208 = bf16[1,1024,1,6,64]{1,4,3,2,0:T(8,128)(2,1)} fusion(f32[6,1024,1024]{1,2,0:T(8,128)} %fusion.207, f32[6,1024,1024]{1,2,0:T(8,128)} %fusion.205, f32[6,1024]{1,0:T(8,128)} %dynamic-slice_bitcast_fusion.8, bf16[1024,3,6,64]{0,3,2,1:T(8,128)(2,1)} %copy-done.1), kind=kOutput, calls=%fused_computation.32.clone.1 | convolution fusion | flops 862329856 | bytes 102301696 | tf_op jit(solution)/shard_map/while/body/eval_jaxpr/hqk,qhd->khd/dot_general | solution.py:56
  1182.6 57.6 %all_to_all.63 = bf16[2,1024,3,1,384]{4,0,3,2,1:T(2,128)(2,1)S(1)} all-to-all(bf16[2,1024,3,1,384]{4,0,3,2,1:T(2,128)(2,1)} %copy.115), channel_id=1, replica_groups=mesh['rep'=2,'shard'=4,'seq'=4] {'seq'}, dimensions={1} | all-to-all | bytes 9437184 | tf_op jit(solution)/shard_map/all_to_all | solution.py:281
  1275.3 19.5 pad_maximum_fusion.2
  1309.9 18.9 fusion.54
  1328.8 26.5 pad_maximum_fusion
  1366.2 19.2 fusion.56
  1385.4 27.0 pad_maximum_fusion.1
  1484.1 79.8 %reduce-scatter.17.cloned.1.call-done = bf16[2,96,4608]{2,1,0:T(8,128)(2,1)} async-done(((bf16[2,1536,4608]{2,1,0:T(8,128)(2,1)}), bf16[2,96,4608]{2,1,0:T(8,128)(2,1)}) %reduce-scatter.17.cloned.1.call-update) | async-done | bytes 1769488 | tf_op jit(solution)/shard_map/reduce_scatter | solution.py:323
  1563.9 371.8 %reduce-scatter.21.cloned.1.call-done = bf16[2,96,6144]{2,1,0:T(8,128)(2,1)} async-done(((bf16[2,1536,6144]{2,1,0:T(8,128)(2,1)}), bf16[2,96,6144]{2,1,0:T(8,128)(2,1)}) %reduce-scatter.21.cloned.1.call-update) | async-done | bytes 2359312 | tf_op jit(solution)/shard_map/reduce_scatter | solution.py:242
  1935.7 371.8 %reduce-scatter.23.cloned.1.call-done = bf16[2,384,1536]{2,1,0:T(8,128)(2,1)} async-done(((bf16[2,6144,1536]{2,1,0:T(8,128)(2,1)}), bf16[2,384,1536]{2,1,0:T(8,128)(2,1)}) %reduce-scatter.23.cloned.1.call-update) | async-done | bytes 2359312 | tf_op jit(solution)/shard_map/reduce_scatter | solution.py:248
  2313.0 53.5 %reduce-scatter.27.cloned.1.call-done = bf16[96,2]{1,0:T(8,128)(2,1)} async-done(((bf16[1536,2]{1,0:T(8,128)(2,1)}), bf16[96,2]{1,0:T(8,128)(2,1)}) %reduce-scatter.27.cloned.1.call-update) | async-done | bytes 400
  2367.3 57.9 %reduce-scatter.31.cloned.1.call-done = bf16[96,2]{1,0:T(8,128)(2,1)} async-done(((bf16[1536,2]{1,0:T(8,128)(2,1)}), bf16[96,2]{1,0:T(8,128)(2,1)}) %reduce-scatter.31.cloned.1.call-update) | async-done | bytes 400
  2426.0 62.2 %reduce-scatter.29.cloned.1.call-done = bf16[384,2]{1,0:T(8,128)(2,1)} async-done(((bf16[6144,2]{1,0:T(8,128)(2,1)}), bf16[384,2]{1,0:T(8,128)(2,1)}) %reduce-scatter.29.cloned.1.call-update) | async-done | bytes 1552
  2489.2 58.7 %reduce-scatter.25.cloned.1.call-done = bf16[192,2]{1,0:T(8,128)(2,1)} async-done(((bf16[3072,2]{1,0:T(8,128)(2,1)}), bf16[192,2]{1,0:T(8,128)(2,1)}) %reduce-scatter.25.cloned.1.call-update) | async-done | bytes 784
  2559.3 82.1 %all-reduce.8.cloned.1.call-done = bf16[2,8,9216]{2,1,0:T(8,128)(2,1)} async-done(((bf16[2,8,9216]{2,1,0:T(8,128)(2,1)}), bf16[2,8,9216]{2,1,0:T(8,128)(2,1)}) %all-reduce.8.cloned.1.call-update) | async-done | bytes 294928 | tf_op jit(solution)/shard_map/psum | solution.py:345
  2643.4 19.6 all-gather.3
  2665.2 16.8 all_gather.46
  2688.4 132.3 %all-reduce.10.cloned.1.call-done = (bf16[2,96,4608]{2,1,0:T(8,128)(2,1)}, bf16[2,96,1536]{2,1,0:T(8,128)(2,1)}, bf16[2,96,6144]{2,1,0:T(8,128)(2,1)}, bf16[2,384,1536]{2,1,0:T(8,128)(2,1)}) async-done(((bf16[2,96,4608]{2,1,0:T(8,128)(2,1)}, bf16[2,96,1536]{2,1,0:T(8,128)(2,1)}, bf16[2,96,6144]{2,1,0:T(8,128)(2,1)}, bf16[2,384,1536]{2,1,0:T(8,128)(2,1)}), (bf16[2,96,4608]{2,1,0:T(8,128)(2,1)}, ...) | async-done | bytes 7077904 | tf_op jit(solution)/shard_map/psum | solution.py:359
  (418 shorter events, 597.3 us)
Async XLA Ops:
  7.2 101.2 %all-reduce.6.cloned.1.call-start = ((), (), s32[]{:S(2)}) async-start(), calls=%async_computation.12 | async-start | bytes 1179648 | tf_op jit(solution)/shard_map/psum | solution.py:109
  14.0 238.4 %all-gather.9.cloned.1.call-start = ((), (), s32[]{:S(2)}) async-start(), calls=%async_computation.13 | async-start | bytes 30081024 | tf_op jit(solution)/shard_map/all_gather | solution.py:114
  14.7 548.1 %all-gather.11.cloned.1.call-start = ((), (), s32[]{:S(2)}) async-start(), calls=%async_computation.14 | async-start | bytes 10027008 | tf_op jit(solution)/shard_map/all_gather | solution.py:116
  15.5 561.5 %all-gather.13.cloned.1.call-start = ((), (), s32[]{:S(2)}) async-start(), calls=%async_computation.15 | async-start | bytes 40108032 | tf_op jit(solution)/shard_map/all_gather | solution.py:118
  16.1 738.2 %all-gather.15.cloned.1.call-start = ((), (), s32[]{:S(2)}) async-start(), calls=%async_computation.16 | async-start | bytes 40108032 | tf_op jit(solution)/shard_map/all_gather | solution.py:120
  46.3 214.0 %copy-start.51 = (f32[2,224]{1,0:T(2,128)}, f32[2,224]{1,0:T(2,128)S(1)}, u32[]{:S(2)}) copy-start(f32[2,224]{1,0:T(2,128)S(1)} %broadcast_multiply_fusion.1) | copy-start | bytes 5380
  118.4 141.9 %copy-start.36 = (f32[2,1,1536]{2,0,1:T(2,128)}, f32[2,1,1536]{2,0,1:T(2,128)S(1)}, u32[]{:S(2)}) copy-start(f32[2,1,1536]{2,0,1:T(2,128)S(1)} %copy.162) | copy-start | bytes 36868
  286.1 97.4 %all-to-all-start = ((bf16[2,256,3,4,384]{4,1,2,0,3:T(8,128)(2,1)}), bf16[2,256,3,4,384]{4,1,2,0,3:T(8,128)(2,1)}, u32[]{:S(2)}, u32[]{:S(2)}) async-start(bf16[2,256,3,4,384]{4,1,2,0,3:T(8,128)(2,1)} %copy.106), calls=%async_computation | async-start | bytes 9437184 | tf_op jit(solution)/shard_map/all_to_all | solution.py:149
  478.8 81.1 %all-to-all-start.1 = ((bf16[2,1024,384]{2,0,1:T(2,128)(2,1)}), bf16[2,1024,384]{2,0,1:T(2,128)(2,1)}, u32[]{:S(2)}, u32[]{:S(2)}) async-start(bf16[2,1024,384]{2,0,1:T(2,128)(2,1)} %copy.108), calls=%async_computation.1 | async-start | bytes 3145728 | tf_op jit(solution)/shard_map/all_to_all | solution.py:161
  554.6 237.8 %copy-start.34 = (f32[2,1,1536]{2,0,1:T(2,128)}, f32[2,1,1536]{2,0,1:T(2,128)S(1)}, u32[]{:S(2)}) copy-start(f32[2,1,1536]{2,0,1:T(2,128)S(1)} %copy.156) | copy-start | bytes 36868
  780.4 13.8 copy-start.11
  794.2 15.5 copy-start.22
  794.3 15.4 copy-start.47
  794.3 15.4 copy-start.53
  846.7 28.3 copy-start.62
  893.7 24.5 all-to-all-start.2
  898.1 586.0 %reduce-scatter.19.cloned.1.call-start = ((), (), s32[]{:S(2)}) async-start(), calls=%async_computation.19 | async-start | bytes 10027008 | tf_op jit(solution)/shard_map/reduce_scatter | solution.py:332
  917.6 646.3 %reduce-scatter.17.cloned.1.call-start = ((), (), s32[]{:S(2)}) async-start(), calls=%async_computation.18 | async-start | bytes 30081024 | tf_op jit(solution)/shard_map/reduce_scatter | solution.py:323
  1294.8 640.8 %reduce-scatter.21.cloned.1.call-start = ((), (), s32[]{:S(2)}) async-start(), calls=%async_computation.20 | async-start | bytes 40108032 | tf_op jit(solution)/shard_map/reduce_scatter | solution.py:242
  1295.5 14.4 copy-start.12
  1295.5 14.4 copy-start.50
  1295.5 14.4 copy-start.63
  1295.5 14.4 copy-start.72
  1295.5 14.4 copy-start.81
  1355.3 952.2 %reduce-scatter.23.cloned.1.call-start = ((), (), s32[]{:S(2)}) async-start(), calls=%async_computation.21 | async-start | bytes 40108032 | tf_op jit(solution)/shard_map/reduce_scatter | solution.py:248
  1412.5 954.1 %reduce-scatter.27.cloned.1.call-start = ((), (), s32[]{:S(2)}) async-start(), calls=%async_computation.23 | async-start | bytes 417792
  1415.4 1009.8 %reduce-scatter.31.cloned.1.call-start = ((), (), s32[]{:S(2)}) async-start(), calls=%async_computation.25 | async-start | bytes 417792
  1421.1 1067.2 %reduce-scatter.29.cloned.1.call-start = ((), (), s32[]{:S(2)}) async-start(), calls=%async_computation.24 | async-start | bytes 1671168
  1432.7 1115.3 %reduce-scatter.25.cloned.1.call-start = ((), (), s32[]{:S(2)}) async-start(), calls=%async_computation.22 | async-start | bytes 835584
  1464.5 14.3 copy-start.46
  1481.7 1159.7 %all-reduce.8.cloned.1.call-start = ((), (), s32[]{:S(2)}) async-start(), calls=%async_computation.17 | async-start | bytes 589824 | tf_op jit(solution)/shard_map/psum | solution.py:345
  1484.0 1336.7 %all-reduce.10.cloned.1.call-start = ((), (), s32[]{:S(2)}) async-start(), calls=%async_computation.26 | async-start | bytes 14155776 | tf_op jit(solution)/shard_map/psum | solution.py:359
  (83 other events, 553.4 us)
Sparse Core Ops, SparseCore 0:
  14.1 94.2 all-reduce.5
  109.9 142.3 all-gather.8
  254.6 104.2 all-gather.10
  360.4 204.1 all-gather.12
  566.0 188.2 all-gather.14
  917.7 112.6 reduce-scatter.18
  1295.0 268.8 reduce-scatter.16
  1568.7 366.8 reduce-scatter.20
  1940.5 366.9 reduce-scatter.22
  2311.8 54.7 reduce-scatter.26
  2370.6 54.5 reduce-scatter.30
  2429.8 58.4 reduce-scatter.28
  2492.4 55.5 reduce-scatter.24
  2552.1 89.2 all-reduce.7
  2644.1 176.5 all-reduce.9
where the time goes:
time: 2850 us; the launch traced here: 2840 us
  waiting for transfers between devices  1630 us (57%)
  matrix products  562 us (20%)
  blocking collectives  285 us (10%)
  other arithmetic  174 us (6%)
  local copies, waits for them, and re-layouts  153 us (5%)
    reduce_scatter x1, waiting for transfers between devices, on_device(): lax.psum_scatter(grad_down_all.astype(jnp.bfloat16), ('shard', 'seq'), sc...  372 us
    reduce_scatter x1, waiting for transfers between devices, on_device(): lax.psum_scatter(grad_up_all.astype(jnp.bfloat16), ('shard', 'seq'), scat...  372 us
    unnamed x19, waiting for transfers between devices  235 us
    all_gather x1, waiting for transfers between devices, on_device(): lax.all_gather(fc2_w, ('shard', 'seq'), axis=1, tiled=True)  166 us
    all_gather x1, waiting for transfers between devices, on_device(): lax.all_gather(qkv_w, ('shard', 'seq'), axis=1, tiled=True)  133 us
    psum x1, waiting for transfers between devices, on_device(): lax.psum(attn_shards[0].astype(jnp.bfloat16), 'rep').astype(jnp.float32)  132 us
    dot_general x8, matrix products, outer_sum(): jnp.einsum('ctd,cte->de', left, right, preferred_element_type=jnp.float32)  94.6 us
    all_gather x1, blocking collectives, on_device(): lax.all_gather(fc1_b, ('shard', 'seq'), axis=1, tiled=True)  91 us
  transfers between devices with their start and end apart: 18, of which 13 were waited for; matrix products, arithmetic and copies ran while one was open for 26% of the time, Pallas kernels for 0%

commit v1 on v0

v1 whole, which is shorter than its diff:
```python
import jax
import jax.numpy as jnp
from jax import lax
from jax.experimental import pallas as pl
from jax.experimental.pallas import tpu as pltpu
from jax.sharding import Mesh, PartitionSpec as P

HD = 64
BF = jnp.bfloat16
F32 = jnp.float32
FLIP = ((0, 1), (1, 0))


def matmul(left, right, left_dim, right_dim):
    return lax.dot_general(
        left, right, (((left_dim,), (right_dim,)), ((), ())), preferred_element_type=F32
    )


def attend_forward_kernel(low_ref, high_ref, out_ref, lse_ref, *, heads, block, scale):
    length = low_ref.shape[1]
    width = heads * HD
    for half, ref in enumerate((low_ref, high_ref)):
        for head in range(heads):
            at = head * HD
            place = half * width + at
            keys = ref[0, :, width + at : width + at + HD]
            values_t = ref[0, :, 2 * width + at : 2 * width + at + HD].T

            def one(step, carry, ref=ref, at=at, place=place, keys=keys, values_t=values_t, row=half * heads + head):
                rows = pl.ds(pl.multiple_of(step * block, block), block)
                queries = ref[0, rows, at : at + HD]
                raw = matmul(keys, queries, 1, 1)
                top = jnp.max(raw, axis=0, keepdims=True)
                grown = jnp.exp((raw - top) * scale)
                total = jnp.sum(grown, axis=0, keepdims=True)
                weights = (grown * (1.0 / total)).astype(BF)
                mixed_t = matmul(values_t, weights, 1, 0)
                out_ref[0, rows, place : place + HD] = mixed_t.T.astype(BF)
                lse_ref[0, row : row + 1, rows] = top * scale + jnp.log(total)
                return carry

            lax.fori_loop(0, length // block, one, 0)


def attend_backward_kernel(
    low_ref, high_ref, lse_ref, grad_ref, low_out, high_out, key_sum, value_sum, *, heads, block, scale
):
    length = low_ref.shape[1]
    width = heads * HD
    for half, (ref, out) in enumerate(((low_ref, low_out), (high_ref, high_out))):
        for head in range(heads):
            at = head * HD
            place = half * width + at
            keys = ref[0, :, width + at : width + at + HD]
            values = ref[0, :, 2 * width + at : 2 * width + at + HD]
            keys_t = keys.T
            key_sum[...] = jnp.zeros_like(key_sum)
            value_sum[...] = jnp.zeros_like(value_sum)

            def one(
                step, carry, ref=ref, out=out, at=at, place=place, keys=keys, values=values, keys_t=keys_t,
                row=half * heads + head,
            ):
                rows = pl.ds(pl.multiple_of(step * block, block), block)
                queries = ref[0, rows, at : at + HD]
                grad = grad_ref[0, rows, place : place + HD]
                raw = matmul(keys, queries, 1, 1)
                prob = jnp.exp(raw * scale - lse_ref[0, row : row + 1, rows])
                value_sum[...] += matmul(prob.astype(BF), grad, 1, 0)
                grad_prob = matmul(values, grad, 1, 1)
                delta = jnp.sum(prob * grad_prob, axis=0, keepdims=True)
                grad_raw = (prob * (grad_prob - delta) * scale).astype(BF)
                key_sum[...] += matmul(grad_raw, queries, 1, 0)
                query_t = matmul(keys_t, grad_raw, 1, 0)
                out[0, rows, at : at + HD] = query_t.T.astype(BF)
                return carry

            lax.fori_loop(0, length // block, one, 0)
            out[0, :, width + at : width + at + HD] = key_sum[...].astype(BF)
            out[0, :, 2 * width + at : 2 * width + at + HD] = value_sum[...].astype(BF)


def query_block(length):
    return 256 if length % 256 == 0 else length


def attend_forward(low, high):
    seqs, length, cols = low.shape
    heads = cols // (3 * HD)
    flops = 2 * 2 * heads * seqs * length * length * HD * 2
    spec = pl.BlockSpec((1, length, cols), lambda s: (s, 0, 0))
    return pl.pallas_call(
        lambda *refs: attend_forward_kernel(*refs, heads=heads, block=query_block(length), scale=HD**-0.5),
        grid=(seqs,),
        in_specs=[spec, spec],
        out_specs=[
            pl.BlockSpec((1, length, 2 * heads * HD), lambda s: (s, 0, 0)),
            pl.BlockSpec((1, 2 * heads, length), lambda s: (s, 0, 0)),
        ],
        out_shape=[
            jax.ShapeDtypeStruct((seqs, length, 2 * heads * HD), BF),
            jax.ShapeDtypeStruct((seqs, 2 * heads, length), F32),
        ],
        compiler_params=pltpu.CompilerParams(vmem_limit_bytes=40 << 20),
        cost_estimate=pl.CostEstimate(
            flops=4 * flops, bytes_accessed=2 * low.size * 2 * 2, transcendentals=seqs * 2 * heads * length * length
        ),
        name="attend_forward",
    )(low, high)


def attend_backward(low, high, lse, grad):
    seqs, length, cols = low.shape
    heads = cols // (3 * HD)
    flops = 5 * 2 * heads * seqs * length * length * HD * 2
    spec = pl.BlockSpec((1, length, cols), lambda s: (s, 0, 0))
    return pl.pallas_call(
        lambda *refs: attend_backward_kernel(*refs, heads=heads, block=query_block(length), scale=HD**-0.5),
        grid=(seqs,),
        in_specs=[
            spec,
            spec,
            pl.BlockSpec((1, 2 * heads, length), lambda s: (s, 0, 0)),
            pl.BlockSpec((1, length, 2 * heads * HD), lambda s: (s, 0, 0)),
        ],
        out_specs=[spec, spec],
        out_shape=[jax.ShapeDtypeStruct(low.shape, BF)] * 2,
        scratch_shapes=[pltpu.VMEM((length, HD), F32), pltpu.VMEM((length, HD), F32)],
        compiler_params=pltpu.CompilerParams(vmem_limit_bytes=40 << 20),
        cost_estimate=pl.CostEstimate(
            flops=4 * flops, bytes_accessed=4 * low.size * 2 * 2, transcendentals=seqs * 2 * heads * length * length
        ),
        name="attend_backward",
    )(low, high, lse, grad)


def swap(value, axis):
    return lax.ppermute(value, axis, FLIP)


def shift_xor(value, axis, bit):
    return lax.ppermute(value, axis, [(i, i ^ bit) for i in range(lax.axis_size(axis))])


def pick(index, first, second):
    return jnp.where(index == 0, first, second)


def paired(index, own, other, axis):
    return jnp.where(
        index == 0, jnp.concatenate([own, other], axis), jnp.concatenate([other, own], axis)
    )


def split_swap(value, dim, index, axis):
    first, second = jnp.split(value, 2, axis=dim)
    return pick(index, first, second), swap(pick(index, second, first), axis)


def spread(value, axes):
    value = value[None]
    for axis in reversed(axes):
        size, here = lax.axis_size(axis), lax.axis_index(axis)
        bit = 1
        while bit < size:
            value = paired((here // bit) % 2, value, shift_xor(value, axis, bit), 0)
            bit *= 2
    return value


def total(value, axes):
    for axis in axes:
        bit = 1
        while bit < lax.axis_size(axis):
            value = value + shift_xor(value, axis, bit)
            bit *= 2
    return value


def gather_square(own):
    half = own.shape[0] // 2
    from_x, from_y = swap(own, "x"), swap(own, "y")
    corner = jnp.concatenate([swap(from_x[:half], "y"), swap(from_y[half:], "x")], 0)
    return jnp.stack([own, from_y, from_x, corner])


def scatter_square(parts):
    half = parts.shape[1] // 2
    sent = parts[3].astype(BF)
    to_x = parts[2].at[:half].add(swap(sent[:half], "y").astype(F32)).astype(BF)
    to_y = parts[1].at[half:].add(swap(sent[half:], "x").astype(F32)).astype(BF)
    return parts[0] + swap(to_x, "x").astype(F32) + swap(to_y, "y").astype(F32)


def exchange_square(parts):
    own, for_y, for_x, for_corner = parts
    half = own.shape[0] // 2
    relay_y = swap(swap(for_corner[:half], "y"), "x")
    relay_x = swap(swap(for_corner[half:], "x"), "y")
    return [own, swap(for_y, "y"), swap(for_x, "x"), jnp.concatenate([relay_y, relay_x], 0)]


def on_device(
    x_img,
    x_txt,
    cond,
    counts,
    ct_img,
    ct_txt,
    ada_w,
    ada_b,
    qkv_w,
    qv_b,
    proj_w,
    proj_b,
    fc1_w,
    fc1_b,
    fc2_w,
    fc2_b,
):
    xi, yi, zi, ci = (lax.axis_index(name) for name in ("x", "y", "z", "c"))
    shards = lax.axis_size("z")
    owners = 4 * shards
    owner = zi * 4 + yi * 2 + ci
    width = x_img.shape[2]
    rows = ada_w.shape[1]
    part = width // 8
    rank_cols = width // 4
    ff_part = fc2_w.shape[1] // 2
    img = x_img.shape[1]
    txt = x_txt.shape[1]
    live = (ci < counts[0]).astype(F32)

    def to_slot(img_part, txt_part):
        both = jnp.concatenate([img_part, txt_part], 1)
        kept, received = split_swap(both, 0, ci, "c")
        return jnp.concatenate([kept, received], 0)

    tokens = to_slot(x_img, x_txt).astype(F32)

    cond_value = cond.astype(F32)
    silu_cond = jax.nn.silu(cond_value).astype(BF)
    silu_own = lax.dynamic_slice_in_dim(silu_cond, owner * rows, rows, 1)
    partial_mod = jnp.einsum("sd,jdm->jsm", silu_own, ada_w, preferred_element_type=F32)
    bias_full = lax.dynamic_update_slice_in_dim(
        jnp.zeros((2, 6 * width), F32), ada_b.astype(F32), owner * ada_b.shape[1], 1
    )
    mod = (partial_mod + bias_full[:, None]).reshape(2, shards, 2, 6 * width)
    kept, received = split_swap(mod, 2, ci, "c")
    mod = (kept + received)[:, :, 0]
    bit = shards // 2
    while bit >= 1:
        here = (zi // bit) % 2
        first, second = jnp.split(mod, 2, axis=1)
        mod = pick(here, first, second) + shift_xor(pick(here, second, first), "z", bit)
        bit //= 2
    mod = mod[:, 0]
    mod = (mod + swap(mod, "y")).reshape(2, 6, width)
    stream_of_row = (jnp.arange(img + txt) >= img)[None, :, None]

    def vector(index):
        return jnp.where(stream_of_row, mod[1, index], mod[0, index])

    small = jnp.concatenate([qv_b, proj_b, fc1_b, fc2_b], 1)
    small = spread(small, ("z", "y", "c"))
    cuts = [0]
    for item in (qv_b, proj_b, fc1_b, fc2_b):
        cuts.append(cuts[-1] + item.shape[1])
    qv_full, projb_full, upb_full, downb_full = (
        small[:, :, cuts[i] : cuts[i + 1]].transpose(1, 0, 2).reshape(2, -1).astype(F32) for i in range(4)
    )

    def at_rank(value, y_dim):
        value = lax.dynamic_index_in_dim(value, yi, y_dim, keepdims=False)
        return lax.dynamic_index_in_dim(value, xi, y_dim, keepdims=False)

    qv_rank = at_rank(qv_full.reshape(2, 2, 2, 2, 2, part), 2)
    qkv_bias = jnp.stack([qv_rank[:, 0], jnp.zeros_like(qv_rank[:, 0]), qv_rank[:, 1]], 2).reshape(2, 2, 3 * part)
    up_rank = upb_full.reshape(2, shards, 2, 2, 2, ff_part)
    up_rank = lax.dynamic_index_in_dim(up_rank, yi, 2, keepdims=False)
    up_rank = lax.dynamic_index_in_dim(up_rank, xi, 3, keepdims=False)
    up_bias = up_rank.transpose(0, 2, 1, 3).reshape(2, 2 * shards * ff_part)

    def column_weight(by_yc):
        cols = by_yc.shape[4]
        kept, received = split_swap(by_yc, 3, ci, "c")
        held = paired(ci, kept, received, 1)[:, :, :, 0]
        kept, received = split_swap(held, 2, yi, "y")
        held = paired(yi, kept, received, 1)[:, :, 0]
        full = lax.all_gather(held, ("c", "z"), axis=1, tiled=True)
        return full.reshape(2, 2, width, cols)

    qkv_x = lax.dynamic_index_in_dim(qkv_w.reshape(2, rows, 3, 2, 2, 2, part), xi, 4, keepdims=False)
    qkv_rank = column_weight(qkv_x.transpose(0, 1, 3, 4, 2, 5).reshape(2, rows, 2, 2, 3 * part))
    proj_full = lax.all_gather(proj_w, ("z", "y", "c"), axis=1, tiled=True)
    up_x = lax.dynamic_index_in_dim(fc1_w.reshape(2, rows, shards, 2, 2, 2, ff_part), xi, 5, keepdims=False)
    up_rank_w = column_weight(up_x.transpose(0, 1, 3, 4, 2, 5).reshape(2, rows, 2, 2, shards * ff_part))
    down_x = lax.dynamic_slice_in_dim(fc2_w, xi * ff_part, ff_part, 1)
    down_rank_w = lax.all_gather(down_x, ("c", "z"), axis=1, tiled=True)

    streams = (slice(0, img), slice(img, img + txt))

    def on_streams(value, weights, equation):
        return jnp.concatenate(
            [
                jnp.einsum(equation, value[..., cut, :], weights[j], preferred_element_type=F32)
                for j, cut in enumerate(streams)
            ],
            -2,
        )

    def with_bias(pair):
        return jnp.where(stream_of_row, pair[1], pair[0])

    def statistics(value):
        centre = jnp.mean(value, axis=-1, keepdims=True)
        offset = value - centre
        return offset, lax.rsqrt(jnp.mean(offset * offset, axis=-1, keepdims=True) + 1e-06)

    def back_normalize(grad, normed, scale):
        return scale * (
            grad
            - jnp.mean(grad, axis=-1, keepdims=True)
            - normed * jnp.mean(grad * normed, axis=-1, keepdims=True)
        )

    offset, spread_one = statistics(tokens)
    normed = offset * spread_one
    hidden = (normed * (1.0 + vector(1)) + vector(0)).astype(BF)
    hidden_all = gather_square(hidden)
    blocks = hidden_all.shape[1]
    seq_len = 2 * blocks * (img + txt)
    halves = []
    for half in range(2):
        value = on_streams(hidden_all, qkv_rank[:, half], "abtd,de->abte") + with_bias(qkv_bias[:, half])
        halves.append(value.astype(BF).reshape(2, seq_len, 3 * part))
    mixed, lse = attend_forward(halves[0], halves[1])
    mixed = mixed.reshape(4, blocks, img + txt, rank_cols)
    attn = jnp.concatenate(exchange_square([mixed[i] for i in range(4)]), -1)
    rank = 2 * yi + xi
    relative = [rank, rank ^ 2, rank ^ 1, rank ^ 3]
    proj_rel = jnp.concatenate(
        [lax.dynamic_slice_in_dim(proj_full, place * rank_cols, rank_cols, 1) for place in relative], 1
    )
    out = on_streams(attn, proj_rel, "btd,de->bte") + with_bias(projb_full)
    after = tokens + vector(2) * out

    offset_two, spread_two = statistics(after)
    normed_two = offset_two * spread_two
    hidden_two = (normed_two * (1.0 + vector(4)) + vector(3)).astype(BF)
    grad_y = to_slot(ct_img, ct_txt).astype(F32) * live
    grad_mlp = (vector(5) * grad_y).astype(BF)
    grad_mlp_all = gather_square(grad_mlp)
    hidden_two_all = gather_square(hidden_two)
    mlp_parts = []
    back_parts = []
    grad_up = []
    grad_down = []
    grad_upb = []
    for j, cut in enumerate(streams):
        hid = hidden_two_all[:, :, cut]
        top = grad_mlp_all[:, :, cut]
        up = up_rank_w[j]
        down = down_rank_w[j]
        pre = jnp.concatenate(
            [jnp.einsum("abtd,df->abtf", hid, up[h], preferred_element_type=F32) for h in range(2)], -1
        ) + up_bias[j]
        act, pull = jax.vjp(lambda v: jax.nn.gelu(v, approximate=True), pre)
        act = act.astype(BF)
        mlp_parts.append(jnp.einsum("abtf,fd->abtd", act, down, preferred_element_type=F32))
        grad_act = jnp.einsum("abtd,fd->abtf", top, down, preferred_element_type=F32)
        grad_pre = pull(grad_act)[0].astype(BF)
        split = grad_pre.shape[-1] // 2
        back_parts.append(
            jnp.einsum("abtf,df->abtd", grad_pre[..., :split], up[0], preferred_element_type=F32)
            + jnp.einsum("abtf,df->abtd", grad_pre[..., split:], up[1], preferred_element_type=F32)
        )
        grad_down.append(jnp.einsum("abtf,abtd->fd", act, top, preferred_element_type=F32).astype(BF))
        grad_up.append(
            jnp.stack(
                [
                    jnp.einsum("abtd,abtf->df", hid, piece, preferred_element_type=F32).astype(BF)
                    for piece in (grad_pre[..., :split], grad_pre[..., split:])
                ]
            )
        )
        grad_upb.append(jnp.sum(grad_pre.astype(F32), axis=(0, 1, 2)))
    mlp = scatter_square(jnp.concatenate(mlp_parts, -2)) + with_bias(downb_full)
    result = ((after + vector(5) * mlp) * live).astype(BF)
    grad_hidden_two = scatter_square(jnp.concatenate(back_parts, -2))

    def token_sums(value):
        return jnp.stack([jnp.sum(value[:, cut], axis=(0, 1)) for cut in streams])

    def to_owner(grad):
        cols = grad.shape[3]
        value = lax.psum_scatter(
            grad.reshape(2, 2 * shards, width // shards, cols), ("c", "z"), scatter_dimension=1, tiled=True
        ).reshape(2, 2, 2, rows, cols)
        kept, received = split_swap(value, 1, yi, "y")
        value = paired(yi, kept, received, 1)
        kept, received = split_swap(value, 2, ci, "c")
        value = paired(ci, kept, received, 2)
        value = value.transpose(0, 3, 1, 2, 4)[:, :, None]
        return paired(xi, value, swap(value, "x"), 2)

    def replicas(value):
        return lax.psum(value, "r") if lax.axis_size("r") > 1 else value

    up_owner = to_owner(jnp.stack(grad_up)).reshape(2, rows, 2, 2, 2, shards, ff_part)
    g_fc1_w = replicas(up_owner).transpose(0, 1, 5, 3, 4, 2, 6).reshape(fc1_w.shape).astype(F32)
    down_owner = lax.psum_scatter(jnp.stack(grad_down), ("c", "z"), scatter_dimension=1, tiled=True)
    g_fc2_w = replicas(paired(xi, down_owner, swap(down_owner, "x"), 1)).astype(F32)

    grad_after = grad_y + back_normalize(grad_hidden_two * (1.0 + vector(4)), normed_two, spread_two)
    grad_out = (vector(2) * grad_after).astype(BF)
    grad_attn = on_streams(grad_out, proj_rel, "bte,de->btd").astype(BF)
    grad_mixed = jnp.stack(
        exchange_square([grad_attn[..., i * rank_cols : (i + 1) * rank_cols] for i in range(4)])
    ).reshape(2, seq_len, rank_cols)
    grad_halves = attend_backward(halves[0], halves[1], lse, grad_mixed)
    grad_halves = [value.reshape(4, blocks, img + txt, 3 * part) for value in grad_halves]
    grad_hidden = scatter_square(
        on_streams(grad_halves[0], qkv_rank[:, 0], "abte,de->abtd")
        + on_streams(grad_halves[1], qkv_rank[:, 1], "abte,de->abtd")
    )
    grad_qkv = jnp.stack(
        [
            jnp.stack(
                [
                    jnp.einsum(
                        "abtd,abte->de", hidden_all[:, :, cut], value[:, :, cut], preferred_element_type=F32
                    ).astype(BF)
                    for value in grad_halves
                ]
            )
            for cut in streams
        ]
    )
    qkv_owner = to_owner(grad_qkv).reshape(2, rows, 2, 2, 2, 3, part)
    g_qkv_w = replicas(qkv_owner).transpose(0, 1, 5, 3, 2, 4, 6).reshape(qkv_w.shape).astype(F32)

    grad_proj = jnp.stack(
        [
            jnp.einsum("btd,bte->de", attn[:, cut], grad_out[:, cut], preferred_element_type=F32).astype(BF)
            for cut in streams
        ]
    )
    grad_proj = jnp.concatenate(
        [
            lax.dynamic_slice_in_dim(grad_proj, place * rank_cols, rank_cols, 1)
            for place in (
                (rank ^ t) * 0 + lax.select_n((rank ^ t), *[jnp.int32(v) for v in (0, 2, 1, 3)]) for t in range(4)
            )
        ],
        1,
    ).reshape(2, shards, 2, 2, rows, width)
    kept, received = split_swap(grad_proj, 3, ci, "c")
    grad_proj = (kept.astype(F32) + received.astype(F32)).astype(BF)
    kept, received = split_swap(grad_proj, 2, yi, "y")
    grad_proj = (kept.astype(F32) + received.astype(F32)).astype(BF).reshape(2, shards * rows, width)
    grad_proj = lax.psum_scatter(grad_proj, "z", scatter_dimension=1, tiled=True)
    g_proj_w = replicas(grad_proj.astype(F32) + swap(grad_proj, "x").astype(F32))

    grad_tokens = grad_after + back_normalize(grad_hidden * (1.0 + vector(1)), normed, spread_one)

    def from_slot(value):
        return paired(ci, value[:1], swap(value[1:], "c"), 0)

    result = from_slot(result)
    grad_tokens = from_slot(grad_tokens)

    sums = jnp.stack(
        [
            token_sums(grad_hidden),
            token_sums(grad_hidden * normed),
            token_sums(out * grad_after),
            token_sums(grad_hidden_two),
            token_sums(grad_hidden_two * normed_two),
            token_sums(mlp * grad_y),
        ],
        1,
    ).reshape(2, 6 * width)
    dmod = (sums + swap(sums, "y")).astype(BF)
    dmod_rep = spread(dmod, ("z", "c"))
    dsilu_part = jnp.einsum("sjm,jdm->sd", dmod_rep, ada_w, preferred_element_type=F32)
    dsilu = spread(dsilu_part, ("z", "y", "c")).transpose(1, 0, 2).reshape(2 * shards, owners * rows)
    gate = jax.nn.sigmoid(cond_value)
    d_cond = dsilu * gate * (1.0 + cond_value * (1.0 - gate))
    dmod_all = spread(dmod_rep, ("x",)).reshape(4 * shards, 2, 6 * width)
    silu_all = spread(silu_cond, ("x",)).reshape(4 * shards, width)
    if lax.axis_size("r") > 1:
        dmod_all = lax.all_gather(dmod_all, "r", axis=0, tiled=True)
        silu_all = lax.all_gather(silu_all, "r", axis=0, tiled=True)
    silu_cols = lax.dynamic_slice_in_dim(silu_all, owner * rows, rows, 1)
    g_ada_w = jnp.einsum("sd,sjm->jdm", silu_cols, dmod_all, preferred_element_type=F32)
    g_ada_b = lax.dynamic_slice_in_dim(
        jnp.sum(dmod_all.astype(F32), axis=0), owner * ada_b.shape[1], ada_b.shape[1], 1
    )

    here = ((jnp.arange(2)[:, None] == yi) & (jnp.arange(2)[None] == xi)).astype(F32)
    half_sums = jnp.stack(
        [
            jnp.stack([jnp.sum(value[:, :, cut].astype(F32), axis=(0, 1, 2)) for value in grad_halves])
            for cut in streams
        ]
    ).reshape(2, 2, 3, part)
    qv_sums = jnp.stack([half_sums[:, :, 0], half_sums[:, :, 2]], 1)
    qv_placed = (qv_sums[:, :, None, None] * here[:, :, None, None]).reshape(2, 2 * width)
    up_sums = jnp.stack(grad_upb).reshape(2, 2, shards, ff_part).transpose(0, 2, 1, 3)
    up_placed = (
        up_sums[:, :, None, :, None] * here[:, None, :, None]
    ).reshape(2, owners * 2 * ff_part)
    biases = jnp.concatenate(
        [qv_placed, token_sums(grad_out.astype(F32)), up_placed, token_sums(grad_mlp.astype(F32))], 1
    )
    biases = replicas(total(biases, ("c", "y", "x", "z")))
    g_biases = []
    start = 0
    for item in (qv_b, proj_b, fc1_b, fc2_b):
        cols = item.shape[1]
        g_biases.append(lax.dynamic_slice_in_dim(biases, start + owner * cols, cols, 1))
        start += owners * cols
    return (
        result[:, :img],
        result[:, img:],
        grad_tokens[:, :img],
        grad_tokens[:, img:],
        d_cond,
        g_ada_w,
        g_ada_b,
        g_qkv_w,
        g_biases[0],
        g_proj_w,
        g_biases[1],
        g_fc1_w,
        g_biases[2],
        g_fc2_w,
        g_biases[3],
    )


def solution(mesh):
    reps, shards, seqs = mesh.shape["rep"], mesh.shape["shard"], mesh.shape["seq"]
    fine = Mesh(mesh.devices.reshape(reps // 2, 2, shards, seqs // 2, 2), ("r", "x", "z", "y", "c"))
    group = ("r", "x", "z")
    token = P(group, ("y", "c"), None)
    cond = P(("r", "x"), None)
    matrix = P(None, ("z", "y", "c"), None)
    vector = P(None, ("z", "y", "c"))
    return jax.shard_map(
        on_device,
        mesh=fine,
        in_specs=(token, token, cond, P(group), token, token) + (matrix, vector) * 5,
        out_specs=(token, token, token, token, cond) + (matrix, vector) * 5,
        check_vma=False,
    )
```

time: 2850 us -> 1410 us (0.49)
  waiting for transfers between devices: 1630 us -> 482 us
  matrix products: 562 us -> 201 us
  blocking collectives: 285 us -> 0 us
  Pallas kernels: 0 us -> 118 us
  local copies, waits for them, and re-layouts: 153 us -> 264 us
  other arithmetic: 174 us -> 246 us
  starting transfers between devices: 14.6 us -> 71.7 us
    reduce_scatter x4 -> x3, waiting for transfers between devices: 823 us -> 73.8 us  [the longest x1 73.8 us: on_device(): lax.psum_scatter(jnp.stack(grad_down), ('c', 'z'), scatter_dimension=1, t...]
    ppermute x0 -> x77, waiting for transfers between devices: none -> 407 us  [the longest x57 299 us: swap(): return lax.ppermute(value, axis, FLIP)]
    dot_general x41 -> x39, matrix products: 562 us -> 201 us  [the longest x12 43.2 us: on_streams(): jnp.einsum(equation, value[..., cut, :], weights[j], preferred_element_ty...]
    all_gather x4, waiting for transfers between devices: 299 us -> 0.01 us  [the longest x2 0.01 us: column_weight(): full = lax.all_gather(held, ('c', 'z'), axis=1, tiled=True)]
    psum x3 -> x0, waiting for transfers between devices: 275 us -> none  [the longest x1 132 us: on_device(): lax.psum(attn_shards[0].astype(jnp.bfloat16), 'rep').astype(jnp.float32)]
    unnamed x19 -> x9, waiting for transfers between devices: 235 us -> 0.81 us
    all_gather x7 -> x0, blocking collectives: 222 us -> none  [the longest x1 91 us: on_device(): lax.all_gather(fc1_b, ('shard', 'seq'), axis=1, tiled=True)]
    pallas_call x0 -> x2, Pallas kernels: none -> 118 us  [the longest x1 65.9 us: attend_backward(): pl.pallas_call(lambda *refs: attend_backward_kernel(*refs, heads=heads, b...]
  transfers between devices with their start and end apart: 18 -> 85, of which waited for: 13 -> 43; matrix products, arithmetic and copies ran while one was open for 26% -> 39% of each run, Pallas kernels for 0% -> 8%
where the time goes in v1:
time: 1410 us; the launch traced here: 1400 us
  waiting for transfers between devices  482 us (34%)
  local copies, waits for them, and re-layouts  264 us (19%)
  other arithmetic  246 us (17%)
  matrix products  201 us (14%)
  Pallas kernels  118 us (8%)
  starting transfers between devices  71.7 us (5%)
  between operations  17.5 us (1%)
    ppermute x57, waiting for transfers between devices, swap(): return lax.ppermute(value, axis, FLIP)  299 us
    ppermute x20, waiting for transfers between devices, shift_xor(): lax.ppermute(value, axis, [(i, i ^ bit) for i in range(lax.axis_size(axis...  109 us
    reduce_scatter x1, waiting for transfers between devices, on_device(): lax.psum_scatter(jnp.stack(grad_down), ('c', 'z'), scatter_dimension=1, t...  73.8 us
    pallas_call x1, Pallas kernels, attend_backward(): pl.pallas_call(lambda *refs: attend_backward_kernel(*refs, heads=heads, b...  65.9 us
    ppermute x57, starting transfers between devices, swap(): return lax.ppermute(value, axis, FLIP)  57.1 us
    pallas_call x1, Pallas kernels, attend_forward(): pl.pallas_call(lambda *refs: attend_forward_kernel(*refs, heads=heads, bl...  52.2 us
    dot_general x12, matrix products, on_streams(): jnp.einsum(equation, value[..., cut, :], weights[j], preferred_element_ty...  43.2 us
  transfers between devices with their start and end apart: 85, of which 43 were waited for; matrix products, arithmetic and copies ran while one was open for 39% of the time, Pallas kernels for 8%

profile of v1, /device:TPU:0, one launch (start us, length us, event | category | flops | bytes accessed | tf_op | source)
XLA Modules:
  0.0 1399.4 jit_solution(16620041384319617293)
XLA Ops:
  38.9 11.8 collective-permute-done.10
  94.7 12.5 collective-permute-done.26
  176.6 23.9 %collective-permute-done.6 = bf16[2,256,1536]{2,1,0:T(8,128)(2,1)} collective-permute-done((bf16[2,256,1536]{2,1,0:T(8,128)(2,1)}, bf16[2,256,1536]{2,1,0:T(8,128)(2,1)}, u32[]{:S(2)}, u32[]{:S(2)}) %collective-permute-start.6) | collective-permute-done | bytes 1572896 | tf_op jit(solution)/shard_map/ppermute | solution.py:139
  203.1 26.1 %collective-permute-done.5 = bf16[2,256,1536]{2,1,0:T(8,128)(2,1)} collective-permute-done((bf16[2,256,1536]{2,1,0:T(8,128)(2,1)}, bf16[2,256,1536]{2,1,0:T(8,128)(2,1)}, u32[]{:S(2)}, u32[]{:S(2)}) %collective-permute-start.5) | collective-permute-done | bytes 1572896 | tf_op jit(solution)/shard_map/ppermute | solution.py:139
  234.7 9.1 collective-permute-done.7
  253.3 16.6 %reshape.1385 = bf16[2,2,1536,576]{2,1,3,0:T(2,128)(2,1)} reshape(bf16[2,3072,576]{1,2,0:T(8,128)(2,1)} %all-gather.5.cloned.1.call-done) | data formatting | bytes 14155776 | tf_op jit(solution)/shard_map/reshape | solution.py:292
  269.9 14.7 %fusion.203 = (bf16[1,1,1536,576]{2,1,3,0:T(2,128)(2,1)S(1)}, bf16[1,1,1536,576]{2,1,3,0:T(2,128)(2,1)S(1)}, bf16[1,1,1536,576]{2,1,3,0:T(2,128)(2,1)S(1)}, bf16[1,1,1536,576]{2,1,3,0:T(2,128)(2,1)S(1)}) fusion(bf16[2,2,1536,576]{2,1,3,0:T(2,128)(2,1)} %reshape.1385), kind=kLoop, calls=%fused_computation.500 | loop fusion | bytes 14155776 | tf_op jit(solution)/shard_map/slice | solution.py:307
  296.8 52.2 %attend_forward.1 = (bf16[2,1024,384]{2,1,0:T(8,128)(2,1)S(1)}, f32[2,6,1024]{2,1,0:T(8,128)S(1)}) custom-call(bf16[2,1024,576]{2,1,0:T(8,128)(2,1)S(1)} %bitcast.476, bf16[2,1024,576]{2,1,0:T(8,128)(2,1)S(1)} %bitcast.474), custom_call_target="tpu_custom_call" | custom-call | flops 12884901888 | bytes 9437184 | tf_op jit(solution)/shard_map/attend_forward/pallas_call | solution.py:93
  394.3 28.3 %collective-permute-done.22 = bf16[2,256,1536]{2,1,0:T(8,128)(2,1)} collective-permute-done((bf16[2,256,1536]{2,1,0:T(8,128)(2,1)}, bf16[2,256,1536]{2,1,0:T(8,128)(2,1)}, u32[]{:S(2)}, u32[]{:S(2)}) %collective-permute-start.22) | collective-permute-done | bytes 1572896 | tf_op jit(solution)/shard_map/ppermute | solution.py:139
  476.4 14.5 %fusion.28 = f32[4,2,224,1536]{3,2,1,0:T(8,128)S(1)} fusion(bf16[2,1536,1536]{2,1,0:T(8,128)(2,1)} %all-gather.11.cloned.1.call-done, f32[4,2,224,768]{3,2,1,0:T(8,128)} %fusion.33, f32[4,2,224,768]{3,2,1,0:T(8,128)} %fusion.35, f32[1536]{0:T(1024)S(1)} %copy-done.103), kind=kOutput, calls=%fused_computation.103 | convolution fusion | flops 8485994496 | bytes 26744832 | tf_op jit(solution)/shard_map/abtf,fd->abtd/dot_general | solution.py:371
  495.7 11.8 collective-permute-done.27
  515.9 23.7 %collective-permute-done.28 = bf16[2,256,1536]{2,1,0:T(8,128)(2,1)} collective-permute-done((bf16[2,256,1536]{2,1,0:T(8,128)(2,1)}, bf16[2,256,1536]{2,1,0:T(8,128)(2,1)}, u32[]{:S(2)}, u32[]{:S(2)}) %collective-permute-start.28) | collective-permute-done | bytes 1572896 | tf_op jit(solution)/shard_map/ppermute | solution.py:139
  549.6 31.2 %collective-permute-done.34 = bf16[2,256,1536]{2,1,0:T(8,128)(2,1)S(1)} collective-permute-done((bf16[2,256,1536]{2,1,0:T(8,128)(2,1)S(1)}, bf16[2,256,1536]{2,1,0:T(8,128)(2,1)S(1)}, u32[]{:S(2)}, u32[]{:S(2)}) %collective-permute-start.34) | collective-permute-done | bytes 1572896 | tf_op jit(solution)/shard_map/ppermute | solution.py:139
  598.7 21.9 %convert_reduce_fusion = (f32[1536]{0:T(1024)}, bf16[4,2,224,1536]{3,2,1,0:T(8,128)(2,1)}) fusion(f32[1536]{0:T(1024)S(1)} %copy-done.103, f32[4,2,224,768]{3,2,1,0:T(8,128)} %fusion.33, f32[4,2,224,768]{3,2,1,0:T(8,128)} %fusion.35, bf16[2,1536,1536]{2,1,0:T(8,128)(2,1)} %all-gather.11.cloned.1.call-done, bf16[4,2,256,1536]{3,2,1,0:T(8,128)(2,1)} %pad_maximum_fusion.9), kind=kOutput, calls=%fused_computation.44 | convolution fusion | flops 8521775616 | bytes 26750976 | tf_op jit(solution)/shard_map/abtd,fd->abtf/dot_general | solution.py:372
  620.6 9.5 fusion.89
  630.2 9.4 fusion.106
  644.4 10.5 convolution_add_fusion.1
  661.7 10.3 collective-permute-done.37
  683.4 9.5 fusion.86
  692.8 10.1 collective-permute-done.38
  748.1 65.9 %attend_backward.1 = (bf16[2,1024,576]{2,1,0:T(8,128)(2,1)S(1)}, bf16[2,1024,576]{2,1,0:T(8,128)(2,1)S(1)}) custom-call(bf16[2,1024,576]{2,1,0:T(8,128)(2,1)S(1)} %bitcast.477, bf16[2,1024,576]{2,1,0:T(8,128)(2,1)S(1)} %bitcast.475, f32[2,6,1024]{2,1,0:T(8,128)S(1)} %copy-done.11, bf16[2,1024,384]{2,1,0:T(8,128)(2,1)S(1)} %bitcast.480), custom_call_target="tpu_custom_call" | custom-call | flops 32212254720 | bytes 18874368 | tf_op jit(solution)/shard_map/attend_backward/pallas_call | solution.py:118
  822.8 9.1 stack.307
  850.6 9.1 stack.303
  922.1 29.3 %collective-permute-done.71 = bf16[2,4,1,1,96,1536]{5,4,3,2,1,0:T(8,128)(2,1)} collective-permute-done((bf16[2,4,1,1,96,1536]{5,4,3,2,1,0:T(8,128)(2,1)}, bf16[2,4,1,1,96,1536]{5,4,3,2,1,0:T(8,128)(2,1)}, u32[]{:S(2)}, u32[]{:S(2)}) %collective-permute-start.71) | collective-permute-done | bytes 2359328 | tf_op jit(solution)/shard_map/ppermute | solution.py:139
  957.1 18.4 %fusion.11 = bf16[1,1536,1536]{2,1,0:T(8,128)(2,1)} fusion(bf16[4,2,256,1536]{3,2,1,0:T(8,128)(2,1)} %pad_maximum_fusion.9, f32[4,2,224,768]{3,2,1,0:T(8,128)} %fusion.33, f32[4,2,224,768]{3,2,1,0:T(8,128)} %fusion.35, f32[1536]{0:T(1024)} %add.478), kind=kOutput, calls=%fused_computation.59 | convolution fusion | flops 8488353792 | bytes 21241856 | tf_op jit(solution)/shard_map/abtf,abtd->fd/dot_general | solution.py:379
  1024.9 14.8 %fusion.201 = (bf16[4,2,256,1536]{3,2,1,0:T(8,128)(2,1)S(1)}, f32[4,2,256,1536]{3,2,1,0:T(8,128)}) fusion(f32[4,2,32,1536]{3,2,1,0:T(8,128)} %fusion.158, f32[4,2,224,1536]{3,2,1,0:T(8,128)} %fusion.120, f32[4,2,32,1536]{3,2,1,0:T(8,128)} %fusion.156, f32[4,2,224,1536]{3,2,1,0:T(8,128)} %fusion.123), kind=kLoop, calls=%fused_computation.498 | loop fusion | flops 12582912 | bytes 44040192 | tf_op jit(solution)/shard_map/convert.10
  1045.0 14.8 %collective-permute-done.47 = bf16[1,256,1536]{2,1,0:T(8,128)(2,1)S(1)} collective-permute-done((bf16[1,256,1536]{2,1,0:T(8,128)(2,1)S(1)}, bf16[1,256,1536]{2,1,0:T(8,128)(2,1)S(1)}, u32[]{:S(2)}, u32[]{:S(2)}) %collective-permute-start.47) | collective-permute-done | bytes 786464 | tf_op jit(solution)/shard_map/ppermute | solution.py:139
  1066.4 35.4 %collective-permute-done.66 = f32[2,12288]{1,0:T(2,128)S(1)} collective-permute-done((f32[2,12288]{1,0:T(2,128)S(1)}, f32[2,12288]{1,0:T(2,128)S(1)}, u32[]{:S(2)}, u32[]{:S(2)}) %collective-permute-start.66) | collective-permute-done | bytes 98336 | tf_op jit(solution)/shard_map/ppermute | solution.py:143
  1108.0 9.0 collective-permute-done.68
  1165.0 17.1 %collective-permute-done.55 = bf16[4,2,9216]{2,1,0:T(2,128)(2,1)S(1)} collective-permute-done((bf16[4,2,9216]{2,1,0:T(2,128)(2,1)S(1)}, bf16[4,2,9216]{2,1,0:T(2,128)(2,1)S(1)}, u32[]{:S(2)}, u32[]{:S(2)}) %collective-permute-start.55) | collective-permute-done | bytes 147488 | tf_op jit(solution)/shard_map/ppermute | solution.py:143
  1256.7 73.8 %reduce-scatter.11.cloned.1.call-done = bf16[2,192,1536]{2,1,0:T(8,128)(2,1)} async-done(((bf16[2,1536,1536]{2,1,0:T(8,128)(2,1)}), bf16[2,192,1536]{2,1,0:T(8,128)(2,1)}) %reduce-scatter.11.cloned.1.call-update) | async-done | bytes 1179664 | tf_op jit(solution)/shard_map/reduce_scatter | solution.py:413
  1340.0 10.4 copy.118
  (707 shorter events, 717.3 us)
Async XLA Ops:
  7.2 246.1 %all-gather.5.cloned.1.call-start = ((), (), s32[]{:S(2)}) async-start(), calls=%async_computation.3 | async-start | bytes 7962624 | tf_op jit(solution)/shard_map/all_gather | solution.py:291
  56.1 314.8 %all-gather.7.cloned.1.call-start = ((), (), s32[]{:S(2)}) async-start(), calls=%async_computation.4 | async-start | bytes 10027008 | tf_op jit(solution)/shard_map/all_gather | solution.py:296
  56.8 391.0 %all-gather.9.cloned.1.call-start = ((), (), s32[]{:S(2)}) async-start(), calls=%async_computation.5 | async-start | bytes 10616832 | tf_op jit(solution)/shard_map/all_gather | solution.py:291
  58.2 55.4 %collective-permute-start.11 = (bf16[1,2,768]{2,1,0:T(2,128)(2,1)S(1)}, bf16[1,2,768]{2,1,0:T(2,128)(2,1)S(1)}, u32[]{:S(2)}, u32[]{:S(2)}) collective-permute-start(bf16[1,2,768]{2,1,0:T(2,128)(2,1)S(1)} %maximum_bitcast_fusion.6), channel_id=1, source_target_pairs={{0,1},{1,0},{2,3},{3,2},{4,5},{5,4},{6,7},{7,6},{8,9},{9,8},{10,11... | collective-permute-start | bytes 9224 | tf_op jit(solution)/shard_map/ppermute | solution.py:143
  108.7 363.3 %all-gather.11.cloned.1.call-start = ((), (), s32[]{:S(2)}) async-start(), calls=%async_computation.6 | async-start | bytes 10616832 | tf_op jit(solution)/shard_map/all_gather | solution.py:300
  122.7 38.9 %collective-permute-start = (bf16[1,256,1536]{2,1,0:T(8,128)(2,1)}, bf16[1,256,1536]{2,1,0:T(8,128)(2,1)}, u32[]{:S(2)}, u32[]{:S(2)}) collective-permute-start(bf16[1,256,1536]{2,1,0:T(8,128)(2,1)} %get-tuple-element.188), channel_id=1, source_target_pairs={{0,1},{1,0},{2,3},{3,2},{4,5},{5,4},{6,7},{7,6},{8,9},{9,8},{10,11... | collective-permute-start | bytes 2359304 | tf_op jit(solution)/shard_map/ppermute | solution.py:139
  168.3 32.2 %collective-permute-start.6 = (bf16[2,256,1536]{2,1,0:T(8,128)(2,1)}, bf16[2,256,1536]{2,1,0:T(8,128)(2,1)}, u32[]{:S(2)}, u32[]{:S(2)}) collective-permute-start(bf16[2,256,1536]{2,1,0:T(8,128)(2,1)} %fusion.50), channel_id=1, source_target_pairs={{0,16},{16,0},{1,17},{17,1},{2,18},{18,2},{3,19},{19,3},{4,20},{20... | collective-permute-start | bytes 4718600 | tf_op jit(solution)/shard_map/ppermute | solution.py:139
  169.7 59.4 %collective-permute-start.5 = (bf16[2,256,1536]{2,1,0:T(8,128)(2,1)}, bf16[2,256,1536]{2,1,0:T(8,128)(2,1)}, u32[]{:S(2)}, u32[]{:S(2)}) collective-permute-start(bf16[2,256,1536]{2,1,0:T(8,128)(2,1)} %fusion.50), channel_id=1, source_target_pairs={{0,2},{2,0},{1,3},{3,1},{4,6},{6,4},{5,7},{7,5},{8,10},{10,8},{9,1... | collective-permute-start | bytes 4718600 | tf_op jit(solution)/shard_map/ppermute | solution.py:139
  172.7 979.4 %all-reduce.3.cloned.1.call-start = ((), (), s32[]{:S(2)}) async-start(), calls=%async_computation.10 | async-start | bytes 18874368
  201.8 42.1 %collective-permute-start.7 = (bf16[1,256,1536]{2,1,0:T(8,128)(2,1)S(1)}, bf16[1,256,1536]{2,1,0:T(8,128)(2,1)S(1)}, u32[]{:S(2)}, u32[]{:S(2)}) collective-permute-start(bf16[1,256,1536]{2,1,0:T(8,128)(2,1)S(1)} %slice.764), channel_id=1, source_target_pairs={{0,2},{2,0},{1,3},{3,1},{4,6},{6,4},{5,7},{7,5},{8,10},{10,8},{9,1... | collective-permute-start | bytes 2359304 | tf_op jit(solution)/shard_map/ppermute | solution.py:139
  389.8 32.9 %collective-permute-start.22 = (bf16[2,256,1536]{2,1,0:T(8,128)(2,1)}, bf16[2,256,1536]{2,1,0:T(8,128)(2,1)}, u32[]{:S(2)}, u32[]{:S(2)}) collective-permute-start(bf16[2,256,1536]{2,1,0:T(8,128)(2,1)} %add_convert_fusion.2), channel_id=1, source_target_pairs={{0,16},{16,0},{1,17},{17,1},{2,18},{18,2},{3,19},{19,3},{4,20},{20... | collective-permute-start | bytes 4718600 | tf_op jit(solution)/shard_map/ppermute | solution.py:139
  390.7 35.6 %collective-permute-start.21 = (bf16[2,256,1536]{2,1,0:T(8,128)(2,1)}, bf16[2,256,1536]{2,1,0:T(8,128)(2,1)}, u32[]{:S(2)}, u32[]{:S(2)}) collective-permute-start(bf16[2,256,1536]{2,1,0:T(8,128)(2,1)} %add_convert_fusion.2), channel_id=1, source_target_pairs={{0,2},{2,0},{1,3},{3,1},{4,6},{6,4},{5,7},{7,5},{8,10},{10,8},{9,1... | collective-permute-start | bytes 4718600 | tf_op jit(solution)/shard_map/ppermute | solution.py:139
  509.6 29.9 %collective-permute-start.28 = (bf16[2,256,1536]{2,1,0:T(8,128)(2,1)}, bf16[2,256,1536]{2,1,0:T(8,128)(2,1)}, u32[]{:S(2)}, u32[]{:S(2)}) collective-permute-start(bf16[2,256,1536]{2,1,0:T(8,128)(2,1)} %get-tuple-element.144), channel_id=1, source_target_pairs={{0,16},{16,0},{1,17},{17,1},{2,18},{18,2},{3,19},{19,3},{4,20},{20... | collective-permute-start | bytes 4718600 | tf_op jit(solution)/shard_map/ppermute | solution.py:139
  510.3 29.2 %collective-permute-start.30 = (bf16[2,256,1536]{2,1,0:T(8,128)(2,1)}, bf16[2,256,1536]{2,1,0:T(8,128)(2,1)}, u32[]{:S(2)}, u32[]{:S(2)}) collective-permute-start(bf16[2,256,1536]{2,1,0:T(8,128)(2,1)} %get-tuple-element.145), channel_id=1, source_target_pairs={{0,2},{2,0},{1,3},{3,1},{4,6},{6,4},{5,7},{7,5},{8,10},{10,8},{9,1... | collective-permute-start | bytes 4718600 | tf_op jit(solution)/shard_map/ppermute | solution.py:139
  547.4 33.4 %collective-permute-start.34 = (bf16[2,256,1536]{2,1,0:T(8,128)(2,1)S(1)}, bf16[2,256,1536]{2,1,0:T(8,128)(2,1)S(1)}, u32[]{:S(2)}, u32[]{:S(2)}) collective-permute-start(bf16[2,256,1536]{2,1,0:T(8,128)(2,1)S(1)} %get-tuple-element.123), channel_id=1, source_target_pairs={{0,16},{16,0},{1,17},{17,1},{2,18},{18,2},{3,19},{19,3},{4,20},{20... | collective-permute-start | bytes 4718600 | tf_op jit(solution)/shard_map/ppermute | solution.py:139
  548.1 34.9 %collective-permute-start.33 = (bf16[2,256,1536]{2,1,0:T(8,128)(2,1)S(1)}, bf16[2,256,1536]{2,1,0:T(8,128)(2,1)S(1)}, u32[]{:S(2)}, u32[]{:S(2)}) collective-permute-start(bf16[2,256,1536]{2,1,0:T(8,128)(2,1)S(1)} %get-tuple-element.123), channel_id=1, source_target_pairs={{0,2},{2,0},{1,3},{3,1},{4,6},{6,4},{5,7},{7,5},{8,10},{10,8},{9,1... | collective-permute-start | bytes 4718600 | tf_op jit(solution)/shard_map/ppermute | solution.py:139
  677.6 25.4 %collective-permute-start.38 = (bf16[2,256,1536]{2,1,0:T(8,128)(2,1)S(1)}, bf16[2,256,1536]{2,1,0:T(8,128)(2,1)S(1)}, u32[]{:S(2)}, u32[]{:S(2)}) collective-permute-start(bf16[2,256,1536]{2,1,0:T(8,128)(2,1)S(1)} %get-tuple-element.140), channel_id=1, source_target_pairs={{0,16},{16,0},{1,17},{17,1},{2,18},{18,2},{3,19},{19,3},{4,20},{20... | collective-permute-start | bytes 4718600 | tf_op jit(solution)/shard_map/ppermute | solution.py:139
  743.2 467.4 %reduce-scatter.7.cloned.1.call-start = ((), (), s32[]{:S(2)}) async-start(), calls=%async_computation.7 | async-start | bytes 7962624 | tf_op jit(solution)/shard_map/reduce_scatter | solution.py:398
  867.9 383.8 %reduce-scatter.9.cloned.1.call-start = ((), (), s32[]{:S(2)}) async-start(), calls=%async_computation.8 | async-start | bytes 2949120 | tf_op jit(solution)/shard_map/reduce_scatter | solution.py:463
  879.6 25.7 %collective-permute-start.61 = (bf16[1,8,1536]{2,1,0:T(8,128)(2,1)}, bf16[1,8,1536]{2,1,0:T(8,128)(2,1)}, u32[]{:S(2)}, u32[]{:S(2)}) collective-permute-start(bf16[1,8,1536]{2,1,0:T(8,128)(2,1)} %fusion.223), channel_id=1, source_target_pairs={{0,16},{16,0},{1,17},{17,1},{2,18},{18,2},{3,19},{19,3},{4,20},{20... | collective-permute-start | bytes 73736 | tf_op jit(solution)/shard_map/ppermute | solution.py:143
  897.4 53.9 %collective-permute-start.71 = (bf16[2,4,1,1,96,1536]{5,4,3,2,1,0:T(8,128)(2,1)}, bf16[2,4,1,1,96,1536]{5,4,3,2,1,0:T(8,128)(2,1)}, u32[]{:S(2)}, u32[]{:S(2)}) collective-permute-start(bf16[2,4,1,1,96,1536]{5,4,3,2,1,0:T(8,128)(2,1)} %broadcast_select_fusion.1), channel_id=1, source_target_pairs={{0,2},{2,0},{1,3},{3,1},{4,6},{6,4},{5,7},{7,5},{8,10},{10,8},{9,1... | collective-permute-start | bytes 7077896 | tf_op jit(solution)/shard_map/ppermute | solution.py:139
  957.0 373.5 %reduce-scatter.11.cloned.1.call-start = ((), (), s32[]{:S(2)}) async-start(), calls=%async_computation.9 | async-start | bytes 10616832 | tf_op jit(solution)/shard_map/reduce_scatter | solution.py:413
  992.6 124.5 %collective-permute-start.31 = (bf16[1,256,1536]{2,1,0:T(8,128)(2,1)}, bf16[1,256,1536]{2,1,0:T(8,128)(2,1)}, u32[]{:S(2)}, u32[]{:S(2)}) collective-permute-start(bf16[1,256,1536]{2,1,0:T(8,128)(2,1)} %get-tuple-element.179), channel_id=1, source_target_pairs={{0,1},{1,0},{2,3},{3,2},{4,5},{5,4},{6,7},{7,6},{8,9},{9,8},{10,11... | collective-permute-start | bytes 2359304 | tf_op jit(solution)/shard_map/ppermute | solution.py:139
  1063.6 67.0 %collective-permute-start.48 = (bf16[2,256,1536]{2,1,0:T(8,128)(2,1)S(1)}, bf16[2,256,1536]{2,1,0:T(8,128)(2,1)S(1)}, u32[]{:S(2)}, u32[]{:S(2)}) collective-permute-start(bf16[2,256,1536]{2,1,0:T(8,128)(2,1)S(1)} %get-tuple-element.136), channel_id=1, source_target_pairs={{0,16},{16,0},{1,17},{17,1},{2,18},{18,2},{3,19},{19,3},{4,20},{20... | collective-permute-start | bytes 4718600 | tf_op jit(solution)/shard_map/ppermute | solution.py:139
  1064.1 66.6 %collective-permute-start.50 = (bf16[2,256,1536]{2,1,0:T(8,128)(2,1)S(1)}, bf16[2,256,1536]{2,1,0:T(8,128)(2,1)S(1)}, u32[]{:S(2)}, u32[]{:S(2)}) collective-permute-start(bf16[2,256,1536]{2,1,0:T(8,128)(2,1)S(1)} %get-tuple-element.137), channel_id=1, source_target_pairs={{0,2},{2,0},{1,3},{3,1},{4,6},{6,4},{5,7},{7,5},{8,10},{10,8},{9,1... | collective-permute-start | bytes 4718600 | tf_op jit(solution)/shard_map/ppermute | solution.py:139
  1064.8 37.0 %collective-permute-start.66 = (f32[2,12288]{1,0:T(2,128)S(1)}, f32[2,12288]{1,0:T(2,128)S(1)}, u32[]{:S(2)}, u32[]{:S(2)}) collective-permute-start(f32[2,12288]{1,0:T(2,128)S(1)} %fusion.222), channel_id=1, source_target_pairs={{0,2},{2,0},{1,3},{3,1},{4,6},{6,4},{5,7},{7,5},{8,10},{10,8},{9,1... | collective-permute-start | bytes 294920 | tf_op jit(solution)/shard_map/ppermute | solution.py:143
  1163.1 24.9 %collective-permute-start.73 = (bf16[2,1,2,96,768]{4,3,2,1,0:T(8,128)(2,1)S(1)}, bf16[2,1,2,96,768]{4,3,2,1,0:T(8,128)(2,1)S(1)}, u32[]{:S(2)}, u32[]{:S(2)}) collective-permute-start(bf16[2,1,2,96,768]{4,3,2,1,0:T(8,128)(2,1)S(1)} %get-tuple-element.194), channel_id=1, source_target_pairs={{0,2},{2,0},{1,3},{3,1},{4,6},{6,4},{5,7},{7,5},{8,10},{10,8},{9,1... | collective-permute-start | bytes 1769480 | tf_op jit(solution)/shard_map/ppermute | solution.py:139
  1185.7 48.9 %collective-permute-start.51 = (f32[1,256,1536]{2,1,0:T(8,128)}, f32[1,256,1536]{2,1,0:T(8,128)}, u32[]{:S(2)}, u32[]{:S(2)}) collective-permute-start(f32[1,256,1536]{2,1,0:T(8,128)} %get-tuple-element.169), channel_id=1, source_target_pairs={{0,1},{1,0},{2,3},{3,2},{4,5},{5,4},{6,7},{7,6},{8,9},{9,8},{10,11... | collective-permute-start | bytes 4718600 | tf_op jit(solution)/shard_map/ppermute | solution.py:139
  1219.0 28.0 %collective-permute-start.75 = (bf16[2,96,1,2,2,768]{5,1,4,3,0,2:T(8,128)(2,1)}, bf16[2,96,1,2,2,768]{5,1,4,3,0,2:T(8,128)(2,1)}, u32[]{:S(2)}, u32[]{:S(2)}) collective-permute-start(bf16[2,96,1,2,2,768]{5,1,4,3,0,2:T(8,128)(2,1)} %get-tuple-element.190), channel_id=1, source_target_pairs={{0,16},{16,0},{1,17},{17,1},{2,18},{18,2},{3,19},{19,3},{4,20},{20... | collective-permute-start | bytes 3538952 | tf_op jit(solution)/shard_map/ppermute | solution.py:139
  1251.6 107.4 %collective-permute-start.72 = (bf16[2,96,1536]{2,1,0:T(8,128)(2,1)}, bf16[2,96,1536]{2,1,0:T(8,128)(2,1)}, u32[]{:S(2)}, u32[]{:S(2)}) collective-permute-start(bf16[2,96,1536]{2,1,0:T(8,128)(2,1)} %reduce-scatter.9.cloned.1.call-done), channel_id=1, source_target_pairs={{0,16},{16,0},{1,17},{17,1},{2,18},{18,2},{3,19},{19,3},{4,20},{20... | collective-permute-start | bytes 1769480 | tf_op jit(solution)/shard_map/ppermute | solution.py:139
  1256.2 107.6 %collective-permute-start.64 = (bf16[2,96,1,2,2,576]{5,1,4,3,0,2:T(8,128)(2,1)}, bf16[2,96,1,2,2,576]{5,1,4,3,0,2:T(8,128)(2,1)}, u32[]{:S(2)}, u32[]{:S(2)}) collective-permute-start(bf16[2,96,1,2,2,576]{5,1,4,3,0,2:T(8,128)(2,1)} %get-tuple-element.204), channel_id=1, source_target_pairs={{0,16},{16,0},{1,17},{17,1},{2,18},{18,2},{3,19},{19,3},{4,20},{20... | collective-permute-start | bytes 2654216 | tf_op jit(solution)/shard_map/ppermute | solution.py:139
  1330.5 56.3 %collective-permute-start.76 = (bf16[2,192,1536]{2,1,0:T(8,128)(2,1)}, bf16[2,192,1536]{2,1,0:T(8,128)(2,1)}, u32[]{:S(2)}, u32[]{:S(2)}) collective-permute-start(bf16[2,192,1536]{2,1,0:T(8,128)(2,1)} %reduce-scatter.11.cloned.1.call-done), channel_id=1, source_target_pairs={{0,16},{16,0},{1,17},{17,1},{2,18},{18,2},{3,19},{19,3},{4,20},{20... | collective-permute-start | bytes 3538952 | tf_op jit(solution)/shard_map/ppermute | solution.py:139
  (171 other events, 2167.1 us)
Sparse Core Ops, SparseCore 0:
  56.2 72.5 all-gather.4
  131.1 106.1 all-gather.6
  239.5 89.1 all-gather.8
  330.7 88.9 all-gather.10
  743.4 192.5 all-reduce.2
  938.7 142.6 reduce-scatter.6
  1083.7 52.7 reduce-scatter.8
  1138.8 191.6 reduce-scatter.10

commit v2 on v1

v2 whole, which is shorter than its diff:
```python
import jax
import jax.numpy as jnp
from jax import lax
from jax.experimental import pallas as pl
from jax.experimental.pallas import tpu as pltpu
from jax.sharding import Mesh, PartitionSpec as P

HD = 64
BF = jnp.bfloat16
F32 = jnp.float32
FLIP = ((0, 1), (1, 0))


def matmul(left, right, left_dim, right_dim):
    return lax.dot_general(
        left, right, (((left_dim,), (right_dim,)), ((), ())), preferred_element_type=F32
    )


def join_streams(img_ref, txt_ref, cut):
    img = img_ref[:, :, cut]
    txt = txt_ref[:, :, cut]
    return jnp.concatenate([img.reshape(-1, HD), txt.reshape(-1, HD)], 0)


def attend_forward_kernel(img_ref, txt_ref, out_ref, lse_ref, *, heads, scale):
    blocks = img_ref.shape[0]
    width = heads * HD
    rows = out_ref.shape[1]
    for head in range(heads):
        cut = slice(head * HD, head * HD + HD)
        keys = join_streams(img_ref, txt_ref, slice(width + cut.start, width + cut.stop))
        values_t = join_streams(img_ref, txt_ref, slice(2 * width + cut.start, 2 * width + cut.stop)).T
        for block in range(blocks):
            queries = jnp.concatenate([img_ref[block, :, cut], txt_ref[block, :, cut]], 0)
            raw = matmul(keys, queries, 1, 1)
            top = jnp.max(raw, axis=0, keepdims=True)
            grown = jnp.exp((raw - top) * scale)
            total = jnp.sum(grown, axis=0, keepdims=True)
            weights = (grown * (1.0 / total)).astype(BF)
            mixed_t = matmul(values_t, weights, 1, 0)
            out_ref[block, :, cut] = mixed_t.T.astype(BF)
            lse_ref[head : head + 1, block * rows : (block + 1) * rows] = top * scale + jnp.log(total)


def attend_backward_kernel(
    img_ref, txt_ref, lse_ref, grad_ref, img_out, txt_out, key_sum, value_sum, *, heads, scale
):
    blocks, img_rows = img_ref.shape[:2]
    txt_rows = txt_ref.shape[1]
    width = heads * HD
    rows = grad_ref.shape[1]
    for head in range(heads):
        cut = slice(head * HD, head * HD + HD)
        key_cut = slice(width + cut.start, width + cut.stop)
        value_cut = slice(2 * width + cut.start, 2 * width + cut.stop)
        keys = join_streams(img_ref, txt_ref, key_cut)
        values = join_streams(img_ref, txt_ref, value_cut)
        keys_t = keys.T
        for block in range(blocks):
            queries = jnp.concatenate([img_ref[block, :, cut], txt_ref[block, :, cut]], 0)
            grad = grad_ref[block, :, cut]
            raw = matmul(keys, queries, 1, 1)
            prob = jnp.exp(raw * scale - lse_ref[head : head + 1, block * rows : (block + 1) * rows])
            value_part = matmul(prob.astype(BF), grad, 1, 0)
            grad_prob = matmul(values, grad, 1, 1)
            delta = jnp.sum(prob * grad_prob, axis=0, keepdims=True)
            grad_raw = (prob * (grad_prob - delta) * scale).astype(BF)
            key_part = matmul(grad_raw, queries, 1, 0)
            if block == 0:
                value_sum[...] = value_part
                key_sum[...] = key_part
            else:
                value_sum[...] += value_part
                key_sum[...] += key_part
            grad_query = matmul(keys_t, grad_raw, 1, 0).T.astype(BF)
            img_out[block, :, cut] = grad_query[:img_rows]
            txt_out[block, :, cut] = grad_query[img_rows:]
        for there, total in ((key_cut, key_sum), (value_cut, value_sum)):
            for block in range(blocks):
                img_out[block, :, there] = total[block * img_rows : (block + 1) * img_rows].astype(BF)
                at = blocks * img_rows + block * txt_rows
                txt_out[block, :, there] = total[at : at + txt_rows].astype(BF)


def whole(shape):
    return pl.BlockSpec(shape, lambda: (0,) * len(shape))


def attend_cost(img, txt, heads, products):
    length = img.shape[0] * (img.shape[1] + txt.shape[1])
    return pl.CostEstimate(
        flops=products * 18 * heads * length * length * HD,
        bytes_accessed=4 * (img.size + txt.size),
        transcendentals=heads * length * length,
    )


def attend_forward(img, txt):
    blocks = img.shape[0]
    rows = img.shape[1] + txt.shape[1]
    heads = img.shape[2] // (3 * HD)
    outs = ((blocks, rows, heads * HD), (heads, blocks * rows))
    return pl.pallas_call(
        lambda *refs: attend_forward_kernel(*refs, heads=heads, scale=HD**-0.5),
        in_specs=[whole(img.shape), whole(txt.shape)],
        out_specs=[whole(shape) for shape in outs],
        out_shape=[jax.ShapeDtypeStruct(outs[0], BF), jax.ShapeDtypeStruct(outs[1], F32)],
        compiler_params=pltpu.CompilerParams(vmem_limit_bytes=40 << 20),
        cost_estimate=attend_cost(img, txt, heads, 2),
        name="attend_forward",
    )(img, txt)


def attend_backward(img, txt, lse, grad):
    heads = img.shape[2] // (3 * HD)
    length = img.shape[0] * (img.shape[1] + txt.shape[1])
    return pl.pallas_call(
        lambda *refs: attend_backward_kernel(*refs, heads=heads, scale=HD**-0.5),
        in_specs=[whole(value.shape) for value in (img, txt, lse, grad)],
        out_specs=[whole(img.shape), whole(txt.shape)],
        out_shape=[jax.ShapeDtypeStruct(img.shape, BF), jax.ShapeDtypeStruct(txt.shape, BF)],
        scratch_shapes=[pltpu.VMEM((length, HD), F32), pltpu.VMEM((length, HD), F32)],
        compiler_params=pltpu.CompilerParams(vmem_limit_bytes=40 << 20),
        cost_estimate=attend_cost(img, txt, heads, 5),
        name="attend_backward",
    )(img, txt, lse, grad)


CURVE = 0.7978845608028654
CUBIC = 0.044715


def gelu_and_slope(value):
    square = value * value
    bend = jnp.tanh(CURVE * value * (1.0 + CUBIC * square))
    rise = 0.5 + 0.5 * bend
    slope = rise + 0.5 * CURVE * value * (1.0 - bend * bend) * (1.0 + 3.0 * CUBIC * square)
    return value * rise, slope


def hidden_kernel(hid_ref, top_ref, up_ref, down_ref, bias_ref, act_ref, grad_ref):
    blocks, rows, width = hid_ref.shape
    cols = act_ref.shape[2]
    pre = matmul(hid_ref[...].reshape(blocks * rows, width), up_ref[...], 1, 0) + bias_ref[...]
    grad_act = matmul(top_ref[...].reshape(blocks * rows, width), down_ref[...], 1, 1)
    act, slope = gelu_and_slope(pre)
    act_ref[...] = act.astype(BF).reshape(blocks, rows, cols)
    grad_ref[...] = (grad_act * slope).astype(BF).reshape(blocks, rows, cols)


def output_kernel(act_ref, grad_ref, up_ref, down_ref, *refs):
    mlp_ref, back_ref = refs[-2:]
    blocks, rows, ff = act_ref.shape
    cols = mlp_ref.shape[2]
    back = matmul(grad_ref[...].reshape(blocks * rows, ff), up_ref[...], 1, 1)
    back_ref[...] = back.astype(BF).reshape(blocks, rows, cols)
    mlp = matmul(act_ref[...].reshape(blocks * rows, ff), down_ref[...], 1, 0)
    mlp_ref[...] = mlp.astype(BF).reshape(blocks, rows, cols)


def feed_forward_hidden(hid, top, up, down, bias, cut):
    blocks, _, width = hid.shape
    rows = cut.stop - cut.start
    ff = up.shape[1]
    tile = 256 if ff % 256 == 0 else ff
    token = pl.BlockSpec((blocks, rows, width), lambda f: (0, cut.start // rows, 0))
    out_spec = pl.BlockSpec((blocks, rows, tile), lambda f: (0, 0, f))
    size = blocks * rows
    return pl.pallas_call(
        hidden_kernel,
        grid=(ff // tile,),
        in_specs=[
            token,
            token,
            pl.BlockSpec((width, tile), lambda f: (0, f)),
            pl.BlockSpec((tile, width), lambda f: (f, 0)),
            pl.BlockSpec((1, tile), lambda f: (0, f)),
        ],
        out_specs=[out_spec, out_spec],
        out_shape=[jax.ShapeDtypeStruct((blocks, rows, ff), BF)] * 2,
        compiler_params=pltpu.CompilerParams(vmem_limit_bytes=48 << 20),
        cost_estimate=pl.CostEstimate(
            flops=8 * size * width * ff, bytes_accessed=4 * size * (width + ff) + 4 * up.size, transcendentals=size * ff
        ),
        name="feed_forward_hidden",
    )(hid, top, up, down, bias)


def feed_forward_output(act, grad_pre, up, down, cut, outs):
    blocks, rows, ff = act.shape
    width = up.shape[0]
    tile = 256 if width % 256 == 0 else width
    token = pl.BlockSpec((blocks, rows, ff), lambda n: (0, 0, 0))
    out_spec = pl.BlockSpec((blocks, rows, tile), lambda n: (0, cut.start // rows, n))
    filled = outs if isinstance(outs, (tuple, list)) else ()
    shape = filled[0].shape if filled else (blocks, outs, width)
    size = blocks * rows
    return pl.pallas_call(
        output_kernel,
        grid=(width // tile,),
        in_specs=[
            token,
            token,
            pl.BlockSpec((tile, ff), lambda n: (n, 0)),
            pl.BlockSpec((ff, tile), lambda n: (0, n)),
            *(pl.BlockSpec(memory_space=pl.ANY) for _ in filled),
        ],
        out_specs=[out_spec, out_spec],
        out_shape=[jax.ShapeDtypeStruct(shape, BF)] * 2,
        input_output_aliases={4: 0, 5: 1} if filled else {},
        compiler_params=pltpu.CompilerParams(vmem_limit_bytes=48 << 20),
        cost_estimate=pl.CostEstimate(
            flops=8 * size * width * ff, bytes_accessed=4 * size * (width + ff) + 4 * up.size, transcendentals=0
        ),
        name="feed_forward_output",
    )(act, grad_pre, up, down, *filled)


def swap(value, axis):
    return lax.ppermute(value, axis, FLIP)


def shift_xor(value, axis, bit):
    return lax.ppermute(value, axis, [(i, i ^ bit) for i in range(lax.axis_size(axis))])


def shift(value, axis, step):
    size = lax.axis_size(axis)
    return lax.ppermute(value, axis, [(i, (i + step) % size) for i in range(size)])


def swap_both(value):
    return lax.ppermute(value, ("x", "y"), [(i, 3 - i) for i in range(4)])


def pick(index, first, second):
    return jnp.where(index == 0, first, second)


def paired(index, own, other, axis):
    return jnp.where(
        index == 0, jnp.concatenate([own, other], axis), jnp.concatenate([other, own], axis)
    )


def split_swap(value, dim, index, axis):
    first, second = jnp.split(value, 2, axis=dim)
    return pick(index, first, second), swap(pick(index, second, first), axis)


def spread(value, axes):
    value = value[None]
    for axis in reversed(axes):
        size, here = lax.axis_size(axis), lax.axis_index(axis)
        bit = 1
        while bit < size:
            value = paired((here // bit) % 2, value, shift_xor(value, axis, bit), 0)
            bit *= 2
    return value


def total(value, axes):
    for axis in axes:
        bit = 1
        while bit < lax.axis_size(axis):
            value = value + shift_xor(value, axis, bit)
            bit *= 2
    return value


def after_these(values, others):
    leaves, tree = jax.tree.flatten(values)
    return jax.tree.unflatten(tree, lax.optimization_barrier((tuple(leaves), tuple(jax.tree.leaves(others))))[0])


def gather_square(own, beside=((), ())):
    from_x, from_y = after_these((swap(own, "x"), swap(own, "y")), beside[0])
    corner_a, corner_b = after_these((swap(from_x[:1], "y"), swap(from_y[1:], "x")), beside[1])
    return jnp.concatenate([own, from_y], 0), jnp.concatenate([from_x, corner_a, corner_b], 0)


def plus(first, second):
    return (first.astype(F32) + second.astype(F32)).astype(BF)


def relay_square(other):
    return swap(other[2:3], "y"), swap(other[3:4], "x")


def send_x(other, relays):
    return swap(plus(other[:1], relays[0]), "x"), swap(other[1:2], "x")


def send_y(own, relays):
    return swap(own[2:3], "y"), swap(plus(own[3:4], relays[1]), "y")


def sum_square(own, from_x, from_y):
    return own[:2].astype(F32) + jnp.concatenate(from_x, 0).astype(F32) + jnp.concatenate(from_y, 0).astype(F32)


def exchange_square(own, for_y, for_x, for_corner):
    return [own, swap(for_y, "y"), swap(for_x, "x"), swap_both(for_corner)]


def on_device(
    x_img,
    x_txt,
    cond,
    counts,
    ct_img,
    ct_txt,
    ada_w,
    ada_b,
    qkv_w,
    qv_b,
    proj_w,
    proj_b,
    fc1_w,
    fc1_b,
    fc2_w,
    fc2_b,
):
    xi, yi, zi, ci = (lax.axis_index(name) for name in ("x", "y", "z", "c"))
    shards = lax.axis_size("z")
    owners = 4 * shards
    owner = zi * 4 + yi * 2 + ci
    width = x_img.shape[2]
    rows = ada_w.shape[1]
    rank_cols = width // 4
    ff_block = fc2_w.shape[1]
    img = x_img.shape[1]
    txt = x_txt.shape[1]
    live = (ci < counts[0]).astype(F32)
    streams = (slice(0, img), slice(img, img + txt))

    def to_slot(img_part, txt_part):
        both = jnp.concatenate([img_part, txt_part], 1)
        kept, received = split_swap(both, 0, ci, "c")
        return jnp.concatenate([kept, received], 0)

    tokens = to_slot(x_img, x_txt).astype(F32)

    cotangents = to_slot(ct_img, ct_txt)
    ct_from_x, ct_from_y = swap(cotangents, "x"), swap(cotangents, "y")

    cond_value = cond.astype(F32)
    silu_cond = jax.nn.silu(cond_value).astype(BF)
    silu_own = lax.dynamic_slice_in_dim(silu_cond, owner * rows, rows, 1).reshape(shards, 2, rows)
    bias_full = lax.dynamic_update_slice_in_dim(
        jnp.zeros((2, 6 * width), F32), ada_b.astype(F32), owner * ada_b.shape[1], 1
    )

    def partial_mod(slots):
        return jnp.einsum("sd,jdm->sjm", slots, ada_w, preferred_element_type=F32) + bias_full

    mod_peer = partial_mod(pick(ci, silu_own[:, 1], silu_own[:, 0]))
    mod_sent = swap(mod_peer, "c")
    mod_own = partial_mod(pick(ci, silu_own[:, 0], silu_own[:, 1]))
    mod = mod_own + mod_sent
    mod_summed = mod
    mod_here = lax.dynamic_index_in_dim(mod, zi, 0, keepdims=False)
    for step in range(1, shards):
        there = lax.dynamic_index_in_dim(mod, (zi + step) % shards, 0, keepdims=False)
        mod_here = mod_here + shift(there, "z", step)
    mod = (mod_here + swap(mod_here, "y")).reshape(2, 6, width)
    stream_of_row = (jnp.arange(img + txt) >= img)[None, :, None]

    def vector(index):
        return jnp.where(stream_of_row, mod[1, index], mod[0, index])

    def with_bias(pair):
        return jnp.where(stream_of_row, pair[1], pair[0])

    def rank_columns(weight, offsets):
        by_y = [
            pick(
                xi,
                *(
                    jnp.concatenate([weight[:, :, at : at + size] for at, size in offsets(y, x)], 2)
                    for x in range(2)
                ),
            )
            for y in range(2)
        ]
        return pick(yi, by_y[0], by_y[1]), swap(pick(yi, by_y[1], by_y[0]), "y")

    def by_owner(kept, received):
        return jnp.stack([pick(yi, kept, received), pick(yi, received, kept)], 1)

    def natural_rows(gathered):
        cols = gathered.shape[3]
        return gathered.reshape(shards, 2, 2, rows, cols).transpose(0, 2, 1, 3, 4).reshape(width, cols)

    def qkv_offsets(y, x):
        return [(third * width + (2 * y + x) * rank_cols, rank_cols) for third in range(3)]

    def up_offsets(y, x):
        return [((z * 4 + y * 2 + x) * ff_block, ff_block) for z in range(shards)]

    qkv_pair = rank_columns(qkv_w, qkv_offsets)
    proj_swapped = swap(after_these(proj_w, qkv_pair[0]), "y")
    qkv_held = by_owner(*after_these(qkv_pair, mod_summed))
    qkv_gathered = lax.all_gather(qkv_held, ("z", "c"), axis=0)
    qkv_rank = [natural_rows(qkv_gathered[:, j]) for j in range(2)]

    def statistics(value):
        centre = jnp.mean(value, axis=-1, keepdims=True)
        offset = value - centre
        return offset, lax.rsqrt(jnp.mean(offset * offset, axis=-1, keepdims=True) + 1e-06)

    def back_normalize(grad, normed, scale):
        return scale * (
            grad
            - jnp.mean(grad, axis=-1, keepdims=True)
            - normed * jnp.mean(grad * normed, axis=-1, keepdims=True)
        )

    offset, spread_one = statistics(tokens)
    normed = offset * spread_one
    hidden = (normed * (1.0 + vector(1)) + vector(0)).astype(BF)
    hidden, ct_from_x, ct_from_y = after_these((hidden, ct_from_x, ct_from_y), (ct_from_x, ct_from_y))
    ct_corner = swap(ct_from_x[:1], "y"), swap(ct_from_y[1:], "x")
    gate_live = mod[:, 5] * live
    gate_other = swap(gate_live, "x")
    small = spread(jnp.concatenate(after_these((qv_b, proj_b, fc1_b, fc2_b), hidden), 1), ("y", "z", "c"))
    hidden_seqs = gather_square(hidden, (small, ct_corner))
    small = small.reshape(2, shards, 2, 2, -1).swapaxes(0, 1).reshape(owners, 2, -1)

    proj_held = by_owner(*after_these((proj_w, proj_swapped), (hidden, qkv_held)))
    fc1_w, fc2_w = after_these((fc1_w, fc2_w), hidden_seqs)
    up_pair = rank_columns(fc1_w, up_offsets)

    cuts = [0]
    for item in (qv_b, proj_b, fc1_b, fc2_b):
        cuts.append(cuts[-1] + item.shape[1])
    qv_full, projb_full, upb_full, downb_full = (
        small[:, :, cuts[i] : cuts[i + 1]].transpose(1, 0, 2).reshape(2, -1).astype(F32) for i in range(4)
    )

    def at_rank(pieces):
        return pick(yi, pick(xi, *pieces[0]), pick(xi, *pieces[1]))

    def rank_vector(value, offsets):
        return at_rank(
            [
                [jnp.concatenate([value[:, at : at + size] for at, size in offsets(y, x)], 1) for x in range(2)]
                for y in range(2)
            ]
        )

    qv_rank = rank_vector(qv_full, lambda y, x: qkv_offsets(y, x)[:2])
    qkv_bias = jnp.concatenate(
        [qv_rank[:, :rank_cols], jnp.zeros((2, rank_cols), F32), qv_rank[:, rank_cols:]], 1
    )
    up_bias = rank_vector(upb_full, up_offsets)

    proj_gathered = lax.all_gather(proj_held, ("z", "c"), axis=0).reshape(shards, 2, 2, 2, rows, width)
    def two_streams(value, weights, equation):
        return [
            jnp.einsum(equation, value[:, cut], weights[j], preferred_element_type=F32)
            for j, cut in enumerate(streams)
        ]

    halves = jnp.split(fc2_w, 2, axis=1)
    down_sent = swap(pick(ci, halves[1], halves[0]), "c")
    qkv_seqs, mixed_seqs, lse_seqs = [], [], []
    for value in hidden_seqs:
        if mixed_seqs:
            value = after_these(value, mixed_seqs)
        pair = [
            (item + qkv_bias[j]).astype(BF)
            for j, item in enumerate(two_streams(value, qkv_rank, "btd,de->bte"))
        ]
        mixed, lse = attend_forward(*pair)
        qkv_seqs.append(pair)
        mixed_seqs.append(mixed)
        lse_seqs.append(lse)
    up_held, down_sent = after_these((by_owner(*up_pair), down_sent), mixed_seqs[0])
    down_held = jnp.where(ci == xi, pick(ci, halves[0], halves[1]), down_sent)

    def gather_up(piece):
        return natural_rows(lax.all_gather(piece, ("z", "c"), axis=0))

    def gather_down(piece):
        return lax.all_gather(piece, ("z", "c"), axis=0, tiled=True)

    up_img = gather_up(up_held[0])
    down_img = gather_down(after_these(down_held[0], mixed_seqs[1]))
    attn = jnp.concatenate(
        exchange_square(mixed_seqs[0][:2], mixed_seqs[0][2:], mixed_seqs[1][:2], mixed_seqs[1][2:]), -1
    )
    up_rank = [up_img, gather_up(after_these(up_held[1], attn))]
    rank = 2 * yi + xi
    relative = (0, 2, 1, 3)
    proj_rel = [
        jnp.concatenate(
            [
                lax.dynamic_index_in_dim(proj_gathered, rank ^ flip, 0, keepdims=False)[:, j]
                .transpose(1, 0, 2, 3)
                .reshape(rank_cols, width)
                for flip in relative
            ],
            0,
        )
        for j in range(2)
    ]
    out = jnp.concatenate(two_streams(attn, proj_rel, "btd,de->bte"), 1) + with_bias(projb_full)
    after = tokens + vector(2) * out

    offset_two, spread_two = statistics(after)
    normed_two = offset_two * spread_two
    hidden_two = (normed_two * (1.0 + vector(4)) + vector(3)).astype(BF)
    grad_y = cotangents.astype(F32) * live

    def gated(gate, blocks):
        return (jnp.where(stream_of_row, gate[1], gate[0]) * jnp.concatenate(blocks, 0).astype(F32)).astype(BF)

    grad_mlp_seqs = [
        gated(gate_live, after_these((cotangents, ct_from_y), hidden_two)),
        gated(gate_other, after_these((ct_from_x, *ct_corner), hidden_two)),
    ]
    grad_mlp = grad_mlp_seqs[0][:2]
    down_rank = [down_img, gather_down(after_these(down_held[1], hidden_two))]
    hidden_two_seqs = gather_square(hidden_two)
    def hidden_of(j, hid, top):
        return feed_forward_hidden(hid, top, up_rank[j], down_rank[j], up_bias[j : j + 1], streams[j])

    act_img_other, pre_img_other = hidden_of(0, hidden_two_seqs[1], grad_mlp_seqs[1])
    outs_other = feed_forward_output(act_img_other, pre_img_other, up_img, down_img, streams[0], img + txt)
    act_img_own, pre_img_own = hidden_of(0, after_these(hidden_two_seqs[0], outs_other), grad_mlp_seqs[0])
    outs_own = feed_forward_output(act_img_own, pre_img_own, up_img, down_img, streams[0], img + txt)
    text_hids = after_these(hidden_two_seqs, outs_own)
    act_txt_other, pre_txt_other = hidden_of(1, text_hids[1], grad_mlp_seqs[1])
    mlp_other, back_other = feed_forward_output(
        act_txt_other, pre_txt_other, up_rank[1], down_rank[1], streams[1], outs_other
    )
    act_txt_own, pre_txt_own = hidden_of(1, after_these(text_hids[0], back_other), grad_mlp_seqs[0])
    mlp_own, back_own = feed_forward_output(act_txt_own, pre_txt_own, up_rank[1], down_rank[1], streams[1], outs_own)
    back_relays = after_these(relay_square(back_other), back_own)

    def replicas(value):
        return lax.psum(value, "r") if lax.axis_size("r") > 1 else value

    def two_sums(lefts, rights):
        first, second = (
            jnp.einsum("btd,bte->de", left, right, preferred_element_type=F32) for left, right in zip(lefts, rights)
        )
        return (first + second).astype(BF)

    def owner_rows(grad):
        cols = grad.shape[1]
        value = grad.reshape(shards, 2, 2, rows, cols).transpose(0, 2, 1, 3, 4).reshape(-1, cols)
        return lax.psum_scatter(value, ("z", "c"), scatter_dimension=0, tiled=True).reshape(2, rows, cols)

    def owner_columns(mine, others, offsets):
        by_rank = {}
        for y in range(2):
            for x in range(2):
                by_rank[y, x] = pick(
                    xi ^ x, pick(yi ^ y, mine[:, 0], mine[:, 1]), pick(yi ^ y, others[:, 0], others[:, 1])
                )
        places = []
        for (y, x), piece in by_rank.items():
            start = 0
            for at, size in offsets(y, x):
                places.append((at, piece[:, :, start : start + size].astype(F32)))
                start += size
        places.sort(key=lambda place: place[0])
        return jnp.concatenate([piece for _, piece in places], 2)

    cut = streams[0]
    down_grad_img = two_sums([act_img_own, act_img_other], [top[:, cut] for top in grad_mlp_seqs])
    up_grad_img = two_sums([hid[:, cut] for hid in hidden_two_seqs], [pre_img_own, pre_img_other])
    back_x, back_y = send_x(back_other, back_relays), send_y(back_own, back_relays)
    cut = streams[1]
    text = after_these((act_txt_own, act_txt_other, pre_txt_own, pre_txt_other), (back_own, back_relays))
    down_grad_txt = two_sums(text[:2], [top[:, cut] for top in grad_mlp_seqs])
    up_grad_txt = two_sums([hid[:, cut] for hid in hidden_two_seqs], text[2:])
    back_x, back_y = after_these((back_x, back_y), (down_grad_txt, up_grad_txt))
    grad_hidden_two = sum_square(back_own, back_x, back_y)
    grad_up = [owner_rows(up_grad_img), owner_rows(up_grad_txt)]
    grad_down = [
        lax.psum_scatter(down, ("z", "c"), scatter_dimension=0, tiled=True)
        for down in (down_grad_img, down_grad_txt)
    ]
    grad_after = grad_y + back_normalize(grad_hidden_two * (1.0 + vector(4)), normed_two, spread_two)
    grad_out = (vector(2) * grad_after).astype(BF)

    grad_attn = jnp.concatenate(
        [item.astype(BF) for item in two_streams(grad_out, proj_rel, "bte,de->btd")], 1
    )
    pieces = [grad_attn[:, :, i * rank_cols : (i + 1) * rank_cols] for i in range(4)]
    back = exchange_square(*pieces)
    grad_mixed_seqs = [jnp.concatenate(back[:2], 0), jnp.concatenate(back[2:], 0)]

    def hidden_back(grad_pair):
        return jnp.concatenate(
            [
                jnp.einsum("bte,de->btd", grad_pair[j], qkv_rank[j], preferred_element_type=F32).astype(BF)
                for j in range(2)
            ],
            1,
        )

    mlp_own, mlp_other = after_these((mlp_own, mlp_other), grad_mixed_seqs)
    mlp_relays = relay_square(mlp_other)
    mlp_x1, mlp_y2 = swap(mlp_other[1:2], "x"), swap(mlp_own[2:3], "y")
    grad_pair_other = attend_backward(*qkv_seqs[1], lse_seqs[1], grad_mixed_seqs[1])
    mlp_relays, mlp_x1, mlp_y2 = after_these((mlp_relays, mlp_x1, mlp_y2), grad_pair_other)
    hidden_back_other = hidden_back(after_these(grad_pair_other, mlp_relays))
    mlp_x0 = swap(plus(mlp_other[:1], mlp_relays[0]), "x")
    mlp_y3 = swap(plus(mlp_own[3:4], mlp_relays[1]), "y")

    grad_late = after_these(grad_out, hidden_back_other)
    position = lax.select_n(
        rank ^ jnp.arange(4), *(jnp.full((4,), place, jnp.int32) for place in (0, 2, 1, 3))
    )

    def proj_rows(core):
        blocks = [attn[:, :, at * rows : (at + 1) * rows] for at in range(16)]
        left = jnp.concatenate([pick(core, blocks[at], blocks[at + 1]) for at in range(0, 16, 2)], -1)
        return [
            jnp.einsum("btd,bte->de", left[:, cut], grad_late[:, cut], preferred_element_type=F32)
            .astype(BF)
            .reshape(4, 2, rows, width)
            for cut in streams
        ]

    proj_sent, proj_kept = jnp.stack(proj_rows(1 - ci)), jnp.stack(proj_rows(ci))
    proj_received = swap(proj_sent, "c")

    hidden_relays = relay_square(hidden_back_other)
    grad_pair_own = attend_backward(
        *qkv_seqs[0], lse_seqs[0], after_these(grad_mixed_seqs[0], (hidden_back_other, mlp_x1, mlp_y2, proj_kept))
    )
    hidden_relays = after_these(hidden_relays, grad_pair_own)
    mlp_x0, mlp_y3 = after_these((mlp_x0, mlp_y3), grad_pair_own)
    hidden_back_own = hidden_back(after_these(grad_pair_own, (hidden_relays, mlp_x0, mlp_y3)))
    mlp = sum_square(mlp_own, (mlp_x0, mlp_x1), (mlp_y2, mlp_y3)) + with_bias(downb_full)
    result = ((after + vector(5) * mlp) * live).astype(BF)
    hidden_x = send_x(hidden_back_other, hidden_relays)
    hidden_y = send_y(hidden_back_own, hidden_relays)

    def qkv_grad(j, pairs):
        return two_sums([hid[:, streams[j]] for hid in hidden_seqs], [pair[j] for pair in pairs])

    grad_pairs = [grad_pair_own, grad_pair_other]
    qkv_grad_img = qkv_grad(0, after_these(grad_pairs, hidden_back_own))
    hidden_x, hidden_y0 = after_these((hidden_x, hidden_y[0]), qkv_grad_img)
    qkv_grad_txt = qkv_grad(1, after_these(grad_pairs, hidden_y0))
    grad_qkv = jnp.stack([qkv_grad_img, qkv_grad_txt])
    cols = grad_qkv.shape[2]
    grad_qkv = grad_qkv.reshape(2, shards, 2, 2, rows, cols).transpose(1, 3, 0, 2, 4, 5)
    grad_qkv = grad_qkv.reshape(2 * shards, 2, 2, rows, cols)
    proj_received = after_these(proj_received, grad_qkv)
    grad_proj = plus(proj_kept, proj_received)
    grad_proj = jnp.concatenate([lax.dynamic_slice_in_dim(grad_proj, position[t], 1, 1) for t in range(4)], 1)
    proj_kept, proj_received = split_swap(grad_proj, 0, xi, "x")
    hidden_last = after_these(hidden_y[1], (grad_qkv, proj_kept))
    grad_hidden = sum_square(hidden_back_own, hidden_x, (hidden_y0, hidden_last))
    grad_qkv = lax.psum_scatter(grad_qkv, ("z", "c"), scatter_dimension=0, tiled=True).reshape(2, 2, rows, cols)

    up_pair = split_swap(replicas(after_these(jnp.stack(grad_up), grad_hidden)), 1, yi, "y")
    down = replicas(after_these(jnp.stack(grad_down), grad_hidden))
    down_other = swap(down, "x")
    grad_hidden_late = after_these(grad_hidden, (up_pair[0], down))

    grad_tokens = grad_after + back_normalize(grad_hidden * (1.0 + vector(1)), normed, spread_one)

    def from_slot(value):
        return paired(ci, value[:1], swap(value[1:], "c"), 0)

    result = from_slot(result)
    grad_tokens = from_slot(grad_tokens)

    def token_sums(value):
        return jnp.stack([jnp.sum(value[:, cut], axis=(0, 1)) for cut in streams])

    sums = jnp.stack(
        [
            token_sums(grad_hidden_late),
            token_sums(grad_hidden_late * normed),
            token_sums(out * grad_after),
            token_sums(grad_hidden_two),
            token_sums(grad_hidden_two * normed_two),
            token_sums(mlp * grad_y),
        ],
        1,
    ).reshape(2, 6 * width)
    up_pair, proj_received = after_these((up_pair, proj_received), sums)
    up_mine = jnp.concatenate(up_pair, 1)
    proj_kept, proj_received = split_swap(plus(proj_kept, proj_received)[0], 1, yi, "y")
    sums = after_these(sums, (up_mine, proj_kept))
    up_others = swap(up_mine, "x")
    dmod = (sums + swap(sums, "y")).astype(BF)
    dmod_rep = spread(dmod, ("z", "c"))
    qkv_pair = split_swap(replicas(grad_qkv), 1, yi, "y")
    up_others, late_pre, late_out, late_mlp, dmod_rep, down_other, proj_received = after_these(
        (
            up_others,
            (pre_img_own, pre_img_other, pre_txt_own, pre_txt_other),
            grad_out,
            grad_mlp,
            dmod_rep,
            down_other,
            proj_received,
        ),
        qkv_pair[0],
    )
    g_fc1_w = owner_columns(up_mine, up_others, up_offsets)
    grad_proj = plus(proj_kept, proj_received).reshape(shards * rows, width)
    grad_proj = replicas(lax.psum_scatter(grad_proj, "z", scatter_dimension=0, tiled=True))
    g_proj_w = paired(xi, grad_proj[None], swap(grad_proj, "x")[None], 0).astype(F32)
    blocks = (pick(xi, down, down_other), pick(xi, down_other, down))
    g_fc2_w = paired(ci, pick(ci, *blocks), swap(pick(ci, blocks[1], blocks[0]), "c"), 1).astype(F32)
    qkv_mine = jnp.concatenate(qkv_pair, 1)
    g_qkv_w = owner_columns(qkv_mine, swap(qkv_mine, "x"), qkv_offsets)
    dsilu_part = jnp.einsum("sjm,jdm->sd", dmod_rep, ada_w, preferred_element_type=F32)
    dsilu = spread(dsilu_part, ("z", "y", "c")).transpose(1, 0, 2).reshape(2 * shards, owners * rows)
    gate = jax.nn.sigmoid(cond_value)
    d_cond = dsilu * gate * (1.0 + cond_value * (1.0 - gate))
    dmod_all = spread(dmod_rep, ("x",)).reshape(4 * shards, 2, 6 * width)
    silu_all = spread(silu_cond, ("x",)).reshape(4 * shards, width)
    if lax.axis_size("r") > 1:
        dmod_all = lax.all_gather(dmod_all, "r", axis=0, tiled=True)
        silu_all = lax.all_gather(silu_all, "r", axis=0, tiled=True)
    silu_cols = lax.dynamic_slice_in_dim(silu_all, owner * rows, rows, 1)
    g_ada_w = jnp.einsum("sd,sjm->jdm", silu_cols, dmod_all, preferred_element_type=F32)
    g_ada_b = jnp.sum(
        lax.dynamic_slice_in_dim(dmod_all, owner * ada_b.shape[1], ada_b.shape[1], 2).astype(F32), axis=0
    )

    here = ((jnp.arange(2)[:, None] == yi) & (jnp.arange(2)[None] == xi)).astype(F32)
    qkv_sums = jnp.stack(
        [sum(jnp.sum(pair[j].astype(F32), axis=(0, 1)) for pair in grad_pairs) for j in range(2)]
    ).reshape(2, 3, rank_cols)
    qv_sums = jnp.stack([qkv_sums[:, 0], qkv_sums[:, 2]], 1)
    qv_placed = (qv_sums[:, :, None, None] * here[:, :, None]).reshape(2, 2 * width)
    up_sums = jnp.stack(
        [sum(jnp.sum(pre.astype(F32), axis=(0, 1)) for pre in late_pre[2 * j : 2 * j + 2]) for j in range(2)]
    ).reshape(2, shards, ff_block)
    up_placed = (up_sums[:, :, None, None] * here[:, :, None]).reshape(2, owners * ff_block)
    biases = jnp.concatenate(
        [qv_placed, token_sums(late_out.astype(F32)), up_placed, token_sums(late_mlp.astype(F32))], 1
    )
    biases = replicas(total(biases, ("c", "y", "x", "z")))
    g_biases = []
    start = 0
    for item in (qv_b, proj_b, fc1_b, fc2_b):
        cols = item.shape[1]
        g_biases.append(lax.dynamic_slice_in_dim(biases, start + owner * cols, cols, 1))
        start += owners * cols
    return (
        result[:, :img],
        result[:, img:],
        grad_tokens[:, :img],
        grad_tokens[:, img:],
        d_cond,
        g_ada_w,
        g_ada_b,
        g_qkv_w,
        g_biases[0],
        g_proj_w,
        g_biases[1],
        g_fc1_w,
        g_biases[2],
        g_fc2_w,
        g_biases[3],
    )


def solution(mesh):
    reps, shards, seqs = mesh.shape["rep"], mesh.shape["shard"], mesh.shape["seq"]
    fine = Mesh(mesh.devices.reshape(reps // 2, 2, shards, seqs // 2, 2), ("r", "x", "z", "y", "c"))
    group = ("r", "x", "z")
    token = P(group, ("y", "c"), None)
    cond = P(("r", "x"), None)
    matrix = P(None, ("z", "y", "c"), None)
    vector = P(None, ("z", "y", "c"))
    return jax.shard_map(
        on_device,
        mesh=fine,
        in_specs=(token, token, cond, P(group), token, token) + (matrix, vector) * 5,
        out_specs=(token, token, token, token, cond) + (matrix, vector) * 5,
        check_vma=False,
    )
```

time: 1410 us -> 1050 us (0.74)
  waiting for transfers between devices: 482 us -> 284 us
  local copies, waits for them, and re-layouts: 264 us -> 173 us
  matrix products: 201 us -> 118 us
  other arithmetic: 246 us -> 175 us
  Pallas kernels: 118 us -> 188 us
    dot_general x37 -> x30, matrix products: 195 us -> 111 us  [the longest x12 64.5 us: two_sums(): jnp.einsum('btd,bte->de', left, right, preferred_element_type=F32)]
    ppermute x57 -> x56, waiting for transfers between devices: 299 us -> 220 us  [swap(): return lax.ppermute(value, axis, FLIP)]
    reduce_scatter x3 -> x6, waiting for transfers between devices: 73.8 us -> 0.04 us  [the longest x2 0.04 us: owner_rows(): lax.psum_scatter(value, ('z', 'c'), scatter_dimension=0, tiled=True)]
    pallas_call x2 -> x12, Pallas kernels: 118 us -> 188 us  [the longest x2 52.3 us: attend_backward(): pl.pallas_call(lambda *refs: attend_backward_kernel(*refs, heads=heads, s...]
    ppermute x20 -> x18, waiting for transfers between devices: 109 us -> 41 us  [shift_xor(): lax.ppermute(value, axis, [(i, i ^ bit) for i in range(lax.axis_size(axis...]
    another operation x22 -> x9, other arithmetic: 54.6 us -> 9.77 us  [the longest x6 4.64 us: by_owner(): return jnp.stack([pick(yi, kept, received), pick(yi, received, kept)], 1)]
    another operation x20 -> x8, local copies, waits for them, and re-layouts: 46.5 us -> 5.76 us  [the longest x7 5.16 us: on_device(): jnp.stack([token_sums(grad_hidden_late), token_sums(grad_hidden_late * no...]
    unnamed x241 -> x398, local copies, waits for them, and re-layouts: 27.1 us -> 61.9 us
  transfers between devices with their start and end apart: 85 -> 91, of which waited for: 43 -> 41; matrix products, arithmetic and copies ran while one was open for 39% -> 40% of each run, Pallas kernels for 8% -> 18%
where the time goes in v2:
time: 1050 us
  waiting for transfers between devices  284 us (27%)
  Pallas kernels  188 us (18%)
  other arithmetic  175 us (17%)
  local copies, waits for them, and re-layouts  173 us (16%)
  matrix products  118 us (11%)
  starting transfers between devices  83.7 us (8%)
  between operations  25.5 us (2%)
    ppermute x56, waiting for transfers between devices, swap(): return lax.ppermute(value, axis, FLIP)  220 us
    dot_general x12, matrix products, two_sums(): jnp.einsum('btd,bte->de', left, right, preferred_element_type=F32)  64.5 us
    unnamed x398, local copies, waits for them, and re-layouts  61.9 us
    ppermute x56, starting transfers between devices, swap(): return lax.ppermute(value, axis, FLIP)  60.1 us
    pallas_call x2, Pallas kernels, attend_backward(): pl.pallas_call(lambda *refs: attend_backward_kernel(*refs, heads=heads, s...  52.3 us
    pallas_call x2, Pallas kernels, attend_forward(): pl.pallas_call(lambda *refs: attend_forward_kernel(*refs, heads=heads, sc...  49.4 us
    pallas_call x4, Pallas kernels, feed_forward_hidden(): pl.pallas_call(hidden_kernel, grid=(ff // tile,), in_specs=[token, token,...  44.5 us
    pallas_call x4, Pallas kernels, feed_forward_output(): pl.pallas_call(output_kernel, grid=(width // tile,), in_specs=[token, tok...  41.3 us
  transfers between devices with their start and end apart: 91, of which 41 were waited for; matrix products, arithmetic and copies ran while one was open for 40% of the time, Pallas kernels for 18%

profile of v2, /device:TPU:0, one launch (start us, length us, event | category | flops | bytes accessed | tf_op | source)
XLA Modules:
  0.0 1047.3 jit_solution(16015929476093388759)
XLA Ops:
  26.1 6.8 collective-permute-done.11
  49.7 8.7 collective-permute-done.3
  88.0 21.6 %collective-permute-done.7 = bf16[2,256,1536]{2,1,0:T(8,128)(2,1)S(1)} collective-permute-done((bf16[2,256,1536]{2,1,0:T(8,128)(2,1)S(1)}, bf16[2,256,1536]{2,1,0:T(8,128)(2,1)S(1)}, u32[]{:S(2)}, u32[]{:S(2)}) %collective-permute-start.7) | collective-permute-done | bytes 1572896 | tf_op jit(solution)/shard_map/ppermute | solution.py:221
  141.0 13.4 %collective-permute-done.15 = bf16[8,2,768]{2,1,0:T(2,128)(2,1)S(1)} collective-permute-done((bf16[8,2,768]{2,1,0:T(2,128)(2,1)S(1)}, bf16[8,2,768]{2,1,0:T(2,128)(2,1)S(1)}, u32[]{:S(2)}, u32[]{:S(2)}) %collective-permute-start.15) | collective-permute-done | bytes 24608 | tf_op jit(solution)/shard_map/ppermute | solution.py:225
  171.4 13.7 %collective-permute-done.17 = bf16[1,256,1536]{2,1,0:T(8,128)(2,1)S(1)} collective-permute-done((bf16[1,256,1536]{2,1,0:T(8,128)(2,1)S(1)}, bf16[1,256,1536]{2,1,0:T(8,128)(2,1)S(1)}, u32[]{:S(2)}, u32[]{:S(2)}) %collective-permute-start.17) | collective-permute-done | bytes 786464 | tf_op jit(solution)/shard_map/ppermute | solution.py:221
  190.0 9.7 collective-permute-done.29
  213.4 29.4 %attend_forward.2 = (bf16[4,256,384]{2,1,0:T(8,128)(2,1)S(1)}, f32[6,1024]{1,0:T(8,128)S(1)}) custom-call(bf16[4,224,1152]{2,1,0:T(8,128)(2,1)S(1)} %fusion.15.refs_0_, bf16[4,32,1152]{2,1,0:T(8,128)(2,1)S(1)} %fusion.36.refs_1_), custom_call_target="tpu_custom_call" | custom-call | flops 14495514624 | bytes 4718592 | tf_op jit(solution)/shard_map/attend_forward/pallas_call | solution.py:104
  256.7 20.0 %attend_forward.3 = (bf16[4,256,384]{2,1,0:T(8,128)(2,1)S(1)}, f32[6,1024]{1,0:T(8,128)S(1)}) custom-call(bf16[4,224,1152]{2,1,0:T(8,128)(2,1)S(1)} %fusion.16.refs_0_, bf16[4,32,1152]{2,1,0:T(8,128)(2,1)S(1)} %fusion.37.refs_1_), custom_call_target="tpu_custom_call" | custom-call | flops 14495514624 | bytes 4718592 | tf_op jit(solution)/shard_map/attend_forward/pallas_call | solution.py:104
  285.9 7.4 collective-permute-done.22
  335.2 27.7 %collective-permute-done.24 = bf16[2,256,1536]{2,1,0:T(8,128)(2,1)} collective-permute-done((bf16[2,256,1536]{2,1,0:T(8,128)(2,1)}, bf16[2,256,1536]{2,1,0:T(8,128)(2,1)}, u32[]{:S(2)}, u32[]{:S(2)}) %collective-permute-start.24) | collective-permute-done | bytes 1572896 | tf_op jit(solution)/shard_map/ppermute | solution.py:221
  390.2 15.4 %feed_forward_hidden.4 = (bf16[4,224,1536]{2,1,0:T(8,128)(2,1)S(1)}, bf16[4,224,1536]{2,1,0:T(8,128)(2,1)S(1)}) custom-call(bf16[4,256,1536]{2,1,0:T(8,128)(2,1)} %constant_dynamic-update-slice_fusion.9.hid_ref, bf16[4,256,1536]{2,1,0:T(8,128)(2,1)} %multiply_convert_fusion.1.top_ref, bf16[1536,1536]{1,0:T(8,128)(2,1)} %bitcast.322, ...), custom_call_target="tpu_custom_call" | custom-call | flops 16911433728 | bytes 20447232 | tf_op jit(solution)/shard_map/feed_forward_hidden/pallas_call | solution.py:170
  405.6 13.6 %feed_forward_output.4 = (bf16[4,256,1536]{2,1,0:T(8,128)(2,1)}, bf16[4,256,1536]{2,1,0:T(8,128)(2,1)}) custom-call(bf16[4,224,1536]{2,1,0:T(8,128)(2,1)S(1)} %get-tuple-element.159.act_ref, bf16[4,224,1536]{2,1,0:T(8,128)(2,1)S(1)} %get-tuple-element.234.grad_ref, bf16[1536,1536]{1,0:T(8,128)(2,1)} %bitcast.323, ...), custom_call_target="tpu_custom_call" | custom-call | flops 16911433728 | bytes 20447232 | tf_op jit(solution)/shard_map/feed_forward_output/pallas_call | solution.py:199
  419.2 15.5 %feed_forward_hidden.5 = (bf16[4,224,1536]{2,1,0:T(8,128)(2,1)S(1)}, bf16[4,224,1536]{2,1,0:T(8,128)(2,1)S(1)}) custom-call(bf16[4,256,1536]{2,1,0:T(8,128)(2,1)} %pad_maximum_fusion.5.hid_ref, bf16[4,256,1536]{2,1,0:T(8,128)(2,1)} %multiply_convert_fusion.top_ref, bf16[1536,1536]{1,0:T(8,128)(2,1)} %bitcast.324, ...), custom_call_target="tpu_custom_call" | custom-call | flops 16911433728 | bytes 20447232 | tf_op jit(solution)/shard_map/feed_forward_hidden/pallas_call | solution.py:170
  434.6 7.8 fusion.26
  442.5 7.5 fusion.2
  456.1 12.7 %feed_forward_output.5 = (bf16[4,256,1536]{2,1,0:T(8,128)(2,1)}, bf16[4,256,1536]{2,1,0:T(8,128)(2,1)}) custom-call(bf16[4,224,1536]{2,1,0:T(8,128)(2,1)S(1)} %copy-done.38, bf16[4,224,1536]{2,1,0:T(8,128)(2,1)S(1)} %copy-done.12, bf16[1536,1536]{1,0:T(8,128)(2,1)} %bitcast.325, bf16[1536,1536]{1,0:T(8,128)(2,1)} %all-gather.12.cloned.1.call-done.down_ref), custom_call_target="tpu_custom_call" | custom-call | flops 16911433728 | bytes 20447232 | tf_op jit(solution)/shard_map/feed_forward_output/pallas_call | solution.py:199
  473.8 7.0 feed_forward_hidden.6
  480.9 7.5 feed_forward_output.6
  494.5 6.7 feed_forward_hidden.7
  501.2 7.5 feed_forward_output.7
  508.8 6.5 fusion.60
  523.1 7.9 fusion.29
  531.1 7.4 fusion.1
  583.0 7.3 collective-permute-done.34
  591.4 9.8 collective-permute-done.33
  643.3 26.2 %attend_backward.2 = (bf16[4,224,1152]{2,1,0:T(8,128)(2,1)S(1)}, bf16[4,32,1152]{2,1,0:T(8,128)(2,1)S(1)}) custom-call(bf16[4,224,1152]{2,1,0:T(8,128)(2,1)S(1)} %copy-done.42, bf16[4,32,1152]{2,1,0:T(8,128)(2,1)S(1)} %copy-done.34, f32[6,1024]{1,0:T(8,128)S(1)} %copy-done.46, bf16[4,256,384]{2,1,0:T(8,128)(2,1)S(1)} %constant_dynamic-update-slice_fusion.12.refs_3_), custom_call_target="tpu_custom_call" | custom-call | flops 36238786560 | bytes 4718592 | tf_op jit(solution)/shard_map/attend_backward/pallas_call | solution.py:118
  683.3 26.0 %attend_backward.3 = (bf16[4,224,1152]{2,1,0:T(8,128)(2,1)S(1)}, bf16[4,32,1152]{2,1,0:T(8,128)(2,1)S(1)}) custom-call(bf16[4,224,1152]{2,1,0:T(8,128)(2,1)S(1)} %copy-done.40, bf16[4,32,1152]{2,1,0:T(8,128)(2,1)S(1)} %copy-done.32, f32[6,1024]{1,0:T(8,128)S(1)} %copy-done.44, bf16[4,256,384]{2,1,0:T(8,128)(2,1)S(1)} %pad_maximum_fusion.17.refs_3_), custom_call_target="tpu_custom_call" | custom-call | flops 36238786560 | bytes 4718592 | tf_op jit(solution)/shard_map/attend_backward/pallas_call | solution.py:118
  766.9 11.1 %collective-permute-done.49 = bf16[1,256,1536]{2,1,0:T(8,128)(2,1)S(1)} collective-permute-done((bf16[1,256,1536]{2,1,0:T(8,128)(2,1)S(1)}, bf16[1,256,1536]{2,1,0:T(8,128)(2,1)S(1)}, u32[]{:S(2)}, u32[]{:S(2)}) %collective-permute-start.49) | collective-permute-done | bytes 786464 | tf_op jit(solution)/shard_map/ppermute | solution.py:221
  778.1 14.1 %collective-permute-done.51 = bf16[1,256,1536]{2,1,0:T(8,128)(2,1)S(1)} collective-permute-done((bf16[1,256,1536]{2,1,0:T(8,128)(2,1)S(1)}, bf16[1,256,1536]{2,1,0:T(8,128)(2,1)S(1)}, u32[]{:S(2)}, u32[]{:S(2)}) %collective-permute-start.51) | collective-permute-done | bytes 786464 | tf_op jit(solution)/shard_map/ppermute | solution.py:221
  837.8 27.1 %collective-permute-done.56 = bf16[1,4,2,96,1536]{4,3,2,1,0:T(8,128)(2,1)} collective-permute-done((bf16[1,4,2,96,1536]{4,3,2,1,0:T(8,128)(2,1)}, bf16[1,4,2,96,1536]{4,3,2,1,0:T(8,128)(2,1)}, u32[]{:S(2)}, u32[]{:S(2)}) %collective-permute-start.56) | collective-permute-done | bytes 2359328 | tf_op jit(solution)/shard_map/ppermute | solution.py:221
  900.3 15.9 %collective-permute-done.62 = bf16[2,192,1536]{2,1,0:T(8,128)(2,1)} collective-permute-done((bf16[2,192,1536]{2,1,0:T(8,128)(2,1)}, bf16[2,192,1536]{2,1,0:T(8,128)(2,1)}, u32[]{:S(2)}, u32[]{:S(2)}) %collective-permute-start.62) | collective-permute-done | bytes 1179680 | tf_op jit(solution)/shard_map/ppermute | solution.py:221
  916.1 23.6 %collective-permute-done.57 = bf16[2,2,96,1536]{3,2,0,1:T(8,128)(2,1)} collective-permute-done((bf16[2,2,96,1536]{3,2,0,1:T(8,128)(2,1)}, bf16[2,2,96,1536]{3,2,0,1:T(8,128)(2,1)}, u32[]{:S(2)}, u32[]{:S(2)}) %collective-permute-start.57) | collective-permute-done | bytes 1179680 | tf_op jit(solution)/shard_map/ppermute | solution.py:221
  (880 shorter events, 579.1 us)
Async XLA Ops:
  7.2 193.7 %all-gather.16.cloned.1.call-start = ((), (), s32[]{:S(2)}) async-start(), calls=%async_computation.15 | async-start | bytes 7962624 | tf_op jit(solution)/shard_map/all_gather | solution.py:405
  34.1 275.3 %all-gather.18.cloned.1.call-start = ((), (), s32[]{:S(2)}) async-start(), calls=%async_computation.16 | async-start | bytes 10616832 | tf_op jit(solution)/shard_map/all_gather | solution.py:459
  36.9 44.4 %collective-permute-start = (bf16[1,256,1536]{2,1,0:T(8,128)(2,1)}, bf16[1,256,1536]{2,1,0:T(8,128)(2,1)}, u32[]{:S(2)}, u32[]{:S(2)}) collective-permute-start(bf16[1,256,1536]{2,1,0:T(8,128)(2,1)} %get-tuple-element.359), channel_id=1, source_target_pairs={{0,1},{1,0},{2,3},{3,2},{4,5},{5,4},{6,7},{7,6},{8,9},{9,8},{10,11... | collective-permute-start | bytes 2359304 | tf_op jit(solution)/shard_map/ppermute | solution.py:221
  48.1 62.8 %collective-permute-start.23 = (bf16[2,96,1536]{2,1,0:T(8,128)(2,1)}, bf16[2,96,1536]{2,1,0:T(8,128)(2,1)}, u32[]{:S(2)}, u32[]{:S(2)}) collective-permute-start(bf16[2,96,1536]{2,1,0:T(8,128)(2,1)} %param.26), channel_id=1, source_target_pairs={{0,2},{2,0},{1,3},{3,1},{4,6},{6,4},{5,7},{7,5},{8,10},{10,8},{9,1... | collective-permute-start | bytes 1769480 | tf_op jit(solution)/shard_map/ppermute | solution.py:221
  74.2 35.4 %collective-permute-start.7 = (bf16[2,256,1536]{2,1,0:T(8,128)(2,1)S(1)}, bf16[2,256,1536]{2,1,0:T(8,128)(2,1)S(1)}, u32[]{:S(2)}, u32[]{:S(2)}) collective-permute-start(bf16[2,256,1536]{2,1,0:T(8,128)(2,1)S(1)} %pad_maximum_fusion.7), channel_id=1, source_target_pairs={{0,16},{16,0},{1,17},{17,1},{2,18},{18,2},{3,19},{19,3},{4,20},{20... | collective-permute-start | bytes 4718600 | tf_op jit(solution)/shard_map/ppermute | solution.py:221
  75.8 35.1 %collective-permute-start.8 = (bf16[2,256,1536]{2,1,0:T(8,128)(2,1)S(1)}, bf16[2,256,1536]{2,1,0:T(8,128)(2,1)S(1)}, u32[]{:S(2)}, u32[]{:S(2)}) collective-permute-start(bf16[2,256,1536]{2,1,0:T(8,128)(2,1)S(1)} %pad_maximum_fusion.7), channel_id=1, source_target_pairs={{0,2},{2,0},{1,3},{3,1},{4,6},{6,4},{5,7},{7,5},{8,10},{10,8},{9,1... | collective-permute-start | bytes 4718600 | tf_op jit(solution)/shard_map/ppermute | solution.py:221
  114.4 266.2 %all-gather.10.cloned.1.call-start = ((), (), s32[]{:S(2)}) async-start(), calls=%async_computation.6 | async-start | bytes 5308416 | tf_op jit(solution)/shard_map/all_gather | solution.py:484
  114.9 45.4 %collective-permute-start.9 = (bf16[2,256,1536]{2,1,0:T(8,128)(2,1)}, bf16[2,256,1536]{2,1,0:T(8,128)(2,1)}, u32[]{:S(2)}, u32[]{:S(2)}) collective-permute-start(bf16[2,256,1536]{2,1,0:T(8,128)(2,1)} %fusion.18), channel_id=1, source_target_pairs={{0,16},{16,0},{1,17},{17,1},{2,18},{18,2},{3,19},{19,3},{4,20},{20... | collective-permute-start | bytes 4718600 | tf_op jit(solution)/shard_map/ppermute | solution.py:221
  116.3 43.9 %collective-permute-start.10 = (bf16[2,256,1536]{2,1,0:T(8,128)(2,1)}, bf16[2,256,1536]{2,1,0:T(8,128)(2,1)}, u32[]{:S(2)}, u32[]{:S(2)}) collective-permute-start(bf16[2,256,1536]{2,1,0:T(8,128)(2,1)} %fusion.18), channel_id=1, source_target_pairs={{0,2},{2,0},{1,3},{3,1},{4,6},{6,4},{5,7},{7,5},{8,10},{10,8},{9,1... | collective-permute-start | bytes 4718600 | tf_op jit(solution)/shard_map/ppermute | solution.py:221
  190.0 54.4 %collective-permute-start.30 = (bf16[2,192,1536]{2,1,0:T(8,128)(2,1)}, bf16[2,192,1536]{2,1,0:T(8,128)(2,1)}, u32[]{:S(2)}, u32[]{:S(2)}) collective-permute-start(bf16[2,192,1536]{2,1,0:T(8,128)(2,1)} %broadcast_select_fusion.9), channel_id=1, source_target_pairs={{0,1},{1,0},{2,3},{3,2},{4,5},{5,4},{6,7},{7,6},{8,9},{9,8},{10,11... | collective-permute-start | bytes 3538952 | tf_op jit(solution)/shard_map/ppermute | solution.py:221
  245.5 144.7 %all-gather.12.cloned.1.call-start = ((), (), s32[]{:S(2)}) async-start(), calls=%async_computation.7 | async-start | bytes 5308416 | tf_op jit(solution)/shard_map/all_gather | solution.py:487
  278.2 190.7 %all-gather.20.cloned.1.call-start = ((), (), s32[]{:S(2)}) async-start(), calls=%async_computation.17 | async-start | bytes 5308416 | tf_op jit(solution)/shard_map/all_gather | solution.py:484
  300.3 173.5 %all-gather.14.cloned.1.call-start = ((), (), s32[]{:S(2)}) async-start(), calls=%async_computation.8 | async-start | bytes 5308416 | tf_op jit(solution)/shard_map/all_gather | solution.py:487
  328.9 34.4 %collective-permute-start.25 = (bf16[2,256,1536]{2,1,0:T(8,128)(2,1)}, bf16[2,256,1536]{2,1,0:T(8,128)(2,1)}, u32[]{:S(2)}, u32[]{:S(2)}) collective-permute-start(bf16[2,256,1536]{2,1,0:T(8,128)(2,1)} %add_convert_fusion.2), channel_id=1, source_target_pairs={{0,2},{2,0},{1,3},{3,1},{4,6},{6,4},{5,7},{7,5},{8,10},{10,8},{9,1... | collective-permute-start | bytes 4718600 | tf_op jit(solution)/shard_map/ppermute | solution.py:221
  330.4 489.0 %reduce-scatter.7.cloned.1.call-start = ((), (), s32[]{:S(2)}) async-start(), calls=%async_computation.9 | async-start | bytes 5308416 | tf_op jit(solution)/shard_map/reduce_scatter | solution.py:555
  452.5 367.0 %reduce-scatter.9.cloned.1.call-start = ((), (), s32[]{:S(2)}) async-start(), calls=%async_computation.10 | async-start | bytes 5308416 | tf_op jit(solution)/shard_map/reduce_scatter | solution.py:555
  523.1 298.9 %reduce-scatter.11.cloned.1.call-start = ((), (), s32[]{:S(2)}) async-start(), calls=%async_computation.11 | async-start | bytes 5308416 | tf_op jit(solution)/shard_map/reduce_scatter | solution.py:585
  538.5 283.5 %reduce-scatter.13.cloned.1.call-start = ((), (), s32[]{:S(2)}) async-start(), calls=%async_computation.12 | async-start | bytes 5308416 | tf_op jit(solution)/shard_map/reduce_scatter | solution.py:585
  582.9 315.1 %reduce-scatter.15.cloned.1.call-start = ((), (), s32[]{:S(2)}) async-start(), calls=%async_computation.13 | async-start | bytes 7962624 | tf_op jit(solution)/shard_map/reduce_scatter | solution.py:663
  711.3 35.6 %collective-permute-start.44 = (bf16[1,256,1536]{2,1,0:T(8,128)(2,1)}, bf16[1,256,1536]{2,1,0:T(8,128)(2,1)}, u32[]{:S(2)}, u32[]{:S(2)}) collective-permute-start(bf16[1,256,1536]{2,1,0:T(8,128)(2,1)} %add_convert_fusion.7), channel_id=1, source_target_pairs={{0,16},{16,0},{1,17},{17,1},{2,18},{18,2},{3,19},{19,3},{4,20},{20... | collective-permute-start | bytes 2359304 | tf_op jit(solution)/shard_map/ppermute | solution.py:221
  712.1 34.9 %collective-permute-start.45 = (bf16[1,256,1536]{2,1,0:T(8,128)(2,1)}, bf16[1,256,1536]{2,1,0:T(8,128)(2,1)}, u32[]{:S(2)}, u32[]{:S(2)}) collective-permute-start(bf16[1,256,1536]{2,1,0:T(8,128)(2,1)} %add_convert_fusion.6), channel_id=1, source_target_pairs={{0,2},{2,0},{1,3},{3,1},{4,6},{6,4},{5,7},{7,5},{8,10},{10,8},{9,1... | collective-permute-start | bytes 2359304 | tf_op jit(solution)/shard_map/ppermute | solution.py:221
  714.2 34.5 %collective-permute-start.48 = (bf16[1,256,1536]{2,1,0:T(8,128)(2,1)}, bf16[1,256,1536]{2,1,0:T(8,128)(2,1)}, u32[]{:S(2)}, u32[]{:S(2)}) collective-permute-start(bf16[1,256,1536]{2,1,0:T(8,128)(2,1)} %get-tuple-element.291), channel_id=1, source_target_pairs={{0,16},{16,0},{1,17},{17,1},{2,18},{18,2},{3,19},{19,3},{4,20},{20... | collective-permute-start | bytes 2359304 | tf_op jit(solution)/shard_map/ppermute | solution.py:221
  715.4 51.5 %collective-permute-start.50 = (bf16[1,256,1536]{2,1,0:T(8,128)(2,1)}, bf16[1,256,1536]{2,1,0:T(8,128)(2,1)}, u32[]{:S(2)}, u32[]{:S(2)}) collective-permute-start(bf16[1,256,1536]{2,1,0:T(8,128)(2,1)} %get-tuple-element.289), channel_id=1, source_target_pairs={{0,16},{16,0},{1,17},{17,1},{2,18},{18,2},{3,19},{19,3},{4,20},{20... | collective-permute-start | bytes 2359304 | tf_op jit(solution)/shard_map/ppermute | solution.py:221
  746.9 57.3 %collective-permute-start.53 = (bf16[2,4,2,96,1536]{4,3,2,1,0:T(8,128)(2,1)}, bf16[2,4,2,96,1536]{4,3,2,1,0:T(8,128)(2,1)}, u32[]{:S(2)}, u32[]{:S(2)}) collective-permute-start(bf16[2,4,2,96,1536]{4,3,2,1,0:T(8,128)(2,1)} %pad_maximum_fusion.3), channel_id=1, source_target_pairs={{0,1},{1,0},{2,3},{3,2},{4,5},{5,4},{6,7},{7,6},{8,9},{9,8},{10,11... | collective-permute-start | bytes 14155784 | tf_op jit(solution)/shard_map/ppermute | solution.py:221
  756.8 56.5 %collective-permute-start.52 = (bf16[1,256,1536]{2,1,0:T(8,128)(2,1)}, bf16[1,256,1536]{2,1,0:T(8,128)(2,1)}, u32[]{:S(2)}, u32[]{:S(2)}) collective-permute-start(bf16[1,256,1536]{2,1,0:T(8,128)(2,1)} %add_convert_fusion.4), channel_id=1, source_target_pairs={{0,2},{2,0},{1,3},{3,1},{4,6},{6,4},{5,7},{7,5},{8,10},{10,8},{9,1... | collective-permute-start | bytes 2359304 | tf_op jit(solution)/shard_map/ppermute | solution.py:221
  804.2 226.6 %reduce-scatter.17.cloned.1.call-start = ((), (), s32[]{:S(2)}) async-start(), calls=%async_computation.14 | async-start | bytes 1474560 | tf_op jit(solution)/shard_map/reduce_scatter | solution.py:714
  813.3 51.7 %collective-permute-start.56 = (bf16[1,4,2,96,1536]{4,3,2,1,0:T(8,128)(2,1)}, bf16[1,4,2,96,1536]{4,3,2,1,0:T(8,128)(2,1)}, u32[]{:S(2)}, u32[]{:S(2)}) collective-permute-start(bf16[1,4,2,96,1536]{4,3,2,1,0:T(8,128)(2,1)} %get-tuple-element.281), channel_id=1, source_target_pairs={{0,16},{16,0},{1,17},{17,1},{2,18},{18,2},{3,19},{19,3},{4,20},{20... | collective-permute-start | bytes 7077896 | tf_op jit(solution)/shard_map/ppermute | solution.py:221
  824.5 40.4 %collective-permute-start.55 = (bf16[2,1,96,1536]{3,2,0,1:T(8,128)(2,1)}, bf16[2,1,96,1536]{3,2,0,1:T(8,128)(2,1)}, u32[]{:S(2)}, u32[]{:S(2)}) collective-permute-start(bf16[2,1,96,1536]{3,2,0,1:T(8,128)(2,1)} %get-tuple-element.360), channel_id=1, source_target_pairs={{0,2},{2,0},{1,3},{3,1},{4,6},{6,4},{5,7},{7,5},{8,10},{10,8},{9,1... | collective-permute-start | bytes 1769480 | tf_op jit(solution)/shard_map/ppermute | solution.py:221
  888.0 51.8 %collective-permute-start.57 = (bf16[2,2,96,1536]{3,2,0,1:T(8,128)(2,1)}, bf16[2,2,96,1536]{3,2,0,1:T(8,128)(2,1)}, u32[]{:S(2)}, u32[]{:S(2)}) collective-permute-start(bf16[2,2,96,1536]{3,2,0,1:T(8,128)(2,1)} %constant_dynamic-update-slice_fusion.14), channel_id=1, source_target_pairs={{0,16},{16,0},{1,17},{17,1},{2,18},{18,2},{3,19},{19,3},{4,20},{20... | collective-permute-start | bytes 3538952 | tf_op jit(solution)/shard_map/ppermute | solution.py:221
  889.0 50.8 %collective-permute-start.63 = (bf16[4,1,96,1536]{3,2,1,0:T(8,128)(2,1)}, bf16[4,1,96,1536]{3,2,1,0:T(8,128)(2,1)}, u32[]{:S(2)}, u32[]{:S(2)}) collective-permute-start(bf16[4,1,96,1536]{3,2,1,0:T(8,128)(2,1)} %get-tuple-element.304), channel_id=1, source_target_pairs={{0,2},{2,0},{1,3},{3,1},{4,6},{6,4},{5,7},{7,5},{8,10},{10,8},{9,1... | collective-permute-start | bytes 3538952 | tf_op jit(solution)/shard_map/ppermute | solution.py:221
  946.0 50.3 %collective-permute-start.68 = (bf16[1,8,2,9216]{3,2,1,0:T(2,128)(2,1)}, bf16[1,8,2,9216]{3,2,1,0:T(2,128)(2,1)}, u32[]{:S(2)}, u32[]{:S(2)}) collective-permute-start(bf16[1,8,2,9216]{3,2,1,0:T(2,128)(2,1)} %bitcast.114), channel_id=1, source_target_pairs={{0,16},{16,0},{1,17},{17,1},{2,18},{18,2},{3,19},{19,3},{4,20},{20... | collective-permute-start | bytes 884744 | tf_op jit(solution)/shard_map/ppermute | solution.py:225
  947.1 55.2 %collective-permute-start.70 = (bf16[2,1,96,1152]{3,2,0,1:T(8,128)(2,1)}, bf16[2,1,96,1152]{3,2,0,1:T(8,128)(2,1)}, u32[]{:S(2)}, u32[]{:S(2)}) collective-permute-start(bf16[2,1,96,1152]{3,2,0,1:T(8,128)(2,1)} %get-tuple-element.368), channel_id=1, source_target_pairs={{0,2},{2,0},{1,3},{3,1},{4,6},{6,4},{5,7},{7,5},{8,10},{10,8},{9,1... | collective-permute-start | bytes 1327112 | tf_op jit(solution)/shard_map/ppermute | solution.py:221
  (238 other events, 2146.4 us)
Sparse Core Ops, SparseCore 0:
  34.2 76.5 all-gather.15
  114.6 91.7 all-gather.17
  245.7 50.5 all-gather.9
  297.8 50.5 all-gather.11
  349.8 50.5 all-gather.19
  401.9 50.5 all-gather.13
  454.7 53.7 reduce-scatter.6
  523.2 52.8 reduce-scatter.8
  578.4 53.3 reduce-scatter.10
  633.9 53.3 reduce-scatter.12
  804.3 75.7 reduce-scatter.14
  966.0 29.3 reduce-scatter.16

commit v3 on v2

--- a/solution.py
+++ b/solution.py
@@ -6,6 +6,7 @@
 from jax.sharding import Mesh, PartitionSpec as P
 
 HD = 64
+LOG2E = 1.4426950408889634
 BF = jnp.bfloat16
 F32 = jnp.float32
 FLIP = ((0, 1), (1, 0))
@@ -33,14 +34,13 @@
         values_t = join_streams(img_ref, txt_ref, slice(2 * width + cut.start, 2 * width + cut.stop)).T
         for block in range(blocks):
             queries = jnp.concatenate([img_ref[block, :, cut], txt_ref[block, :, cut]], 0)
-            raw = matmul(keys, queries, 1, 1)
+            raw = matmul(keys, queries, 1, 1) * scale
             top = jnp.max(raw, axis=0, keepdims=True)
-            grown = jnp.exp((raw - top) * scale)
+            grown = jnp.exp2(raw - top)
             total = jnp.sum(grown, axis=0, keepdims=True)
-            weights = (grown * (1.0 / total)).astype(BF)
-            mixed_t = matmul(values_t, weights, 1, 0)
+            mixed_t = matmul(values_t, grown.astype(BF), 1, 0) * (1.0 / total)
             out_ref[block, :, cut] = mixed_t.T.astype(BF)
-            lse_ref[head : head + 1, block * rows : (block + 1) * rows] = top * scale + jnp.log(total)
+            lse_ref[head : head + 1, block * rows : (block + 1) * rows] = top + jnp.log2(total)
 
 
 def attend_backward_kernel(
@@ -61,11 +61,11 @@
             queries = jnp.concatenate([img_ref[block, :, cut], txt_ref[block, :, cut]], 0)
             grad = grad_ref[block, :, cut]
             raw = matmul(keys, queries, 1, 1)
-            prob = jnp.exp(raw * scale - lse_ref[head : head + 1, block * rows : (block + 1) * rows])
+            prob = jnp.exp2(raw * scale - lse_ref[head : head + 1, block * rows : (block + 1) * rows])
             value_part = matmul(prob.astype(BF), grad, 1, 0)
             grad_prob = matmul(values, grad, 1, 1)
             delta = jnp.sum(prob * grad_prob, axis=0, keepdims=True)
-            grad_raw = (prob * (grad_prob - delta) * scale).astype(BF)
+            grad_raw = (prob * (grad_prob - delta)).astype(BF)
             key_part = matmul(grad_raw, queries, 1, 0)
             if block == 0:
                 value_sum[...] = value_part
@@ -73,14 +73,14 @@
             else:
                 value_sum[...] += value_part
                 key_sum[...] += key_part
-            grad_query = matmul(keys_t, grad_raw, 1, 0).T.astype(BF)
+            grad_query = (matmul(keys_t, grad_raw, 1, 0) * HD**-0.5).T.astype(BF)
             img_out[block, :, cut] = grad_query[:img_rows]
             txt_out[block, :, cut] = grad_query[img_rows:]
-        for there, total in ((key_cut, key_sum), (value_cut, value_sum)):
+        for there, total, factor in ((key_cut, key_sum, HD**-0.5), (value_cut, value_sum, 1.0)):
             for block in range(blocks):
-                img_out[block, :, there] = total[block * img_rows : (block + 1) * img_rows].astype(BF)
+                img_out[block, :, there] = (total[block * img_rows : (block + 1) * img_rows] * factor).astype(BF)
                 at = blocks * img_rows + block * txt_rows
-                txt_out[block, :, there] = total[at : at + txt_rows].astype(BF)
+                txt_out[block, :, there] = (total[at : at + txt_rows] * factor).astype(BF)
 
 
 def whole(shape):
@@ -102,7 +102,7 @@
     heads = img.shape[2] // (3 * HD)
     outs = ((blocks, rows, heads * HD), (heads, blocks * rows))
     return pl.pallas_call(
-        lambda *refs: attend_forward_kernel(*refs, heads=heads, scale=HD**-0.5),
+        lambda *refs: attend_forward_kernel(*refs, heads=heads, scale=HD**-0.5 * LOG2E),
         in_specs=[whole(img.shape), whole(txt.shape)],
         out_specs=[whole(shape) for shape in outs],
         out_shape=[jax.ShapeDtypeStruct(outs[0], BF), jax.ShapeDtypeStruct(outs[1], F32)],
@@ -116,7 +116,7 @@
     heads = img.shape[2] // (3 * HD)
     length = img.shape[0] * (img.shape[1] + txt.shape[1])
     return pl.pallas_call(
-        lambda *refs: attend_backward_kernel(*refs, heads=heads, scale=HD**-0.5),
+        lambda *refs: attend_backward_kernel(*refs, heads=heads, scale=HD**-0.5 * LOG2E),
         in_specs=[whole(value.shape) for value in (img, txt, lse, grad)],
         out_specs=[whole(img.shape), whole(txt.shape)],
         out_shape=[jax.ShapeDtypeStruct(img.shape, BF), jax.ShapeDtypeStruct(txt.shape, BF)],
@@ -139,82 +139,166 @@
     return value * rise, slope
 
 
-def hidden_kernel(hid_ref, top_ref, up_ref, down_ref, bias_ref, act_ref, grad_ref):
-    blocks, rows, width = hid_ref.shape
-    cols = act_ref.shape[2]
-    pre = matmul(hid_ref[...].reshape(blocks * rows, width), up_ref[...], 1, 0) + bias_ref[...]
-    grad_act = matmul(top_ref[...].reshape(blocks * rows, width), down_ref[...], 1, 1)
+def rows_of(refs):
+    values = [ref[...].reshape(-1, ref.shape[2]) for ref in refs]
+    return values[0] if len(values) == 1 else jnp.concatenate(values, 0)
+
+
+def store_rows(refs, value):
+    start = 0
+    for ref in refs:
+        stop = start + ref.shape[0] * ref.shape[1]
+        ref[...] = value[start:stop].reshape(ref.shape)
+        start = stop
+
+
+def hidden_kernel(*refs, count):
+    hids, tops, (up_ref, down_ref, bias_ref) = refs[:count], refs[count : 2 * count], refs[2 * count : 2 * count + 3]
+    acts, grads = refs[2 * count + 3 : 3 * count + 3], refs[3 * count + 3 :]
+    pre = matmul(rows_of(hids), up_ref[...], 1, 0) + bias_ref[...]
+    grad_act = matmul(rows_of(tops), down_ref[...], 1, 1)
     act, slope = gelu_and_slope(pre)
-    act_ref[...] = act.astype(BF).reshape(blocks, rows, cols)
-    grad_ref[...] = (grad_act * slope).astype(BF).reshape(blocks, rows, cols)
-
-
-def output_kernel(act_ref, grad_ref, up_ref, down_ref, *refs):
-    mlp_ref, back_ref = refs[-2:]
-    blocks, rows, ff = act_ref.shape
-    cols = mlp_ref.shape[2]
-    back = matmul(grad_ref[...].reshape(blocks * rows, ff), up_ref[...], 1, 1)
-    back_ref[...] = back.astype(BF).reshape(blocks, rows, cols)
-    mlp = matmul(act_ref[...].reshape(blocks * rows, ff), down_ref[...], 1, 0)
-    mlp_ref[...] = mlp.astype(BF).reshape(blocks, rows, cols)
-
-
-def feed_forward_hidden(hid, top, up, down, bias, cut):
-    blocks, _, width = hid.shape
+    store_rows(acts, act.astype(BF))
+    store_rows(grads, (grad_act * slope).astype(BF))
+
+
+def output_kernel(*refs, count):
+    acts, grads, (up_ref, down_ref) = refs[:count], refs[count : 2 * count], refs[2 * count : 2 * count + 2]
+    mlps, backs = refs[-2 * count : -count], refs[-count:]
+    store_rows(backs, matmul(rows_of(grads), up_ref[...], 1, 1).astype(BF))
+    store_rows(mlps, matmul(rows_of(acts), down_ref[...], 1, 0).astype(BF))
+
+
+def feed_forward_hidden(hids, tops, up, down, bias, cut):
+    count = len(hids)
+    blocks, _, width = hids[0].shape
     rows = cut.stop - cut.start
     ff = up.shape[1]
     tile = 256 if ff % 256 == 0 else ff
     token = pl.BlockSpec((blocks, rows, width), lambda f: (0, cut.start // rows, 0))
     out_spec = pl.BlockSpec((blocks, rows, tile), lambda f: (0, 0, f))
-    size = blocks * rows
-    return pl.pallas_call(
-        hidden_kernel,
+    size = count * blocks * rows
+    outs = pl.pallas_call(
+        lambda *refs: hidden_kernel(*refs, count=count),
         grid=(ff // tile,),
         in_specs=[
-            token,
-            token,
+            *[token] * (2 * count),
             pl.BlockSpec((width, tile), lambda f: (0, f)),
             pl.BlockSpec((tile, width), lambda f: (f, 0)),
             pl.BlockSpec((1, tile), lambda f: (0, f)),
         ],
-        out_specs=[out_spec, out_spec],
-        out_shape=[jax.ShapeDtypeStruct((blocks, rows, ff), BF)] * 2,
+        out_specs=[out_spec] * (2 * count),
+        out_shape=[jax.ShapeDtypeStruct((blocks, rows, ff), BF)] * (2 * count),
         compiler_params=pltpu.CompilerParams(vmem_limit_bytes=48 << 20),
         cost_estimate=pl.CostEstimate(
             flops=8 * size * width * ff, bytes_accessed=4 * size * (width + ff) + 4 * up.size, transcendentals=size * ff
         ),
         name="feed_forward_hidden",
-    )(hid, top, up, down, bias)
-
-
-def feed_forward_output(act, grad_pre, up, down, cut, outs):
-    blocks, rows, ff = act.shape
+    )(*hids, *tops, up, down, bias)
+    return outs[:count], outs[count:]
+
+
+def feed_forward_output(acts, grads, up, down, cut, filled, all_rows):
+    count = len(acts)
+    blocks, rows, ff = acts[0].shape
     width = up.shape[0]
     tile = 256 if width % 256 == 0 else width
     token = pl.BlockSpec((blocks, rows, ff), lambda n: (0, 0, 0))
     out_spec = pl.BlockSpec((blocks, rows, tile), lambda n: (0, cut.start // rows, n))
-    filled = outs if isinstance(outs, (tuple, list)) else ()
-    shape = filled[0].shape if filled else (blocks, outs, width)
-    size = blocks * rows
-    return pl.pallas_call(
-        output_kernel,
+    size = count * blocks * rows
+    outs = pl.pallas_call(
+        lambda *refs: output_kernel(*refs, count=count),
         grid=(width // tile,),
         in_specs=[
-            token,
-            token,
+            *[token] * (2 * count),
             pl.BlockSpec((tile, ff), lambda n: (n, 0)),
             pl.BlockSpec((ff, tile), lambda n: (0, n)),
             *(pl.BlockSpec(memory_space=pl.ANY) for _ in filled),
         ],
-        out_specs=[out_spec, out_spec],
-        out_shape=[jax.ShapeDtypeStruct(shape, BF)] * 2,
-        input_output_aliases={4: 0, 5: 1} if filled else {},
+        out_specs=[out_spec] * (2 * count),
+        out_shape=[jax.ShapeDtypeStruct((blocks, all_rows, width), BF)] * (2 * count),
+        input_output_aliases={2 * count + 2 + at: at for at in range(len(filled))},
         compiler_params=pltpu.CompilerParams(vmem_limit_bytes=48 << 20),
         cost_estimate=pl.CostEstimate(
             flops=8 * size * width * ff, bytes_accessed=4 * size * (width + ff) + 4 * up.size, transcendentals=0
         ),
         name="feed_forward_output",
-    )(act, grad_pre, up, down, *filled)
+    )(*acts, *grads, up, down, *filled)
+    return outs[:count], outs[count:]
+
+
+def weight_grad_kernel(*refs, count):
+    lefts, rights, out_ref, turned = refs[:count], refs[count : 2 * count], refs[2 * count], refs[2 * count + 1]
+    rows = lefts[0].shape[0] * lefts[0].shape[1]
+
+    @pl.when(pl.program_id(0) == 0)
+    def _():
+        for at, left in enumerate(lefts):
+            turned[:, at * rows : (at + 1) * rows] = left[...].reshape(rows, left.shape[2]).T
+
+    total = matmul(turned[:, :rows], rights[0][...].reshape(rows, -1), 1, 0)
+    for at in range(1, count):
+        total = total + matmul(turned[:, at * rows : (at + 1) * rows], rights[at][...].reshape(rows, -1), 1, 0)
+    out_ref[...] = total.astype(BF)
+
+
+def weight_grad(lefts, rights, left_cut, right_cut):
+    count = len(lefts)
+
+    def rows_and_place(value, cut):
+        rows = value.shape[1] if cut is None else cut.stop - cut.start
+        return rows, 0 if cut is None else cut.start // rows
+
+    blocks, _, left_cols = lefts[0].shape
+    right_cols = rights[0].shape[2]
+    rows, left_at = rows_and_place(lefts[0], left_cut)
+    _, right_at = rows_and_place(rights[0], right_cut)
+    tile = next(tile for tile in (512, 384, right_cols) if right_cols % tile == 0)
+    tokens = count * blocks * rows
+    return pl.pallas_call(
+        lambda *refs: weight_grad_kernel(*refs, count=count),
+        grid=(right_cols // tile,),
+        in_specs=[
+            *[pl.BlockSpec((blocks, rows, left_cols), lambda n: (0, left_at, 0))] * count,
+            *[pl.BlockSpec((blocks, rows, tile), lambda n: (0, right_at, n))] * count,
+        ],
+        out_specs=pl.BlockSpec((left_cols, tile), lambda n: (0, n)),
+        out_shape=jax.ShapeDtypeStruct((left_cols, right_cols), BF),
+        scratch_shapes=[pltpu.VMEM((left_cols, tokens), BF)],
+        compiler_params=pltpu.CompilerParams(vmem_limit_bytes=48 << 20),
+        cost_estimate=pl.CostEstimate(
+            flops=3 * tokens * left_cols * right_cols,
+            bytes_accessed=2 * tokens * (left_cols + right_cols) + 2 * left_cols * right_cols,
+            transcendentals=0,
+        ),
+        name="weight_grad",
+    )(*lefts, *rights)
+
+
+def owner_kernel(place_ref, mine_ref, others_ref, out_ref):
+    take_mine = pl.program_id(1) % 2 == place_ref[0]
+    out_ref[...] = jnp.where(take_mine, mine_ref[:, 0], others_ref[:, 0]).astype(F32)
+
+
+def owner_columns(mine, others, xi, yi, parts):
+    streams, _, rows, cols = mine.shape
+    block = cols // parts
+    place = jnp.stack([xi, yi]).astype(jnp.int32)
+    spec = pl.BlockSpec(
+        (streams, 1, rows, block), lambda part, rank, place: (0, (rank // 2 + place[1]) % 2, 0, part)
+    )
+    return pl.pallas_call(
+        owner_kernel,
+        grid_spec=pltpu.PrefetchScalarGridSpec(
+            num_scalar_prefetch=1,
+            grid=(parts, 4),
+            in_specs=[spec, spec],
+            out_specs=pl.BlockSpec((streams, rows, block), lambda part, rank, place: (0, 0, part * 4 + rank)),
+        ),
+        out_shape=jax.ShapeDtypeStruct((streams, rows, 4 * cols), F32),
+        cost_estimate=pl.CostEstimate(flops=0, bytes_accessed=24 * mine.size, transcendentals=0),
+        name="owner_columns",
+    )(place, mine, others)
 
 
 def swap(value, axis):
@@ -269,14 +353,13 @@
     return value
 
 
-def after_these(values, others):
-    leaves, tree = jax.tree.flatten(values)
-    return jax.tree.unflatten(tree, lax.optimization_barrier((tuple(leaves), tuple(jax.tree.leaves(others))))[0])
-
-
-def gather_square(own, beside=((), ())):
-    from_x, from_y = after_these((swap(own, "x"), swap(own, "y")), beside[0])
-    corner_a, corner_b = after_these((swap(from_x[:1], "y"), swap(from_y[1:], "x")), beside[1])
+def together(values, others):
+    return lax.optimization_barrier((values, others))
+
+
+def gather_square(own):
+    from_x, from_y = swap(own, "x"), swap(own, "y")
+    corner_a, corner_b = swap(from_x[:1], "y"), swap(from_y[1:], "x")
     return jnp.concatenate([own, from_y], 0), jnp.concatenate([from_x, corner_a, corner_b], 0)
 
 
@@ -359,7 +442,9 @@
     mod_sent = swap(mod_peer, "c")
     mod_own = partial_mod(pick(ci, silu_own[:, 0], silu_own[:, 1]))
     mod = mod_own + mod_sent
-    mod_summed = mod
+    small = spread(jnp.concatenate([qv_b, proj_b, fc1_b, fc2_b], 1), ("z", "c", "y"))
+    small, mod = together(small, mod)
+    small = small.reshape(shards, 2, 2, 2, -1).swapaxes(1, 2).reshape(owners, 2, -1)
     mod_here = lax.dynamic_index_in_dim(mod, zi, 0, keepdims=False)
     for step in range(1, shards):
         there = lax.dynamic_index_in_dim(mod, (zi + step) % shards, 0, keepdims=False)
@@ -400,8 +485,8 @@
         return [((z * 4 + y * 2 + x) * ff_block, ff_block) for z in range(shards)]
 
     qkv_pair = rank_columns(qkv_w, qkv_offsets)
-    proj_swapped = swap(after_these(proj_w, qkv_pair[0]), "y")
-    qkv_held = by_owner(*after_these(qkv_pair, mod_summed))
+    proj_swapped = swap(proj_w, "y")
+    qkv_held = by_owner(*qkv_pair)
     qkv_gathered = lax.all_gather(qkv_held, ("z", "c"), axis=0)
     qkv_rank = [natural_rows(qkv_gathered[:, j]) for j in range(2)]
 
@@ -420,16 +505,19 @@
     offset, spread_one = statistics(tokens)
     normed = offset * spread_one
     hidden = (normed * (1.0 + vector(1)) + vector(0)).astype(BF)
-    hidden, ct_from_x, ct_from_y = after_these((hidden, ct_from_x, ct_from_y), (ct_from_x, ct_from_y))
-    ct_corner = swap(ct_from_x[:1], "y"), swap(ct_from_y[1:], "x")
     gate_live = mod[:, 5] * live
     gate_other = swap(gate_live, "x")
-    small = spread(jnp.concatenate(after_these((qv_b, proj_b, fc1_b, fc2_b), hidden), 1), ("y", "z", "c"))
-    hidden_seqs = gather_square(hidden, (small, ct_corner))
-    small = small.reshape(2, shards, 2, 2, -1).swapaxes(0, 1).reshape(owners, 2, -1)
-
-    proj_held = by_owner(*after_these((proj_w, proj_swapped), (hidden, qkv_held)))
-    fc1_w, fc2_w = after_these((fc1_w, fc2_w), hidden_seqs)
+    hidden_x, hidden_y = swap(hidden, "x"), swap(hidden, "y")
+    (ct_from_x, ct_from_y), (hidden_x, hidden_y) = together((ct_from_x, ct_from_y), (hidden_x, hidden_y))
+    hidden_corner = swap(hidden_x[:1], "y"), swap(hidden_y[1:], "x")
+    ct_corner = swap(ct_from_x[:1], "y"), swap(ct_from_y[1:], "x")
+    hidden_seqs = [
+        jnp.concatenate([hidden, hidden_y], 0),
+        jnp.concatenate([hidden_x, *hidden_corner], 0),
+    ]
+
+    proj_held = by_owner(proj_w, proj_swapped)
+    (fc1_w, fc2_w), hidden_seqs = together((fc1_w, fc2_w), hidden_seqs)
     up_pair = rank_columns(fc1_w, up_offsets)
 
     cuts = [0]
@@ -468,16 +556,18 @@
     qkv_seqs, mixed_seqs, lse_seqs = [], [], []
     for value in hidden_seqs:
         if mixed_seqs:
-            value = after_these(value, mixed_seqs)
+            value, mixed_seqs = together(value, mixed_seqs)
         pair = [
             (item + qkv_bias[j]).astype(BF)
             for j, item in enumerate(two_streams(value, qkv_rank, "btd,de->bte"))
         ]
+        if not mixed_seqs:
+            up_pair, pair = together(up_pair, pair)
+            up_held = by_owner(*up_pair)
         mixed, lse = attend_forward(*pair)
         qkv_seqs.append(pair)
         mixed_seqs.append(mixed)
         lse_seqs.append(lse)
-    up_held, down_sent = after_these((by_owner(*up_pair), down_sent), mixed_seqs[0])
     down_held = jnp.where(ci == xi, pick(ci, halves[0], halves[1]), down_sent)
 
     def gather_up(piece):
@@ -487,11 +577,11 @@
         return lax.all_gather(piece, ("z", "c"), axis=0, tiled=True)
 
     up_img = gather_up(up_held[0])
-    down_img = gather_down(after_these(down_held[0], mixed_seqs[1]))
+    down_img = gather_down(down_held[0])
     attn = jnp.concatenate(
         exchange_square(mixed_seqs[0][:2], mixed_seqs[0][2:], mixed_seqs[1][:2], mixed_seqs[1][2:]), -1
     )
-    up_rank = [up_img, gather_up(after_these(up_held[1], attn))]
+    up_rank = [up_img, gather_up(up_held[1])]
     rank = 2 * yi + xi
     relative = (0, 2, 1, 3)
     proj_rel = [
@@ -512,33 +602,42 @@
     offset_two, spread_two = statistics(after)
     normed_two = offset_two * spread_two
     hidden_two = (normed_two * (1.0 + vector(4)) + vector(3)).astype(BF)
+    (silu_cond, cotangents, ct_from_x, ct_corner), hidden_two = together(
+        (silu_cond, cotangents, ct_from_x, ct_corner), hidden_two
+    )
+    silu_all = spread(silu_cond, ("x",)).reshape(4 * shards, width)
     grad_y = cotangents.astype(F32) * live
 
     def gated(gate, blocks):
         return (jnp.where(stream_of_row, gate[1], gate[0]) * jnp.concatenate(blocks, 0).astype(F32)).astype(BF)
 
     grad_mlp_seqs = [
-        gated(gate_live, after_these((cotangents, ct_from_y), hidden_two)),
-        gated(gate_other, after_these((ct_from_x, *ct_corner), hidden_two)),
+        gated(gate_live, (cotangents, ct_from_y)),
+        gated(gate_other, (ct_from_x, *ct_corner)),
     ]
     grad_mlp = grad_mlp_seqs[0][:2]
-    down_rank = [down_img, gather_down(after_these(down_held[1], hidden_two))]
+    down_rank = [down_img, gather_down(down_held[1])]
     hidden_two_seqs = gather_square(hidden_two)
-    def hidden_of(j, hid, top):
-        return feed_forward_hidden(hid, top, up_rank[j], down_rank[j], up_bias[j : j + 1], streams[j])
-
-    act_img_other, pre_img_other = hidden_of(0, hidden_two_seqs[1], grad_mlp_seqs[1])
-    outs_other = feed_forward_output(act_img_other, pre_img_other, up_img, down_img, streams[0], img + txt)
-    act_img_own, pre_img_own = hidden_of(0, after_these(hidden_two_seqs[0], outs_other), grad_mlp_seqs[0])
-    outs_own = feed_forward_output(act_img_own, pre_img_own, up_img, down_img, streams[0], img + txt)
-    text_hids = after_these(hidden_two_seqs, outs_own)
-    act_txt_other, pre_txt_other = hidden_of(1, text_hids[1], grad_mlp_seqs[1])
-    mlp_other, back_other = feed_forward_output(
-        act_txt_other, pre_txt_other, up_rank[1], down_rank[1], streams[1], outs_other
-    )
-    act_txt_own, pre_txt_own = hidden_of(1, after_these(text_hids[0], back_other), grad_mlp_seqs[0])
-    mlp_own, back_own = feed_forward_output(act_txt_own, pre_txt_own, up_rank[1], down_rank[1], streams[1], outs_own)
-    back_relays = after_these(relay_square(back_other), back_own)
+    rows_all = img + txt
+
+    def hidden_of(j, hids, tops):
+        return feed_forward_hidden(hids, tops, up_rank[j], down_rank[j], up_bias[j : j + 1], streams[j])
+
+    def output_of(j, acts, pres, filled):
+        return feed_forward_output(acts, pres, up_rank[j], down_rank[j], streams[j], filled, rows_all)
+
+    act_img_other, pre_img_other = hidden_of(0, hidden_two_seqs[1:], grad_mlp_seqs[1:])
+    mlp_other, back_other = output_of(0, act_img_other, pre_img_other, ())
+    act_img_own, pre_img_own = hidden_of(0, hidden_two_seqs[:1], grad_mlp_seqs[:1])
+    mlp_own, back_own = output_of(0, act_img_own, pre_img_own, ())
+    act_img, pre_img = [*act_img_own, *act_img_other], [*pre_img_own, *pre_img_other]
+    act_txt, pre_txt = hidden_of(1, hidden_two_seqs, grad_mlp_seqs)
+    (mlp_own, mlp_other), (back_own, back_other) = output_of(
+        1, act_txt, pre_txt, (*mlp_own, *mlp_other, *back_own, *back_other)
+    )
+    (pre_img, act_txt, pre_txt), (back_own, back_other) = together((pre_img, act_txt, pre_txt), (back_own, back_other))
+    back_relays = relay_square(back_other)
+    back_first = swap(back_other[1:2], "x"), swap(back_own[2:3], "y")
 
     def replicas(value):
         return lax.psum(value, "r") if lax.axis_size("r") > 1 else value
@@ -554,32 +653,18 @@
         value = grad.reshape(shards, 2, 2, rows, cols).transpose(0, 2, 1, 3, 4).reshape(-1, cols)
         return lax.psum_scatter(value, ("z", "c"), scatter_dimension=0, tiled=True).reshape(2, rows, cols)
 
-    def owner_columns(mine, others, offsets):
-        by_rank = {}
-        for y in range(2):
-            for x in range(2):
-                by_rank[y, x] = pick(
-                    xi ^ x, pick(yi ^ y, mine[:, 0], mine[:, 1]), pick(yi ^ y, others[:, 0], others[:, 1])
-                )
-        places = []
-        for (y, x), piece in by_rank.items():
-            start = 0
-            for at, size in offsets(y, x):
-                places.append((at, piece[:, :, start : start + size].astype(F32)))
-                start += size
-        places.sort(key=lambda place: place[0])
-        return jnp.concatenate([piece for _, piece in places], 2)
-
     cut = streams[0]
-    down_grad_img = two_sums([act_img_own, act_img_other], [top[:, cut] for top in grad_mlp_seqs])
-    up_grad_img = two_sums([hid[:, cut] for hid in hidden_two_seqs], [pre_img_own, pre_img_other])
-    back_x, back_y = send_x(back_other, back_relays), send_y(back_own, back_relays)
-    cut = streams[1]
-    text = after_these((act_txt_own, act_txt_other, pre_txt_own, pre_txt_other), (back_own, back_relays))
-    down_grad_txt = two_sums(text[:2], [top[:, cut] for top in grad_mlp_seqs])
-    up_grad_txt = two_sums([hid[:, cut] for hid in hidden_two_seqs], text[2:])
-    back_x, back_y = after_these((back_x, back_y), (down_grad_txt, up_grad_txt))
-    grad_hidden_two = sum_square(back_own, back_x, back_y)
+    down_grad_img = two_sums(act_img, [top[:, cut] for top in grad_mlp_seqs])
+    up_grad_img = two_sums([hid[:, cut] for hid in hidden_two_seqs], pre_img)
+    down_grad_txt = weight_grad(act_txt, grad_mlp_seqs, None, streams[1])
+    (back_relays, back_first), (up_grad_img, down_grad_txt) = together(
+        (back_relays, back_first), (up_grad_img, down_grad_txt)
+    )
+    pre_txt, back_relays = together(pre_txt, back_relays)
+    back_last = swap(plus(back_other[:1], back_relays[0]), "x"), swap(plus(back_own[3:4], back_relays[1]), "y")
+    up_grad_txt = weight_grad(hidden_two_seqs, pre_txt, streams[1], None)
+    back_last, up_grad_txt = together(back_last, up_grad_txt)
+    grad_hidden_two = sum_square(back_own, (back_last[0], back_first[0]), (back_first[1], back_last[1]))
     grad_up = [owner_rows(up_grad_img), owner_rows(up_grad_txt)]
     grad_down = [
         lax.psum_scatter(down, ("z", "c"), scatter_dimension=0, tiled=True)
@@ -591,6 +676,7 @@
     grad_attn = jnp.concatenate(
         [item.astype(BF) for item in two_streams(grad_out, proj_rel, "bte,de->btd")], 1
     )
+    attn_late, grad_attn = together(attn, grad_attn)
     pieces = [grad_attn[:, :, i * rank_cols : (i + 1) * rank_cols] for i in range(4)]
     back = exchange_square(*pieces)
     grad_mixed_seqs = [jnp.concatenate(back[:2], 0), jnp.concatenate(back[2:], 0)]
@@ -604,22 +690,22 @@
             1,
         )
 
-    mlp_own, mlp_other = after_these((mlp_own, mlp_other), grad_mixed_seqs)
-    mlp_relays = relay_square(mlp_other)
-    mlp_x1, mlp_y2 = swap(mlp_other[1:2], "x"), swap(mlp_own[2:3], "y")
+    (mlp_own, mlp_other), grad_mixed_seqs = together((mlp_own, mlp_other), grad_mixed_seqs)
+    mlp_first = relay_square(mlp_other), swap(mlp_other[1:2], "x"), swap(mlp_own[2:3], "y")
     grad_pair_other = attend_backward(*qkv_seqs[1], lse_seqs[1], grad_mixed_seqs[1])
-    mlp_relays, mlp_x1, mlp_y2 = after_these((mlp_relays, mlp_x1, mlp_y2), grad_pair_other)
-    hidden_back_other = hidden_back(after_these(grad_pair_other, mlp_relays))
+    mlp_first, grad_pair_other = together(mlp_first, grad_pair_other)
+    mlp_relays, mlp_x1, mlp_y2 = mlp_first
+    hidden_back_other = hidden_back(grad_pair_other)
     mlp_x0 = swap(plus(mlp_other[:1], mlp_relays[0]), "x")
     mlp_y3 = swap(plus(mlp_own[3:4], mlp_relays[1]), "y")
 
-    grad_late = after_these(grad_out, hidden_back_other)
+    grad_late, hidden_back_other = together(grad_out, hidden_back_other)
     position = lax.select_n(
         rank ^ jnp.arange(4), *(jnp.full((4,), place, jnp.int32) for place in (0, 2, 1, 3))
     )
 
     def proj_rows(core):
-        blocks = [attn[:, :, at * rows : (at + 1) * rows] for at in range(16)]
+        blocks = [attn_late[:, :, at * rows : (at + 1) * rows] for at in range(16)]
         left = jnp.concatenate([pick(core, blocks[at], blocks[at + 1]) for at in range(0, 16, 2)], -1)
         return [
             jnp.einsum("btd,bte->de", left[:, cut], grad_late[:, cut], preferred_element_type=F32)
@@ -632,40 +718,47 @@
     proj_received = swap(proj_sent, "c")
 
     hidden_relays = relay_square(hidden_back_other)
-    grad_pair_own = attend_backward(
-        *qkv_seqs[0], lse_seqs[0], after_these(grad_mixed_seqs[0], (hidden_back_other, mlp_x1, mlp_y2, proj_kept))
-    )
-    hidden_relays = after_these(hidden_relays, grad_pair_own)
-    mlp_x0, mlp_y3 = after_these((mlp_x0, mlp_y3), grad_pair_own)
-    hidden_back_own = hidden_back(after_these(grad_pair_own, (hidden_relays, mlp_x0, mlp_y3)))
-    mlp = sum_square(mlp_own, (mlp_x0, mlp_x1), (mlp_y2, mlp_y3)) + with_bias(downb_full)
-    result = ((after + vector(5) * mlp) * live).astype(BF)
-    hidden_x = send_x(hidden_back_other, hidden_relays)
-    hidden_y = send_y(hidden_back_own, hidden_relays)
+    grad_mixed_own, (hidden_back_other, proj_kept) = together(grad_mixed_seqs[0], (hidden_back_other, proj_kept))
+    grad_pair_own = attend_backward(*qkv_seqs[0], lse_seqs[0], grad_mixed_own)
+    (hidden_relays, mlp_x0, mlp_y3), grad_pair_own = together((hidden_relays, mlp_x0, mlp_y3), grad_pair_own)
+    hidden_back_own = hidden_back(grad_pair_own)
+    grad_pairs, hidden_back_own = together([grad_pair_own, grad_pair_other], hidden_back_own)
+    hidden_first = swap(hidden_back_other[1:2], "x"), swap(hidden_back_own[2:3], "y")
+    hidden_last = (
+        swap(plus(hidden_back_other[:1], hidden_relays[0]), "x"),
+        swap(plus(hidden_back_own[3:4], hidden_relays[1]), "y"),
+    )
 
     def qkv_grad(j, pairs):
         return two_sums([hid[:, streams[j]] for hid in hidden_seqs], [pair[j] for pair in pairs])
 
-    grad_pairs = [grad_pair_own, grad_pair_other]
-    qkv_grad_img = qkv_grad(0, after_these(grad_pairs, hidden_back_own))
-    hidden_x, hidden_y0 = after_these((hidden_x, hidden_y[0]), qkv_grad_img)
-    qkv_grad_txt = qkv_grad(1, after_these(grad_pairs, hidden_y0))
+    qkv_grad_img = qkv_grad(0, grad_pairs)
+    hidden_first, qkv_grad_img = together(hidden_first, qkv_grad_img)
+    (grad_pairs, proj_received), hidden_first = together((grad_pairs, proj_received), hidden_first)
+    grad_proj = plus(proj_kept, proj_received)
+    grad_proj = jnp.concatenate([lax.dynamic_slice_in_dim(grad_proj, position[t], 1, 1) for t in range(4)], 1)
+    proj_kept, proj_received = split_swap(grad_proj, 2, yi, "y")
+    qkv_grad_txt = qkv_grad(1, grad_pairs)
     grad_qkv = jnp.stack([qkv_grad_img, qkv_grad_txt])
     cols = grad_qkv.shape[2]
     grad_qkv = grad_qkv.reshape(2, shards, 2, 2, rows, cols).transpose(1, 3, 0, 2, 4, 5)
     grad_qkv = grad_qkv.reshape(2 * shards, 2, 2, rows, cols)
-    proj_received = after_these(proj_received, grad_qkv)
-    grad_proj = plus(proj_kept, proj_received)
-    grad_proj = jnp.concatenate([lax.dynamic_slice_in_dim(grad_proj, position[t], 1, 1) for t in range(4)], 1)
-    proj_kept, proj_received = split_swap(grad_proj, 0, xi, "x")
-    hidden_last = after_these(hidden_y[1], (grad_qkv, proj_kept))
-    grad_hidden = sum_square(hidden_back_own, hidden_x, (hidden_y0, hidden_last))
+    hidden_last, (grad_qkv, proj_kept) = together(hidden_last, (grad_qkv, proj_kept))
+    grad_hidden = sum_square(
+        hidden_back_own, (hidden_last[0], hidden_first[0]), (hidden_first[1], hidden_last[1])
+    )
     grad_qkv = lax.psum_scatter(grad_qkv, ("z", "c"), scatter_dimension=0, tiled=True).reshape(2, 2, rows, cols)
 
-    up_pair = split_swap(replicas(after_these(jnp.stack(grad_up), grad_hidden)), 1, yi, "y")
-    down = replicas(after_these(jnp.stack(grad_down), grad_hidden))
+    (mlp_own, grad_pairs, grad_up, grad_down), grad_hidden = together(
+        (mlp_own, grad_pairs, grad_up, grad_down), grad_hidden
+    )
+    mlp = sum_square(mlp_own, (mlp_x0, mlp_x1), (mlp_y2, mlp_y3)) + with_bias(downb_full)
+    result = ((after + vector(5) * mlp) * live).astype(BF)
+    up_pair = split_swap(replicas(jnp.stack(grad_up)), 1, yi, "y")
+    down = replicas(jnp.stack(grad_down))
     down_other = swap(down, "x")
-    grad_hidden_late = after_these(grad_hidden, (up_pair[0], down))
+    grad_hidden_late, (up_kept, down) = together(grad_hidden, (up_pair[0], down))
+    up_pair = up_kept, up_pair[1]
 
     grad_tokens = grad_after + back_normalize(grad_hidden * (1.0 + vector(1)), normed, spread_one)
 
@@ -689,40 +782,29 @@
         ],
         1,
     ).reshape(2, 6 * width)
-    up_pair, proj_received = after_these((up_pair, proj_received), sums)
+    up_pair, sums = together(up_pair, sums)
     up_mine = jnp.concatenate(up_pair, 1)
-    proj_kept, proj_received = split_swap(plus(proj_kept, proj_received)[0], 1, yi, "y")
-    sums = after_these(sums, (up_mine, proj_kept))
-    up_others = swap(up_mine, "x")
     dmod = (sums + swap(sums, "y")).astype(BF)
+    (late_pre, late_out, late_mlp, proj_received), dmod = together(
+        ((pre_img, pre_txt), grad_out, grad_mlp, proj_received), dmod
+    )
+    proj_kept, proj_received = split_swap(plus(proj_kept, proj_received), 0, xi, "x")
     dmod_rep = spread(dmod, ("z", "c"))
     qkv_pair = split_swap(replicas(grad_qkv), 1, yi, "y")
-    up_others, late_pre, late_out, late_mlp, dmod_rep, down_other, proj_received = after_these(
-        (
-            up_others,
-            (pre_img_own, pre_img_other, pre_txt_own, pre_txt_other),
-            grad_out,
-            grad_mlp,
-            dmod_rep,
-            down_other,
-            proj_received,
-        ),
-        qkv_pair[0],
-    )
-    g_fc1_w = owner_columns(up_mine, up_others, up_offsets)
+    (dmod_rep, proj_kept), qkv_kept = together((dmod_rep, proj_kept), qkv_pair[0])
+    qkv_pair = qkv_kept, qkv_pair[1]
     grad_proj = plus(proj_kept, proj_received).reshape(shards * rows, width)
     grad_proj = replicas(lax.psum_scatter(grad_proj, "z", scatter_dimension=0, tiled=True))
     g_proj_w = paired(xi, grad_proj[None], swap(grad_proj, "x")[None], 0).astype(F32)
     blocks = (pick(xi, down, down_other), pick(xi, down_other, down))
     g_fc2_w = paired(ci, pick(ci, *blocks), swap(pick(ci, blocks[1], blocks[0]), "c"), 1).astype(F32)
     qkv_mine = jnp.concatenate(qkv_pair, 1)
-    g_qkv_w = owner_columns(qkv_mine, swap(qkv_mine, "x"), qkv_offsets)
+    g_qkv_w = owner_columns(qkv_mine, swap(qkv_mine, "x"), xi, yi, 3)
     dsilu_part = jnp.einsum("sjm,jdm->sd", dmod_rep, ada_w, preferred_element_type=F32)
     dsilu = spread(dsilu_part, ("z", "y", "c")).transpose(1, 0, 2).reshape(2 * shards, owners * rows)
     gate = jax.nn.sigmoid(cond_value)
     d_cond = dsilu * gate * (1.0 + cond_value * (1.0 - gate))
     dmod_all = spread(dmod_rep, ("x",)).reshape(4 * shards, 2, 6 * width)
-    silu_all = spread(silu_cond, ("x",)).reshape(4 * shards, width)
     if lax.axis_size("r") > 1:
         dmod_all = lax.all_gather(dmod_all, "r", axis=0, tiled=True)
         silu_all = lax.all_gather(silu_all, "r", axis=0, tiled=True)
@@ -739,13 +821,15 @@
     qv_sums = jnp.stack([qkv_sums[:, 0], qkv_sums[:, 2]], 1)
     qv_placed = (qv_sums[:, :, None, None] * here[:, :, None]).reshape(2, 2 * width)
     up_sums = jnp.stack(
-        [sum(jnp.sum(pre.astype(F32), axis=(0, 1)) for pre in late_pre[2 * j : 2 * j + 2]) for j in range(2)]
+        [sum(jnp.sum(pre.astype(F32), axis=(0, 1)) for pre in late_pre[j]) for j in range(2)]
     ).reshape(2, shards, ff_block)
     up_placed = (up_sums[:, :, None, None] * here[:, :, None]).reshape(2, owners * ff_block)
     biases = jnp.concatenate(
         [qv_placed, token_sums(late_out.astype(F32)), up_placed, token_sums(late_mlp.astype(F32))], 1
     )
-    biases = replicas(total(biases, ("c", "y", "x", "z")))
+    biases = replicas(total(biases, ("c", "y", "z", "x")))
+    up_mine, biases = together(up_mine, biases)
+    g_fc1_w = owner_columns(up_mine, swap(up_mine, "x"), xi, yi, shards)
     g_biases = []
     start = 0
     for item in (qv_b, proj_b, fc1_b, fc2_b):

time: 1050 us -> 977 us (0.930)
  waiting for transfers between devices: 284 us -> 220 us
  matrix products: 118 us -> 98.9 us
  other arithmetic: 175 us -> 186 us
    ppermute x56, waiting for transfers between devices: 220 us -> 169 us  [swap(): return lax.ppermute(value, axis, FLIP)]
    pallas_call x8 -> x10, Pallas kernels: 85.8 us -> 103 us  [the longest x3 39.2 us: feed_forward_hidden(): pl.pallas_call(lambda *refs: hidden_kernel(*refs, count=count), grid=(ff...]
    pallas_call x2, Pallas kernels: 49.4 us -> 33.2 us  [attend_forward(): pl.pallas_call(lambda *refs: attend_forward_kernel(*refs, heads=heads, sc...]
    dot_general x12 -> x8, matrix products: 64.5 us -> 53.1 us  [two_sums(): jnp.einsum('btd,bte->de', left, right, preferred_element_type=F32)]
    unnamed x398 -> x315, local copies, waits for them, and re-layouts: 61.9 us -> 51.4 us
    convert_element_type x8 -> x9, other arithmetic: 17.7 us -> 22.5 us  [plus(): return (first.astype(F32) + second.astype(F32)).astype(BF)]
    select_n x20 -> x16, other arithmetic: 30 us -> 27.7 us  [pick(): return jnp.where(index == 0, first, second)]
  transfers between devices with their start and end apart: 91 -> 91, of which waited for: 41 -> 34; matrix products, arithmetic and copies ran while one was open for 40% -> 41% of each run, Pallas kernels for 18% -> 20%
where the time goes in v3:
time: 977 us; the launch traced here: 968 us
  waiting for transfers between devices  220 us (23%)
  Pallas kernels  189 us (19%)
  other arithmetic  186 us (19%)
  local copies, waits for them, and re-layouts  164 us (17%)
  matrix products  98.9 us (10%)
  starting transfers between devices  84.8 us (9%)
  between operations  25.2 us (3%)
    ppermute x56, waiting for transfers between devices, swap(): return lax.ppermute(value, axis, FLIP)  169 us
    ppermute x56, starting transfers between devices, swap(): return lax.ppermute(value, axis, FLIP)  59.1 us
    dot_general x8, matrix products, two_sums(): jnp.einsum('btd,bte->de', left, right, preferred_element_type=F32)  53.1 us
    pallas_call x2, Pallas kernels, attend_backward(): pl.pallas_call(lambda *refs: attend_backward_kernel(*refs, heads=heads, s...  52.3 us
    unnamed x315, local copies, waits for them, and re-layouts  51.4 us
    pallas_call x3, Pallas kernels, feed_forward_hidden(): pl.pallas_call(lambda *refs: hidden_kernel(*refs, count=count), grid=(ff...  39.2 us
    pallas_call x2, Pallas kernels, attend_forward(): pl.pallas_call(lambda *refs: attend_forward_kernel(*refs, heads=heads, sc...  33.2 us
    pallas_call x3, Pallas kernels, feed_forward_output(): pl.pallas_call(lambda *refs: output_kernel(*refs, count=count), grid=(wid...  32.7 us
  transfers between devices with their start and end apart: 91, of which 34 were waited for; matrix products, arithmetic and copies ran while one was open for 41% of the time, Pallas kernels for 20%

profile of v3, /device:TPU:0, one launch (start us, length us, event | category | flops | bytes accessed | tf_op | source)
XLA Modules:
  0.0 968.0 jit_solution(15941752648014926681)
XLA Ops:
  12.5 10.2 %collective-permute-done.18 = bf16[2,96,1152]{2,1,0:T(8,128)(2,1)S(1)} collective-permute-done((bf16[2,96,1152]{2,1,0:T(8,128)(2,1)S(1)}, bf16[2,96,1152]{2,1,0:T(8,128)(2,1)S(1)}, u32[]{:S(2)}, u32[]{:S(2)}) %collective-permute-start.18) | collective-permute-done | bytes 442400 | tf_op jit(solution)/shard_map/ppermute | solution.py:305
  30.8 9.8 %collective-permute-done.22 = bf16[2,96,1536]{2,1,0:T(8,128)(2,1)} collective-permute-done((bf16[2,96,1536]{2,1,0:T(8,128)(2,1)}, bf16[2,96,1536]{2,1,0:T(8,128)(2,1)}, u32[]{:S(2)}, u32[]{:S(2)}) %collective-permute-start.22) | collective-permute-done | bytes 589856 | tf_op jit(solution)/shard_map/ppermute | solution.py:305
  120.7 27.4 %collective-permute-done.13 = bf16[2,256,1536]{2,1,0:T(8,128)(2,1)} collective-permute-done((bf16[2,256,1536]{2,1,0:T(8,128)(2,1)}, bf16[2,256,1536]{2,1,0:T(8,128)(2,1)}, u32[]{:S(2)}, u32[]{:S(2)}) %collective-permute-start.13) | collective-permute-done | bytes 1572896 | tf_op jit(solution)/shard_map/ppermute | solution.py:305
  149.6 29.4 %collective-permute-done.11 = bf16[2,256,1536]{2,1,0:T(8,128)(2,1)} collective-permute-done((bf16[2,256,1536]{2,1,0:T(8,128)(2,1)}, bf16[2,256,1536]{2,1,0:T(8,128)(2,1)}, u32[]{:S(2)}, u32[]{:S(2)}) %collective-permute-start.11) | collective-permute-done | bytes 1572896 | tf_op jit(solution)/shard_map/ppermute | solution.py:305
  188.9 8.5 collective-permute-done.15
  236.9 16.6 %attend_forward.2 = (bf16[4,256,384]{2,1,0:T(8,128)(2,1)S(1)}, f32[6,1024]{1,0:T(8,128)S(1)}) custom-call(bf16[4,224,1152]{2,1,0:T(8,128)(2,1)S(1)} %copy-done.31, bf16[4,32,1152]{2,1,0:T(8,128)(2,1)S(1)} %copy-done.23), custom_call_target="tpu_custom_call" | custom-call | flops 14495514624 | bytes 4718592 | tf_op jit(solution)/shard_map/attend_forward/pallas_call | solution.py:104
  259.5 16.6 %attend_forward.3 = (bf16[4,256,384]{2,1,0:T(8,128)(2,1)S(1)}, f32[6,1024]{1,0:T(8,128)S(1)}) custom-call(bf16[4,224,1152]{2,1,0:T(8,128)(2,1)S(1)} %fusion.14.refs_0_, bf16[4,32,1152]{2,1,0:T(8,128)(2,1)S(1)} %fusion.34.refs_1_), custom_call_target="tpu_custom_call" | custom-call | flops 14495514624 | bytes 4718592 | tf_op jit(solution)/shard_map/attend_forward/pallas_call | solution.py:104
  290.7 8.4 collective-permute-done.21
  334.8 24.0 %collective-permute-done.26 = bf16[2,256,1536]{2,1,0:T(8,128)(2,1)S(1)} collective-permute-done((bf16[2,256,1536]{2,1,0:T(8,128)(2,1)S(1)}, bf16[2,256,1536]{2,1,0:T(8,128)(2,1)S(1)}, u32[]{:S(2)}, u32[]{:S(2)}) %collective-permute-start.26) | collective-permute-done | bytes 1572896 | tf_op jit(solution)/shard_map/ppermute | solution.py:305
  365.7 10.0 %collective-permute-done.27 = bf16[1,256,1536]{2,1,0:T(8,128)(2,1)S(1)} collective-permute-done((bf16[1,256,1536]{2,1,0:T(8,128)(2,1)S(1)}, bf16[1,256,1536]{2,1,0:T(8,128)(2,1)S(1)}, u32[]{:S(2)}, u32[]{:S(2)}) %collective-permute-start.27) | collective-permute-done | bytes 786464 | tf_op jit(solution)/shard_map/ppermute | solution.py:305
  382.7 15.5 %feed_forward_hidden.4 = (bf16[4,224,1536]{2,1,0:T(8,128)(2,1)S(1)}, bf16[4,224,1536]{2,1,0:T(8,128)(2,1)S(1)}) custom-call(bf16[4,256,1536]{2,1,0:T(8,128)(2,1)} %constant_dynamic-update-slice_fusion.4.refs_0_, bf16[4,256,1536]{2,1,0:T(8,128)(2,1)} %multiply_convert_fusion.1.refs_2_.refs_1_, bf16[1536,1536]{1,0:T(8,128)(2,1)} %bitcast.275, ...), custom_call_target="tpu_custom_call" | custom-call | flops 16911433728 | bytes 20447232 | tf_op jit(solution)/shard_map/feed_forward_hidden/pallas_call | solution.py:181
  399.8 7.8 fusion.24
  409.0 15.6 %feed_forward_hidden.5 = (bf16[4,224,1536]{2,1,0:T(8,128)(2,1)S(1)}, bf16[4,224,1536]{2,1,0:T(8,128)(2,1)S(1)}) custom-call(bf16[4,256,1536]{2,1,0:T(8,128)(2,1)} %constant_dynamic-update-slice_fusion.6.refs_1_.refs_0_, bf16[4,256,1536]{2,1,0:T(8,128)(2,1)} %multiply_convert_fusion.refs_3_.refs_1_, bf16[1536,1536]{1,0:T(8,128)(2,1)} %bitcast.276, ...), custom_call_target="tpu_custom_call" | custom-call | flops 16911433728 | bytes 20447232 | tf_op jit(solution)/shard_map/feed_forward_hidden/pallas_call | solution.py:181
  426.2 9.2 fusion.1
  441.9 8.2 feed_forward_hidden.3
  452.2 12.5 %feed_forward_output.4 = (bf16[4,256,1536]{2,1,0:T(8,128)(2,1)}, bf16[4,256,1536]{2,1,0:T(8,128)(2,1)}) custom-call(bf16[4,224,1536]{2,1,0:T(8,128)(2,1)S(1)} %copy-done.28, bf16[4,224,1536]{2,1,0:T(8,128)(2,1)S(1)} %copy-done.14, bf16[1536,1536]{1,0:T(8,128)(2,1)} %bitcast.277, bf16[1536,1536]{1,0:T(8,128)(2,1)} %bitcast.321), custom_call_target="tpu_custom_call" | custom-call | flops 16911433728 | bytes 20447232 | tf_op jit(solution)/shard_map/feed_forward_output/pallas_call | solution.py:209
  466.6 12.4 %feed_forward_output.3 = (bf16[4,256,1536]{2,1,0:T(8,128)(2,1)}, bf16[4,256,1536]{2,1,0:T(8,128)(2,1)}) custom-call(bf16[4,224,1536]{2,1,0:T(8,128)(2,1)S(1)} %copy-done.30, bf16[4,224,1536]{2,1,0:T(8,128)(2,1)S(1)} %copy-done.11, bf16[1536,1536]{1,0:T(8,128)(2,1)} %bitcast.278, bf16[1536,1536]{1,0:T(8,128)(2,1)} %bitcast.322), custom_call_target="tpu_custom_call" | custom-call | flops 16911433728 | bytes 20447232 | tf_op jit(solution)/shard_map/feed_forward_output/pallas_call | solution.py:209
  480.9 7.7 feed_forward_output.5
  505.4 7.9 fusion.27
  513.3 7.7 fusion.2
  521.1 6.9 collective-permute-done.33
  556.5 5.8 weight_grad.3
  606.9 26.3 %attend_backward.2 = (bf16[4,224,1152]{2,1,0:T(8,128)(2,1)S(1)}, bf16[4,32,1152]{2,1,0:T(8,128)(2,1)S(1)}) custom-call(bf16[4,224,1152]{2,1,0:T(8,128)(2,1)S(1)} %copy-done.34, bf16[4,32,1152]{2,1,0:T(8,128)(2,1)S(1)} %copy-done.26, f32[6,1024]{1,0:T(8,128)S(1)} %copy-done.38, bf16[4,256,384]{2,1,0:T(8,128)(2,1)S(1)} %pad_maximum_fusion.19.refs_3_), custom_call_target="tpu_custom_call" | custom-call | flops 36238786560 | bytes 4718592 | tf_op jit(solution)/shard_map/attend_backward/pallas_call | solution.py:118
  660.6 26.1 %attend_backward.3 = (bf16[4,224,1152]{2,1,0:T(8,128)(2,1)S(1)}, bf16[4,32,1152]{2,1,0:T(8,128)(2,1)S(1)}) custom-call(bf16[4,224,1152]{2,1,0:T(8,128)(2,1)S(1)} %copy-done.32, bf16[4,32,1152]{2,1,0:T(8,128)(2,1)S(1)} %copy-done.24, f32[6,1024]{1,0:T(8,128)S(1)} %copy-done.36, bf16[4,256,384]{2,1,0:T(8,128)(2,1)S(1)} %pad_maximum_fusion.18.refs_3_), custom_call_target="tpu_custom_call" | custom-call | flops 36238786560 | bytes 4718592 | tf_op jit(solution)/shard_map/attend_backward/pallas_call | solution.py:118
  704.1 6.2 convolution_bitcast_fusion.4
  710.3 8.1 fusion.5
  750.4 7.1 fusion.22
  795.7 15.2 %collective-permute-done.56 = bf16[2,1,96,1536]{3,2,1,0:T(8,128)(2,1)} collective-permute-done((bf16[2,1,96,1536]{3,2,1,0:T(8,128)(2,1)}, bf16[2,1,96,1536]{3,2,1,0:T(8,128)(2,1)}, u32[]{:S(2)}, u32[]{:S(2)}) %collective-permute-start.56) | collective-permute-done | bytes 589856 | tf_op jit(solution)/shard_map/ppermute | solution.py:305
  859.4 9.3 collective-permute-done.73
  885.0 9.7 collective-permute-done.76.others_ref
  894.6 11.4 %owner_columns.3 = f32[2,96,6144]{2,1,0:T(8,128)} custom-call(s32[2]{0:T(128)} %pad_add_fusion.place_ref, bf16[2,2,96,1536]{3,2,1,0:T(8,128)(2,1)} %pad_maximum_fusion.16.mine_ref, bf16[2,2,96,1536]{3,2,1,0:T(8,128)(2,1)} %collective-permute-done.76.others_ref), custom_call_target="tpu_custom_call" | custom-call | bytes 14155776 | tf_op jit(solution)/shard_map/owner_columns/pallas_call | solution.py:290
  949.8 8.8 owner_columns.2
  (789 shorter events, 536.6 us)
Async XLA Ops:
  7.2 199.2 %all-gather.15.cloned.1.call-start = ((), (), s32[]{:S(2)}) async-start(), calls=%async_computation.14 | async-start | bytes 7962624 | tf_op jit(solution)/shard_map/all_gather | solution.py:490
  23.8 281.0 %all-gather.17.cloned.1.call-start = ((), (), s32[]{:S(2)}) async-start(), calls=%async_computation.15 | async-start | bytes 10616832 | tf_op jit(solution)/shard_map/all_gather | solution.py:547
  43.1 334.7 %all-gather.13.cloned.1.call-start = ((), (), s32[]{:S(2)}) async-start(), calls=%async_computation.7 | async-start | bytes 5308416 | tf_op jit(solution)/shard_map/all_gather | solution.py:574
  46.9 56.9 %collective-permute-start = (bf16[1,256,1536]{2,1,0:T(8,128)(2,1)}, bf16[1,256,1536]{2,1,0:T(8,128)(2,1)}, u32[]{:S(2)}, u32[]{:S(2)}) collective-permute-start(bf16[1,256,1536]{2,1,0:T(8,128)(2,1)} %get-tuple-element.411), channel_id=1, source_target_pairs={{0,1},{1,0},{2,3},{3,2},{4,5},{5,4},{6,7},{7,6},{8,9},{9,8},{10,11... | collective-permute-start | bytes 2359304 | tf_op jit(solution)/shard_map/ppermute | solution.py:305
  56.1 57.4 %collective-permute-start.10 = (bf16[1,256,1536]{2,1,0:T(8,128)(2,1)}, bf16[1,256,1536]{2,1,0:T(8,128)(2,1)}, u32[]{:S(2)}, u32[]{:S(2)}) collective-permute-start(bf16[1,256,1536]{2,1,0:T(8,128)(2,1)} %get-tuple-element.413), channel_id=1, source_target_pairs={{0,1},{1,0},{2,3},{3,2},{4,5},{5,4},{6,7},{7,6},{8,9},{9,8},{10,11... | collective-permute-start | bytes 2359304 | tf_op jit(solution)/shard_map/ppermute | solution.py:305
  110.5 37.7 %collective-permute-start.13 = (bf16[2,256,1536]{2,1,0:T(8,128)(2,1)}, bf16[2,256,1536]{2,1,0:T(8,128)(2,1)}, u32[]{:S(2)}, u32[]{:S(2)}) collective-permute-start(bf16[2,256,1536]{2,1,0:T(8,128)(2,1)} %fusion.16), channel_id=1, source_target_pairs={{0,16},{16,0},{1,17},{17,1},{2,18},{18,2},{3,19},{19,3},{4,20},{20... | collective-permute-start | bytes 4718600 | tf_op jit(solution)/shard_map/ppermute | solution.py:305
  112.0 37.7 %collective-permute-start.14 = (bf16[2,256,1536]{2,1,0:T(8,128)(2,1)}, bf16[2,256,1536]{2,1,0:T(8,128)(2,1)}, u32[]{:S(2)}, u32[]{:S(2)}) collective-permute-start(bf16[2,256,1536]{2,1,0:T(8,128)(2,1)} %fusion.16), channel_id=1, source_target_pairs={{0,2},{2,0},{1,3},{3,1},{4,6},{6,4},{5,7},{7,5},{8,10},{10,8},{9,1... | collective-permute-start | bytes 4718600 | tf_op jit(solution)/shard_map/ppermute | solution.py:305
  116.1 62.9 %collective-permute-start.11 = (bf16[2,256,1536]{2,1,0:T(8,128)(2,1)}, bf16[2,256,1536]{2,1,0:T(8,128)(2,1)}, u32[]{:S(2)}, u32[]{:S(2)}) collective-permute-start(bf16[2,256,1536]{2,1,0:T(8,128)(2,1)} %pad_maximum_fusion.9), channel_id=1, source_target_pairs={{0,16},{16,0},{1,17},{17,1},{2,18},{18,2},{3,19},{19,3},{4,20},{20... | collective-permute-start | bytes 4718600 | tf_op jit(solution)/shard_map/ppermute | solution.py:305
  116.6 63.3 %collective-permute-start.12 = (bf16[2,256,1536]{2,1,0:T(8,128)(2,1)}, bf16[2,256,1536]{2,1,0:T(8,128)(2,1)}, u32[]{:S(2)}, u32[]{:S(2)}) collective-permute-start(bf16[2,256,1536]{2,1,0:T(8,128)(2,1)} %pad_maximum_fusion.9), channel_id=1, source_target_pairs={{0,2},{2,0},{1,3},{3,1},{4,6},{6,4},{5,7},{7,5},{8,10},{10,8},{9,1... | collective-permute-start | bytes 4718600 | tf_op jit(solution)/shard_map/ppermute | solution.py:305
  222.8 159.9 %all-gather.21.cloned.1.call-start = ((), (), s32[]{:S(2)}) async-start(), calls=%async_computation.17 | async-start | bytes 5308416 | tf_op jit(solution)/shard_map/all_gather | solution.py:577
  231.7 205.2 %all-gather.11.cloned.1.call-start = ((), (), s32[]{:S(2)}) async-start(), calls=%async_computation.6 | async-start | bytes 5308416 | tf_op jit(solution)/shard_map/all_gather | solution.py:574
  232.3 209.6 %all-gather.19.cloned.1.call-start = ((), (), s32[]{:S(2)}) async-start(), calls=%async_computation.16 | async-start | bytes 5308416 | tf_op jit(solution)/shard_map/all_gather | solution.py:577
  285.1 39.4 %collective-permute-start.23 = (bf16[1,256,1536]{2,1,0:T(8,128)(2,1)}, bf16[1,256,1536]{2,1,0:T(8,128)(2,1)}, u32[]{:S(2)}, u32[]{:S(2)}) collective-permute-start(bf16[1,256,1536]{2,1,0:T(8,128)(2,1)} %slice.734), channel_id=1, source_target_pairs={{0,2},{2,0},{1,3},{3,1},{4,6},{6,4},{5,7},{7,5},{8,10},{10,8},{9,1... | collective-permute-start | bytes 2359304 | tf_op jit(solution)/shard_map/ppermute | solution.py:305
  288.9 35.6 %collective-permute-start.24 = (bf16[1,256,1536]{2,1,0:T(8,128)(2,1)}, bf16[1,256,1536]{2,1,0:T(8,128)(2,1)}, u32[]{:S(2)}, u32[]{:S(2)}) collective-permute-start(bf16[1,256,1536]{2,1,0:T(8,128)(2,1)} %slice.735), channel_id=1, source_target_pairs={{0,16},{16,0},{1,17},{17,1},{2,18},{18,2},{3,19},{19,3},{4,20},{20... | collective-permute-start | bytes 2359304 | tf_op jit(solution)/shard_map/ppermute | solution.py:305
  290.6 459.8 %reduce-scatter.11.cloned.1.call-start = ((), (), s32[]{:S(2)}) async-start(), calls=%async_computation.10 | async-start | bytes 5308416 | tf_op jit(solution)/shard_map/reduce_scatter | solution.py:670
  324.6 34.2 %collective-permute-start.26 = (bf16[2,256,1536]{2,1,0:T(8,128)(2,1)S(1)}, bf16[2,256,1536]{2,1,0:T(8,128)(2,1)S(1)}, u32[]{:S(2)}, u32[]{:S(2)}) collective-permute-start(bf16[2,256,1536]{2,1,0:T(8,128)(2,1)S(1)} %add_convert_fusion.2), channel_id=1, source_target_pairs={{0,16},{16,0},{1,17},{17,1},{2,18},{18,2},{3,19},{19,3},{4,20},{20... | collective-permute-start | bytes 4718600 | tf_op jit(solution)/shard_map/ppermute | solution.py:305
  436.9 313.5 %reduce-scatter.7.cloned.1.call-start = ((), (), s32[]{:S(2)}) async-start(), calls=%async_computation.8 | async-start | bytes 5308416 | tf_op jit(solution)/shard_map/reduce_scatter | solution.py:654
  530.4 220.0 %reduce-scatter.13.cloned.1.call-start = ((), (), s32[]{:S(2)}) async-start(), calls=%async_computation.11 | async-start | bytes 5308416 | tf_op jit(solution)/shard_map/reduce_scatter | solution.py:670
  531.2 219.2 %reduce-scatter.9.cloned.1.call-start = ((), (), s32[]{:S(2)}) async-start(), calls=%async_computation.9 | async-start | bytes 5308416 | tf_op jit(solution)/shard_map/reduce_scatter | solution.py:654
  591.6 283.8 %reduce-scatter.15.cloned.1.call-start = ((), (), s32[]{:S(2)}) async-start(), calls=%async_computation.12 | async-start | bytes 7962624 | tf_op jit(solution)/shard_map/reduce_scatter | solution.py:750
  651.6 37.0 %collective-permute-start.47 = (bf16[1,256,1536]{2,1,0:T(8,128)(2,1)}, bf16[1,256,1536]{2,1,0:T(8,128)(2,1)S(1)}, u32[]{:S(2)}, u32[]{:S(2)}) collective-permute-start(bf16[1,256,1536]{2,1,0:T(8,128)(2,1)} %add_convert_fusion.6), channel_id=1, source_target_pairs={{0,2},{2,0},{1,3},{3,1},{4,6},{6,4},{5,7},{7,5},{8,10},{10,8},{9,1... | collective-permute-start | bytes 2359304 | tf_op jit(solution)/shard_map/ppermute | solution.py:305
  655.1 35.4 %collective-permute-start.46 = (bf16[1,256,1536]{2,1,0:T(8,128)(2,1)}, bf16[1,256,1536]{2,1,0:T(8,128)(2,1)S(1)}, u32[]{:S(2)}, u32[]{:S(2)}) collective-permute-start(bf16[1,256,1536]{2,1,0:T(8,128)(2,1)} %add_convert_fusion.7), channel_id=1, source_target_pairs={{0,16},{16,0},{1,17},{17,1},{2,18},{18,2},{3,19},{19,3},{4,20},{20... | collective-permute-start | bytes 2359304 | tf_op jit(solution)/shard_map/ppermute | solution.py:305
  660.5 59.7 %collective-permute-start.48 = (bf16[2,4,2,96,1536]{4,3,2,1,0:T(8,128)(2,1)}, bf16[2,4,2,96,1536]{4,3,2,1,0:T(8,128)(2,1)}, u32[]{:S(2)}, u32[]{:S(2)}) collective-permute-start(bf16[2,4,2,96,1536]{4,3,2,1,0:T(8,128)(2,1)} %pad_maximum_fusion.2), channel_id=1, source_target_pairs={{0,1},{1,0},{2,3},{3,2},{4,5},{5,4},{6,7},{7,6},{8,9},{9,8},{10,11... | collective-permute-start | bytes 14155784 | tf_op jit(solution)/shard_map/ppermute | solution.py:305
  700.4 44.4 %collective-permute-start.52 = (bf16[1,256,1536]{2,1,0:T(8,128)(2,1)}, bf16[1,256,1536]{2,1,0:T(8,128)(2,1)}, u32[]{:S(2)}, u32[]{:S(2)}) collective-permute-start(bf16[1,256,1536]{2,1,0:T(8,128)(2,1)} %add_convert_fusion.4), channel_id=1, source_target_pairs={{0,2},{2,0},{1,3},{3,1},{4,6},{6,4},{5,7},{7,5},{8,10},{10,8},{9,1... | collective-permute-start | bytes 2359304 | tf_op jit(solution)/shard_map/ppermute | solution.py:305
  703.8 41.0 %collective-permute-start.51 = (bf16[1,256,1536]{2,1,0:T(8,128)(2,1)}, bf16[1,256,1536]{2,1,0:T(8,128)(2,1)}, u32[]{:S(2)}, u32[]{:S(2)}) collective-permute-start(bf16[1,256,1536]{2,1,0:T(8,128)(2,1)} %add_convert_fusion.5), channel_id=1, source_target_pairs={{0,16},{16,0},{1,17},{17,1},{2,18},{18,2},{3,19},{19,3},{4,20},{20... | collective-permute-start | bytes 2359304 | tf_op jit(solution)/shard_map/ppermute | solution.py:305
  744.8 71.1 %collective-permute-start.55 = (bf16[2,4,1,96,1536]{4,3,2,1,0:T(8,128)(2,1)}, bf16[2,4,1,96,1536]{4,3,2,1,0:T(8,128)(2,1)}, u32[]{:S(2)}, u32[]{:S(2)}) collective-permute-start(bf16[2,4,1,96,1536]{4,3,2,1,0:T(8,128)(2,1)} %get-tuple-element.330), channel_id=1, source_target_pairs={{0,2},{2,0},{1,3},{3,1},{4,6},{6,4},{5,7},{7,5},{8,10},{10,8},{9,1... | collective-permute-start | bytes 7077896 | tf_op jit(solution)/shard_map/ppermute | solution.py:305
  745.7 193.4 %reduce-scatter.17.cloned.1.call-start = ((), (), s32[]{:S(2)}) async-start(), calls=%async_computation.13 | async-start | bytes 1474560 | tf_op jit(solution)/shard_map/reduce_scatter | solution.py:797
  760.0 112.2 %collective-permute-start.77 = (bf16[2,192,1536]{2,1,0:T(8,128)(2,1)}, bf16[2,192,1536]{2,1,0:T(8,128)(2,1)}, u32[]{:S(2)}, u32[]{:S(2)}) collective-permute-start(bf16[2,192,1536]{2,1,0:T(8,128)(2,1)} %pad_maximum_fusion.15), channel_id=1, source_target_pairs={{0,16},{16,0},{1,17},{17,1},{2,18},{18,2},{3,19},{19,3},{4,20},{20... | collective-permute-start | bytes 3538952 | tf_op jit(solution)/shard_map/ppermute | solution.py:305
  788.7 91.5 %collective-permute-start.54 = (f32[1,256,1536]{2,1,0:T(8,128)}, f32[1,256,1536]{2,1,0:T(8,128)}, u32[]{:S(2)}, u32[]{:S(2)}) collective-permute-start(f32[1,256,1536]{2,1,0:T(8,128)} %get-tuple-element.337), channel_id=1, source_target_pairs={{0,1},{1,0},{2,3},{3,2},{4,5},{5,4},{6,7},{7,6},{8,9},{9,8},{10,11... | collective-permute-start | bytes 4718600 | tf_op jit(solution)/shard_map/ppermute | solution.py:305
  790.0 57.2 %collective-permute-start.53 = (bf16[1,256,1536]{2,1,0:T(8,128)(2,1)}, bf16[1,256,1536]{2,1,0:T(8,128)(2,1)}, u32[]{:S(2)}, u32[]{:S(2)}) collective-permute-start(bf16[1,256,1536]{2,1,0:T(8,128)(2,1)} %get-tuple-element.389), channel_id=1, source_target_pairs={{0,1},{1,0},{2,3},{3,2},{4,5},{5,4},{6,7},{7,6},{8,9},{9,8},{10,11... | collective-permute-start | bytes 2359304 | tf_op jit(solution)/shard_map/ppermute | solution.py:305
  840.2 66.9 %collective-permute-start.74 = (bf16[1,4,1,96,1536]{4,3,2,1,0:T(8,128)(2,1)}, bf16[1,4,1,96,1536]{4,3,2,1,0:T(8,128)(2,1)}, u32[]{:S(2)}, u32[]{:S(2)}) collective-permute-start(bf16[1,4,1,96,1536]{4,3,2,1,0:T(8,128)(2,1)} %get-tuple-element.348), channel_id=1, source_target_pairs={{0,16},{16,0},{1,17},{17,1},{2,18},{18,2},{3,19},{19,3},{4,20},{20... | collective-permute-start | bytes 3538952 | tf_op jit(solution)/shard_map/ppermute | solution.py:305
  875.4 35.8 %collective-permute-start.78 = (bf16[2,192,1536]{2,1,0:T(8,128)(2,1)}, bf16[2,192,1536]{2,1,0:T(8,128)(2,1)}, u32[]{:S(2)}, u32[]{:S(2)}) collective-permute-start(bf16[2,192,1536]{2,1,0:T(8,128)(2,1)} %get-tuple-element.347), channel_id=1, source_target_pairs={{0,1},{1,0},{2,3},{3,2},{4,5},{5,4},{6,7},{7,6},{8,9},{9,8},{10,11... | collective-permute-start | bytes 3538952 | tf_op jit(solution)/shard_map/ppermute | solution.py:305
  (211 other events, 1996.4 us)
Sparse Core Ops, SparseCore 0:
  23.9 79.9 all-gather.14
  106.0 89.3 all-gather.16
  222.9 53.3 all-gather.12
  277.8 50.4 all-gather.20
  329.8 50.4 all-gather.10
  381.8 50.5 all-gather.18
  437.0 57.3 reduce-scatter.10
  530.6 57.5 reduce-scatter.6
  590.5 53.3 reduce-scatter.12
  646.6 53.3 reduce-scatter.8
  745.9 78.8 reduce-scatter.14
  910.1 28.9 reduce-scatter.16

commit v4 on v3

--- a/solution.py
+++ b/solution.py
@@ -44,7 +44,7 @@
 
 
 def attend_backward_kernel(
-    img_ref, txt_ref, lse_ref, grad_ref, img_out, txt_out, key_sum, value_sum, *, heads, scale
+    img_ref, txt_ref, lse_ref, grad_ref, img_out, txt_out, sums_out, key_sum, value_sum, *, heads, scale
 ):
     blocks, img_rows = img_ref.shape[:2]
     txt_rows = txt_ref.shape[1]
@@ -57,6 +57,7 @@
         keys = join_streams(img_ref, txt_ref, key_cut)
         values = join_streams(img_ref, txt_ref, value_cut)
         keys_t = keys.T
+        query_sums = [0.0, 0.0]
         for block in range(blocks):
             queries = jnp.concatenate([img_ref[block, :, cut], txt_ref[block, :, cut]], 0)
             grad = grad_ref[block, :, cut]
@@ -76,6 +77,18 @@
             grad_query = (matmul(keys_t, grad_raw, 1, 0) * HD**-0.5).T.astype(BF)
             img_out[block, :, cut] = grad_query[:img_rows]
             txt_out[block, :, cut] = grad_query[img_rows:]
+            grad_query = grad_query.astype(F32)
+            query_sums[0] += jnp.sum(grad_query[:img_rows], axis=0, keepdims=True)
+            query_sums[1] += jnp.sum(grad_query[img_rows:], axis=0, keepdims=True)
+        rounded = value_sum[...].astype(BF).astype(F32)
+        value_sums = (
+            jnp.sum(rounded[: blocks * img_rows], axis=0, keepdims=True),
+            jnp.sum(rounded[blocks * img_rows :], axis=0, keepdims=True),
+        )
+        for stream in range(2):
+            sums_out[stream : stream + 1, cut] = query_sums[stream]
+            sums_out[stream : stream + 1, key_cut] = jnp.zeros((1, HD), F32)
+            sums_out[stream : stream + 1, value_cut] = value_sums[stream]
         for there, total, factor in ((key_cut, key_sum, HD**-0.5), (value_cut, value_sum, 1.0)):
             for block in range(blocks):
                 img_out[block, :, there] = (total[block * img_rows : (block + 1) * img_rows] * factor).astype(BF)
@@ -118,8 +131,12 @@
     return pl.pallas_call(
         lambda *refs: attend_backward_kernel(*refs, heads=heads, scale=HD**-0.5 * LOG2E),
         in_specs=[whole(value.shape) for value in (img, txt, lse, grad)],
-        out_specs=[whole(img.shape), whole(txt.shape)],
-        out_shape=[jax.ShapeDtypeStruct(img.shape, BF), jax.ShapeDtypeStruct(txt.shape, BF)],
+        out_specs=[whole(img.shape), whole(txt.shape), whole((2, img.shape[2]))],
+        out_shape=[
+            jax.ShapeDtypeStruct(img.shape, BF),
+            jax.ShapeDtypeStruct(txt.shape, BF),
+            jax.ShapeDtypeStruct((2, img.shape[2]), F32),
+        ],
         scratch_shapes=[pltpu.VMEM((length, HD), F32), pltpu.VMEM((length, HD), F32)],
         compiler_params=pltpu.CompilerParams(vmem_limit_bytes=40 << 20),
         cost_estimate=attend_cost(img, txt, heads, 5),
@@ -154,12 +171,14 @@
 
 def hidden_kernel(*refs, count):
     hids, tops, (up_ref, down_ref, bias_ref) = refs[:count], refs[count : 2 * count], refs[2 * count : 2 * count + 3]
-    acts, grads = refs[2 * count + 3 : 3 * count + 3], refs[3 * count + 3 :]
+    acts, grads, sums_ref = refs[2 * count + 3 : 3 * count + 3], refs[3 * count + 3 : -1], refs[-1]
     pre = matmul(rows_of(hids), up_ref[...], 1, 0) + bias_ref[...]
     grad_act = matmul(rows_of(tops), down_ref[...], 1, 1)
     act, slope = gelu_and_slope(pre)
     store_rows(acts, act.astype(BF))
-    store_rows(grads, (grad_act * slope).astype(BF))
+    grad_pre = (grad_act * slope).astype(BF)
+    store_rows(grads, grad_pre)
+    sums_ref[...] = jnp.sum(grad_pre.astype(F32), axis=0, keepdims=True)
 
 
 def output_kernel(*refs, count):
@@ -187,15 +206,18 @@
             pl.BlockSpec((tile, width), lambda f: (f, 0)),
             pl.BlockSpec((1, tile), lambda f: (0, f)),
         ],
-        out_specs=[out_spec] * (2 * count),
-        out_shape=[jax.ShapeDtypeStruct((blocks, rows, ff), BF)] * (2 * count),
+        out_specs=[*[out_spec] * (2 * count), pl.BlockSpec((1, tile), lambda f: (0, f))],
+        out_shape=[
+            *[jax.ShapeDtypeStruct((blocks, rows, ff), BF)] * (2 * count),
+            jax.ShapeDtypeStruct((1, ff), F32),
+        ],
         compiler_params=pltpu.CompilerParams(vmem_limit_bytes=48 << 20),
         cost_estimate=pl.CostEstimate(
             flops=8 * size * width * ff, bytes_accessed=4 * size * (width + ff) + 4 * up.size, transcendentals=size * ff
         ),
         name="feed_forward_hidden",
     )(*hids, *tops, up, down, bias)
-    return outs[:count], outs[count:]
+    return outs[:count], outs[count : 2 * count], outs[-1]
 
 
 def feed_forward_output(acts, grads, up, down, cut, filled, all_rows):
@@ -276,26 +298,28 @@
 
 
 def owner_kernel(place_ref, mine_ref, others_ref, out_ref):
-    take_mine = pl.program_id(1) % 2 == place_ref[0]
-    out_ref[...] = jnp.where(take_mine, mine_ref[:, 0], others_ref[:, 0]).astype(F32)
+    block = mine_ref.shape[3]
+    for rank in range(4):
+        y = (rank // 2 + place_ref[1]) % 2
+        piece = jnp.where(rank % 2 == place_ref[0], mine_ref[:, y], others_ref[:, y])
+        out_ref[:, :, rank * block : (rank + 1) * block] = piece.astype(F32)
 
 
 def owner_columns(mine, others, xi, yi, parts):
     streams, _, rows, cols = mine.shape
     block = cols // parts
     place = jnp.stack([xi, yi]).astype(jnp.int32)
-    spec = pl.BlockSpec(
-        (streams, 1, rows, block), lambda part, rank, place: (0, (rank // 2 + place[1]) % 2, 0, part)
-    )
+    spec = pl.BlockSpec((streams, 2, rows, block), lambda part, place: (0, 0, 0, part))
     return pl.pallas_call(
         owner_kernel,
         grid_spec=pltpu.PrefetchScalarGridSpec(
             num_scalar_prefetch=1,
-            grid=(parts, 4),
+            grid=(parts,),
             in_specs=[spec, spec],
-            out_specs=pl.BlockSpec((streams, rows, block), lambda part, rank, place: (0, 0, part * 4 + rank)),
+            out_specs=pl.BlockSpec((streams, rows, 4 * block), lambda part, place: (0, 0, part)),
         ),
         out_shape=jax.ShapeDtypeStruct((streams, rows, 4 * cols), F32),
+        compiler_params=pltpu.CompilerParams(vmem_limit_bytes=32 << 20),
         cost_estimate=pl.CostEstimate(flops=0, bytes_accessed=24 * mine.size, transcendentals=0),
         name="owner_columns",
     )(place, mine, others)
@@ -626,12 +650,12 @@
     def output_of(j, acts, pres, filled):
         return feed_forward_output(acts, pres, up_rank[j], down_rank[j], streams[j], filled, rows_all)
 
-    act_img_other, pre_img_other = hidden_of(0, hidden_two_seqs[1:], grad_mlp_seqs[1:])
+    act_img_other, pre_img_other, sums_other = hidden_of(0, hidden_two_seqs[1:], grad_mlp_seqs[1:])
     mlp_other, back_other = output_of(0, act_img_other, pre_img_other, ())
-    act_img_own, pre_img_own = hidden_of(0, hidden_two_seqs[:1], grad_mlp_seqs[:1])
+    act_img_own, pre_img_own, sums_own = hidden_of(0, hidden_two_seqs[:1], grad_mlp_seqs[:1])
     mlp_own, back_own = output_of(0, act_img_own, pre_img_own, ())
     act_img, pre_img = [*act_img_own, *act_img_other], [*pre_img_own, *pre_img_other]
-    act_txt, pre_txt = hidden_of(1, hidden_two_seqs, grad_mlp_seqs)
+    act_txt, pre_txt, sums_txt = hidden_of(1, hidden_two_seqs, grad_mlp_seqs)
     (mlp_own, mlp_other), (back_own, back_other) = output_of(
         1, act_txt, pre_txt, (*mlp_own, *mlp_other, *back_own, *back_other)
     )
@@ -673,6 +697,10 @@
     grad_after = grad_y + back_normalize(grad_hidden_two * (1.0 + vector(4)), normed_two, spread_two)
     grad_out = (vector(2) * grad_after).astype(BF)
 
+    def token_sums(value):
+        return jnp.stack([jnp.sum(value[:, cut].astype(F32), axis=(0, 1)) for cut in streams])
+
+    out_sums, mlp_sums = token_sums(grad_out), token_sums(grad_mlp)
     grad_attn = jnp.concatenate(
         [item.astype(BF) for item in two_streams(grad_out, proj_rel, "bte,de->btd")], 1
     )
@@ -749,9 +777,7 @@
     )
     grad_qkv = lax.psum_scatter(grad_qkv, ("z", "c"), scatter_dimension=0, tiled=True).reshape(2, 2, rows, cols)
 
-    (mlp_own, grad_pairs, grad_up, grad_down), grad_hidden = together(
-        (mlp_own, grad_pairs, grad_up, grad_down), grad_hidden
-    )
+    (mlp_own, grad_up, grad_down), grad_hidden = together((mlp_own, grad_up, grad_down), grad_hidden)
     mlp = sum_square(mlp_own, (mlp_x0, mlp_x1), (mlp_y2, mlp_y3)) + with_bias(downb_full)
     result = ((after + vector(5) * mlp) * live).astype(BF)
     up_pair = split_swap(replicas(jnp.stack(grad_up)), 1, yi, "y")
@@ -767,9 +793,6 @@
 
     result = from_slot(result)
     grad_tokens = from_slot(grad_tokens)
-
-    def token_sums(value):
-        return jnp.stack([jnp.sum(value[:, cut], axis=(0, 1)) for cut in streams])
 
     sums = jnp.stack(
         [
@@ -785,9 +808,7 @@
     up_pair, sums = together(up_pair, sums)
     up_mine = jnp.concatenate(up_pair, 1)
     dmod = (sums + swap(sums, "y")).astype(BF)
-    (late_pre, late_out, late_mlp, proj_received), dmod = together(
-        ((pre_img, pre_txt), grad_out, grad_mlp, proj_received), dmod
-    )
+    proj_received, dmod = together(proj_received, dmod)
     proj_kept, proj_received = split_swap(plus(proj_kept, proj_received), 0, xi, "x")
     dmod_rep = spread(dmod, ("z", "c"))
     qkv_pair = split_swap(replicas(grad_qkv), 1, yi, "y")
@@ -815,17 +836,13 @@
     )
 
     here = ((jnp.arange(2)[:, None] == yi) & (jnp.arange(2)[None] == xi)).astype(F32)
-    qkv_sums = jnp.stack(
-        [sum(jnp.sum(pair[j].astype(F32), axis=(0, 1)) for pair in grad_pairs) for j in range(2)]
-    ).reshape(2, 3, rank_cols)
+    qkv_sums = (grad_pair_own[2] + grad_pair_other[2]).reshape(2, 3, rank_cols)
     qv_sums = jnp.stack([qkv_sums[:, 0], qkv_sums[:, 2]], 1)
     qv_placed = (qv_sums[:, :, None, None] * here[:, :, None]).reshape(2, 2 * width)
-    up_sums = jnp.stack(
-        [sum(jnp.sum(pre.astype(F32), axis=(0, 1)) for pre in late_pre[j]) for j in range(2)]
-    ).reshape(2, shards, ff_block)
+    up_sums = jnp.concatenate([sums_own + sums_other, sums_txt], 0).reshape(2, shards, ff_block)
     up_placed = (up_sums[:, :, None, None] * here[:, :, None]).reshape(2, owners * ff_block)
     biases = jnp.concatenate(
-        [qv_placed, token_sums(late_out.astype(F32)), up_placed, token_sums(late_mlp.astype(F32))], 1
+        [qv_placed, out_sums, up_placed, mlp_sums], 1
     )
     biases = replicas(total(biases, ("c", "y", "z", "x")))
     up_mine, biases = together(up_mine, biases)

time: 977 us -> 963 us (0.986)
    ppermute x56, waiting for transfers between devices: 169 us -> 190 us  [swap(): return lax.ppermute(value, axis, FLIP)]
    ppermute x18, waiting for transfers between devices: 32.2 us -> 17 us  [shift_xor(): lax.ppermute(value, axis, [(i, i ^ bit) for i in range(lax.axis_size(axis...]
    pallas_call x2, Pallas kernels: 20.2 us -> 9.08 us  [owner_columns(): pl.pallas_call(owner_kernel, grid_spec=pltpu.PrefetchScalarGridSpec(num_s...]
    unnamed x315 -> x326, local copies, waits for them, and re-layouts: 51.4 us -> 49.7 us
  transfers between devices with their start and end apart: 91 -> 91, of which waited for: 34 -> 35; matrix products, arithmetic and copies ran while one was open for 41% -> 41% of each run, Pallas kernels for 20% -> 19%
where the time goes in v4:
time: 963 us; the launch traced here: 953 us
  waiting for transfers between devices  226 us (23%)
  Pallas kernels  181 us (19%)
  other arithmetic  179 us (19%)
  local copies, waits for them, and re-layouts  161 us (17%)
  matrix products  93.3 us (10%)
  starting transfers between devices  87.9 us (9%)
  between operations  25.2 us (3%)
    ppermute x56, waiting for transfers between devices, swap(): return lax.ppermute(value, axis, FLIP)  190 us
    ppermute x56, starting transfers between devices, swap(): return lax.ppermute(value, axis, FLIP)  55 us
    pallas_call x2, Pallas kernels, attend_backward(): pl.pallas_call(lambda *refs: attend_backward_kernel(*refs, heads=heads, s...  52.5 us
    unnamed x326, local copies, waits for them, and re-layouts  49.7 us
    dot_general x8, matrix products, two_sums(): jnp.einsum('btd,bte->de', left, right, preferred_element_type=F32)  46.7 us
    pallas_call x3, Pallas kernels, feed_forward_hidden(): pl.pallas_call(lambda *refs: hidden_kernel(*refs, count=count), grid=(ff...  41.8 us
    pallas_call x2, Pallas kernels, attend_forward(): pl.pallas_call(lambda *refs: attend_forward_kernel(*refs, heads=heads, sc...  33.2 us
    pallas_call x3, Pallas kernels, feed_forward_output(): pl.pallas_call(lambda *refs: output_kernel(*refs, count=count), grid=(wid...  32.8 us
  transfers between devices with their start and end apart: 91, of which 35 were waited for; matrix products, arithmetic and copies ran while one was open for 41% of the time, Pallas kernels for 19%

profile of v4, /device:TPU:0, one launch (start us, length us, event | category | flops | bytes accessed | tf_op | source)
XLA Modules:
  0.0 953.3 jit_solution(9146557890853600535)
XLA Ops:
  12.5 10.2 %collective-permute-done.18 = bf16[2,96,1152]{2,1,0:T(8,128)(2,1)S(1)} collective-permute-done((bf16[2,96,1152]{2,1,0:T(8,128)(2,1)S(1)}, bf16[2,96,1152]{2,1,0:T(8,128)(2,1)S(1)}, u32[]{:S(2)}, u32[]{:S(2)}) %collective-permute-start.18) | collective-permute-done | bytes 442400 | tf_op jit(solution)/shard_map/ppermute | solution.py:329
  30.0 10.6 %collective-permute-done.22 = bf16[2,96,1536]{2,1,0:T(8,128)(2,1)} collective-permute-done((bf16[2,96,1536]{2,1,0:T(8,128)(2,1)}, bf16[2,96,1536]{2,1,0:T(8,128)(2,1)}, u32[]{:S(2)}, u32[]{:S(2)}) %collective-permute-start.22) | collective-permute-done | bytes 589856 | tf_op jit(solution)/shard_map/ppermute | solution.py:329
  98.5 5.2 broadcast_select_fusion.11
  120.8 27.4 %collective-permute-done.13 = bf16[2,256,1536]{2,1,0:T(8,128)(2,1)} collective-permute-done((bf16[2,256,1536]{2,1,0:T(8,128)(2,1)}, bf16[2,256,1536]{2,1,0:T(8,128)(2,1)}, u32[]{:S(2)}, u32[]{:S(2)}) %collective-permute-start.13) | collective-permute-done | bytes 1572896 | tf_op jit(solution)/shard_map/ppermute | solution.py:329
  149.7 29.4 %collective-permute-done.11 = bf16[2,256,1536]{2,1,0:T(8,128)(2,1)} collective-permute-done((bf16[2,256,1536]{2,1,0:T(8,128)(2,1)}, bf16[2,256,1536]{2,1,0:T(8,128)(2,1)}, u32[]{:S(2)}, u32[]{:S(2)}) %collective-permute-start.11) | collective-permute-done | bytes 1572896 | tf_op jit(solution)/shard_map/ppermute | solution.py:329
  189.0 8.4 collective-permute-done.15
  236.8 16.6 %attend_forward.2 = (bf16[4,256,384]{2,1,0:T(8,128)(2,1)S(1)}, f32[6,1024]{1,0:T(8,128)S(1)}) custom-call(bf16[4,224,1152]{2,1,0:T(8,128)(2,1)S(1)} %copy-done.38, bf16[4,32,1152]{2,1,0:T(8,128)(2,1)S(1)} %copy-done.16), custom_call_target="tpu_custom_call" | custom-call | flops 14495514624 | bytes 4718592 | tf_op jit(solution)/shard_map/attend_forward/pallas_call | solution.py:117
  260.0 16.6 %attend_forward.3 = (bf16[4,256,384]{2,1,0:T(8,128)(2,1)S(1)}, f32[6,1024]{1,0:T(8,128)S(1)}) custom-call(bf16[4,224,1152]{2,1,0:T(8,128)(2,1)S(1)} %fusion.14.refs_0_, bf16[4,32,1152]{2,1,0:T(8,128)(2,1)S(1)} %fusion.34.refs_1_), custom_call_target="tpu_custom_call" | custom-call | flops 14495514624 | bytes 4718592 | tf_op jit(solution)/shard_map/attend_forward/pallas_call | solution.py:117
  291.2 8.3 collective-permute-done.21
  335.9 23.5 %collective-permute-done.26 = bf16[2,256,1536]{2,1,0:T(8,128)(2,1)S(1)} collective-permute-done((bf16[2,256,1536]{2,1,0:T(8,128)(2,1)S(1)}, bf16[2,256,1536]{2,1,0:T(8,128)(2,1)S(1)}, u32[]{:S(2)}, u32[]{:S(2)}) %collective-permute-start.26) | collective-permute-done | bytes 1572896 | tf_op jit(solution)/shard_map/ppermute | solution.py:329
  366.1 10.2 %collective-permute-done.27 = bf16[1,256,1536]{2,1,0:T(8,128)(2,1)S(1)} collective-permute-done((bf16[1,256,1536]{2,1,0:T(8,128)(2,1)S(1)}, bf16[1,256,1536]{2,1,0:T(8,128)(2,1)S(1)}, u32[]{:S(2)}, u32[]{:S(2)}) %collective-permute-start.27) | collective-permute-done | bytes 786464 | tf_op jit(solution)/shard_map/ppermute | solution.py:329
  384.1 16.6 %feed_forward_hidden.4 = (bf16[4,224,1536]{2,1,0:T(8,128)(2,1)S(1)}, bf16[4,224,1536]{2,1,0:T(8,128)(2,1)S(1)}, f32[1,1536]{1,0:T(1,128)S(1)}) custom-call(bf16[4,256,1536]{2,1,0:T(8,128)(2,1)} %constant_dynamic-update-slice_fusion.4.refs_0_, bf16[4,256,1536]{2,1,0:T(8,128)(2,1)} %multiply_convert_fusion.1.refs_2_.refs_1_, bf16[1536,1536]{1,0:T(8,128)(2,1)} %bitcast.275, ...), custom_call_target="tpu_custom_call" | custom-call | flops 16911433728 | bytes 20447232 | tf_op jit(solution)/shard_map/feed_forward_hidden/pallas_call | solution.py:200
  400.7 7.7 fusion.24
  409.9 16.5 %feed_forward_hidden.5 = (bf16[4,224,1536]{2,1,0:T(8,128)(2,1)S(1)}, bf16[4,224,1536]{2,1,0:T(8,128)(2,1)S(1)}, f32[1,1536]{1,0:T(1,128)S(1)}) custom-call(bf16[4,256,1536]{2,1,0:T(8,128)(2,1)} %constant_dynamic-update-slice_fusion.6.refs_1_.refs_0_, bf16[4,256,1536]{2,1,0:T(8,128)(2,1)} %multiply_convert_fusion.refs_3_.refs_1_, ...), custom_call_target="tpu_custom_call" | custom-call | flops 16911433728 | bytes 20447232 | tf_op jit(solution)/shard_map/feed_forward_hidden/pallas_call | solution.py:200
  428.6 9.1 fusion.1
  444.3 8.7 feed_forward_hidden.3
  453.6 12.7 %feed_forward_output.4 = (bf16[4,256,1536]{2,1,0:T(8,128)(2,1)}, bf16[4,256,1536]{2,1,0:T(8,128)(2,1)}) custom-call(bf16[4,224,1536]{2,1,0:T(8,128)(2,1)S(1)} %copy-done.33, bf16[4,224,1536]{2,1,0:T(8,128)(2,1)S(1)} %copy-done.30, bf16[1536,1536]{1,0:T(8,128)(2,1)} %bitcast.277, bf16[1536,1536]{1,0:T(8,128)(2,1)} %bitcast.324), custom_call_target="tpu_custom_call" | custom-call | flops 16911433728 | bytes 20447232 | tf_op jit(solution)/shard_map/feed_forward_output/pallas_call | solution.py:231
  466.3 12.4 %feed_forward_output.3 = (bf16[4,256,1536]{2,1,0:T(8,128)(2,1)}, bf16[4,256,1536]{2,1,0:T(8,128)(2,1)}) custom-call(bf16[4,224,1536]{2,1,0:T(8,128)(2,1)S(1)} %copy-done.37, bf16[4,224,1536]{2,1,0:T(8,128)(2,1)S(1)} %copy-done.35, bf16[1536,1536]{1,0:T(8,128)(2,1)} %bitcast.278, bf16[1536,1536]{1,0:T(8,128)(2,1)} %bitcast.325), custom_call_target="tpu_custom_call" | custom-call | flops 16911433728 | bytes 20447232 | tf_op jit(solution)/shard_map/feed_forward_output/pallas_call | solution.py:231
  480.7 7.7 feed_forward_output.5
  499.5 5.6 weight_grad.2
  505.1 7.9 fusion.27
  513.0 7.7 fusion.2
  520.8 6.5 collective-permute-done.33
  564.9 5.8 weight_grad.3
  622.2 26.4 %attend_backward.2 = (bf16[4,224,1152]{2,1,0:T(8,128)(2,1)S(1)}, bf16[4,32,1152]{2,1,0:T(8,128)(2,1)S(1)}, f32[2,1152]{1,0:T(2,128)S(1)}) custom-call(bf16[4,224,1152]{2,1,0:T(8,128)(2,1)S(1)} %copy-done.41, bf16[4,32,1152]{2,1,0:T(8,128)(2,1)S(1)} %copy-done.19, f32[6,1024]{1,0:T(8,128)S(1)} %copy-done.45, bf16[4,256,384]{2,1,0:T(8,128)(2,1)S(1)} %pad_maximum_fusion.19.refs_3_), custom_call_target="tpu_custom_call" | custom-call | flops 36238786560 | bytes 4718592 | tf_op jit(solution)/shard_map/attend_backward/pallas_call | solution.py:131
  673.8 26.2 %attend_backward.3 = (bf16[4,224,1152]{2,1,0:T(8,128)(2,1)S(1)}, bf16[4,32,1152]{2,1,0:T(8,128)(2,1)S(1)}, f32[2,1152]{1,0:T(2,128)S(1)}) custom-call(bf16[4,224,1152]{2,1,0:T(8,128)(2,1)S(1)} %copy-done.39, bf16[4,32,1152]{2,1,0:T(8,128)(2,1)S(1)} %copy-done.17, f32[6,1024]{1,0:T(8,128)S(1)} %copy-done.43, bf16[4,256,384]{2,1,0:T(8,128)(2,1)S(1)} %pad_maximum_fusion.18.refs_3_), custom_call_target="tpu_custom_call" | custom-call | flops 36238786560 | bytes 4718592 | tf_op jit(solution)/shard_map/attend_backward/pallas_call | solution.py:131
  707.0 5.4 convolution_convert_fusion
  740.3 5.9 fusion.5
  789.9 5.6 fusion.22
  812.3 28.3 %collective-permute-done.56 = bf16[2,1,96,1536]{3,2,1,0:T(8,128)(2,1)} collective-permute-done((bf16[2,1,96,1536]{3,2,1,0:T(8,128)(2,1)}, bf16[2,1,96,1536]{3,2,1,0:T(8,128)(2,1)}, u32[]{:S(2)}, u32[]{:S(2)}) %collective-permute-start.56) | collective-permute-done | bytes 589856 | tf_op jit(solution)/shard_map/ppermute | solution.py:329
  887.9 9.9 %collective-permute-done.74 = bf16[1,4,1,96,1536]{4,3,2,1,0:T(8,128)(2,1)} collective-permute-done((bf16[1,4,1,96,1536]{4,3,2,1,0:T(8,128)(2,1)}, bf16[1,4,1,96,1536]{4,3,2,1,0:T(8,128)(2,1)}, u32[]{:S(2)}, u32[]{:S(2)}) %collective-permute-start.74) | collective-permute-done | bytes 1179680 | tf_op jit(solution)/shard_map/ppermute | solution.py:329
  902.2 5.3 fusion.36
  (784 shorter events, 523.8 us)
Async XLA Ops:
  7.2 199.2 %all-gather.15.cloned.1.call-start = ((), (), s32[]{:S(2)}) async-start(), calls=%async_computation.14 | async-start | bytes 7962624 | tf_op jit(solution)/shard_map/all_gather | solution.py:514
  23.8 281.5 %all-gather.17.cloned.1.call-start = ((), (), s32[]{:S(2)}) async-start(), calls=%async_computation.15 | async-start | bytes 10616832 | tf_op jit(solution)/shard_map/all_gather | solution.py:571
  43.1 335.3 %all-gather.13.cloned.1.call-start = ((), (), s32[]{:S(2)}) async-start(), calls=%async_computation.7 | async-start | bytes 5308416 | tf_op jit(solution)/shard_map/all_gather | solution.py:598
  46.9 56.9 %collective-permute-start = (bf16[1,256,1536]{2,1,0:T(8,128)(2,1)}, bf16[1,256,1536]{2,1,0:T(8,128)(2,1)}, u32[]{:S(2)}, u32[]{:S(2)}) collective-permute-start(bf16[1,256,1536]{2,1,0:T(8,128)(2,1)} %get-tuple-element.401), channel_id=1, source_target_pairs={{0,1},{1,0},{2,3},{3,2},{4,5},{5,4},{6,7},{7,6},{8,9},{9,8},{10,11... | collective-permute-start | bytes 2359304 | tf_op jit(solution)/shard_map/ppermute | solution.py:329
  56.1 57.5 %collective-permute-start.10 = (bf16[1,256,1536]{2,1,0:T(8,128)(2,1)}, bf16[1,256,1536]{2,1,0:T(8,128)(2,1)}, u32[]{:S(2)}, u32[]{:S(2)}) collective-permute-start(bf16[1,256,1536]{2,1,0:T(8,128)(2,1)} %get-tuple-element.403), channel_id=1, source_target_pairs={{0,1},{1,0},{2,3},{3,2},{4,5},{5,4},{6,7},{7,6},{8,9},{9,8},{10,11... | collective-permute-start | bytes 2359304 | tf_op jit(solution)/shard_map/ppermute | solution.py:329
  110.5 37.7 %collective-permute-start.13 = (bf16[2,256,1536]{2,1,0:T(8,128)(2,1)}, bf16[2,256,1536]{2,1,0:T(8,128)(2,1)}, u32[]{:S(2)}, u32[]{:S(2)}) collective-permute-start(bf16[2,256,1536]{2,1,0:T(8,128)(2,1)} %fusion.16), channel_id=1, source_target_pairs={{0,16},{16,0},{1,17},{17,1},{2,18},{18,2},{3,19},{19,3},{4,20},{20... | collective-permute-start | bytes 4718600 | tf_op jit(solution)/shard_map/ppermute | solution.py:329
  112.0 37.6 %collective-permute-start.14 = (bf16[2,256,1536]{2,1,0:T(8,128)(2,1)}, bf16[2,256,1536]{2,1,0:T(8,128)(2,1)}, u32[]{:S(2)}, u32[]{:S(2)}) collective-permute-start(bf16[2,256,1536]{2,1,0:T(8,128)(2,1)} %fusion.16), channel_id=1, source_target_pairs={{0,2},{2,0},{1,3},{3,1},{4,6},{6,4},{5,7},{7,5},{8,10},{10,8},{9,1... | collective-permute-start | bytes 4718600 | tf_op jit(solution)/shard_map/ppermute | solution.py:329
  116.2 62.9 %collective-permute-start.11 = (bf16[2,256,1536]{2,1,0:T(8,128)(2,1)}, bf16[2,256,1536]{2,1,0:T(8,128)(2,1)}, u32[]{:S(2)}, u32[]{:S(2)}) collective-permute-start(bf16[2,256,1536]{2,1,0:T(8,128)(2,1)} %pad_maximum_fusion.9), channel_id=1, source_target_pairs={{0,16},{16,0},{1,17},{17,1},{2,18},{18,2},{3,19},{19,3},{4,20},{20... | collective-permute-start | bytes 4718600 | tf_op jit(solution)/shard_map/ppermute | solution.py:329
  116.7 63.3 %collective-permute-start.12 = (bf16[2,256,1536]{2,1,0:T(8,128)(2,1)}, bf16[2,256,1536]{2,1,0:T(8,128)(2,1)}, u32[]{:S(2)}, u32[]{:S(2)}) collective-permute-start(bf16[2,256,1536]{2,1,0:T(8,128)(2,1)} %pad_maximum_fusion.9), channel_id=1, source_target_pairs={{0,2},{2,0},{1,3},{3,1},{4,6},{6,4},{5,7},{7,5},{8,10},{10,8},{9,1... | collective-permute-start | bytes 4718600 | tf_op jit(solution)/shard_map/ppermute | solution.py:329
  222.7 160.6 %all-gather.21.cloned.1.call-start = ((), (), s32[]{:S(2)}) async-start(), calls=%async_computation.17 | async-start | bytes 5308416 | tf_op jit(solution)/shard_map/all_gather | solution.py:601
  231.6 207.7 %all-gather.11.cloned.1.call-start = ((), (), s32[]{:S(2)}) async-start(), calls=%async_computation.6 | async-start | bytes 5308416 | tf_op jit(solution)/shard_map/all_gather | solution.py:598
  232.2 212.0 %all-gather.19.cloned.1.call-start = ((), (), s32[]{:S(2)}) async-start(), calls=%async_computation.16 | async-start | bytes 5308416 | tf_op jit(solution)/shard_map/all_gather | solution.py:601
  285.6 39.4 %collective-permute-start.23 = (bf16[1,256,1536]{2,1,0:T(8,128)(2,1)}, bf16[1,256,1536]{2,1,0:T(8,128)(2,1)}, u32[]{:S(2)}, u32[]{:S(2)}) collective-permute-start(bf16[1,256,1536]{2,1,0:T(8,128)(2,1)} %slice.730), channel_id=1, source_target_pairs={{0,2},{2,0},{1,3},{3,1},{4,6},{6,4},{5,7},{7,5},{8,10},{10,8},{9,1... | collective-permute-start | bytes 2359304 | tf_op jit(solution)/shard_map/ppermute | solution.py:329
  289.4 35.6 %collective-permute-start.24 = (bf16[1,256,1536]{2,1,0:T(8,128)(2,1)}, bf16[1,256,1536]{2,1,0:T(8,128)(2,1)}, u32[]{:S(2)}, u32[]{:S(2)}) collective-permute-start(bf16[1,256,1536]{2,1,0:T(8,128)(2,1)} %slice.731), channel_id=1, source_target_pairs={{0,16},{16,0},{1,17},{17,1},{2,18},{18,2},{3,19},{19,3},{4,20},{20... | collective-permute-start | bytes 2359304 | tf_op jit(solution)/shard_map/ppermute | solution.py:329
  291.1 491.5 %reduce-scatter.11.cloned.1.call-start = ((), (), s32[]{:S(2)}) async-start(), calls=%async_computation.10 | async-start | bytes 5308416 | tf_op jit(solution)/shard_map/reduce_scatter | solution.py:694
  439.3 343.4 %reduce-scatter.7.cloned.1.call-start = ((), (), s32[]{:S(2)}) async-start(), calls=%async_computation.8 | async-start | bytes 5308416 | tf_op jit(solution)/shard_map/reduce_scatter | solution.py:678
  529.7 252.9 %reduce-scatter.13.cloned.1.call-start = ((), (), s32[]{:S(2)}) async-start(), calls=%async_computation.11 | async-start | bytes 5308416 | tf_op jit(solution)/shard_map/reduce_scatter | solution.py:694
  559.5 223.2 %reduce-scatter.9.cloned.1.call-start = ((), (), s32[]{:S(2)}) async-start(), calls=%async_computation.9 | async-start | bytes 5308416 | tf_op jit(solution)/shard_map/reduce_scatter | solution.py:678
  606.9 265.3 %reduce-scatter.15.cloned.1.call-start = ((), (), s32[]{:S(2)}) async-start(), calls=%async_computation.12 | async-start | bytes 7962624 | tf_op jit(solution)/shard_map/reduce_scatter | solution.py:778
  666.2 38.6 %collective-permute-start.47 = (bf16[1,256,1536]{2,1,0:T(8,128)(2,1)}, bf16[1,256,1536]{2,1,0:T(8,128)(2,1)S(1)}, u32[]{:S(2)}, u32[]{:S(2)}) collective-permute-start(bf16[1,256,1536]{2,1,0:T(8,128)(2,1)} %add_convert_fusion.6), channel_id=1, source_target_pairs={{0,2},{2,0},{1,3},{3,1},{4,6},{6,4},{5,7},{7,5},{8,10},{10,8},{9,1... | collective-permute-start | bytes 2359304 | tf_op jit(solution)/shard_map/ppermute | solution.py:329
  669.4 35.4 %collective-permute-start.46 = (bf16[1,256,1536]{2,1,0:T(8,128)(2,1)}, bf16[1,256,1536]{2,1,0:T(8,128)(2,1)S(1)}, u32[]{:S(2)}, u32[]{:S(2)}) collective-permute-start(bf16[1,256,1536]{2,1,0:T(8,128)(2,1)} %add_convert_fusion.7), channel_id=1, source_target_pairs={{0,16},{16,0},{1,17},{17,1},{2,18},{18,2},{3,19},{19,3},{4,20},{20... | collective-permute-start | bytes 2359304 | tf_op jit(solution)/shard_map/ppermute | solution.py:329
  670.8 36.2 %collective-permute-start.45 = (bf16[1,256,1536]{2,1,0:T(8,128)(2,1)}, bf16[1,256,1536]{2,1,0:T(8,128)(2,1)S(1)}, u32[]{:S(2)}, u32[]{:S(2)}) collective-permute-start(bf16[1,256,1536]{2,1,0:T(8,128)(2,1)} %get-tuple-element.328), channel_id=1, source_target_pairs={{0,16},{16,0},{1,17},{17,1},{2,18},{18,2},{3,19},{19,3},{4,20},{20... | collective-permute-start | bytes 2359304 | tf_op jit(solution)/shard_map/ppermute | solution.py:329
  673.4 78.4 %collective-permute-start.50 = (bf16[1,256,1536]{2,1,0:T(8,128)(2,1)}, bf16[1,256,1536]{2,1,0:T(8,128)(2,1)}, u32[]{:S(2)}, u32[]{:S(2)}) collective-permute-start(bf16[1,256,1536]{2,1,0:T(8,128)(2,1)} %slice.818), channel_id=1, source_target_pairs={{0,16},{16,0},{1,17},{17,1},{2,18},{18,2},{3,19},{19,3},{4,20},{20... | collective-permute-start | bytes 2359304 | tf_op jit(solution)/shard_map/ppermute | solution.py:329
  704.8 47.9 %collective-permute-start.52 = (bf16[2,4,2,96,1536]{4,3,2,1,0:T(8,128)(2,1)}, bf16[2,4,2,96,1536]{4,3,2,1,0:T(8,128)(2,1)}, u32[]{:S(2)}, u32[]{:S(2)}) collective-permute-start(bf16[2,4,2,96,1536]{4,3,2,1,0:T(8,128)(2,1)} %pad_maximum_fusion.2), channel_id=1, source_target_pairs={{0,1},{1,0},{2,3},{3,2},{4,5},{5,4},{6,7},{7,6},{8,9},{9,8},{10,11... | collective-permute-start | bytes 14155784 | tf_op jit(solution)/shard_map/ppermute | solution.py:329
  733.6 43.3 %collective-permute-start.49 = (bf16[1,256,1536]{2,1,0:T(8,128)(2,1)}, bf16[1,256,1536]{2,1,0:T(8,128)(2,1)}, u32[]{:S(2)}, u32[]{:S(2)}) collective-permute-start(bf16[1,256,1536]{2,1,0:T(8,128)(2,1)} %add_convert_fusion.4), channel_id=1, source_target_pairs={{0,2},{2,0},{1,3},{3,1},{4,6},{6,4},{5,7},{7,5},{8,10},{10,8},{9,1... | collective-permute-start | bytes 2359304 | tf_op jit(solution)/shard_map/ppermute | solution.py:329
  776.8 72.4 %collective-permute-start.55 = (bf16[2,4,1,96,1536]{4,3,2,1,0:T(8,128)(2,1)}, bf16[2,4,1,96,1536]{4,3,2,1,0:T(8,128)(2,1)}, u32[]{:S(2)}, u32[]{:S(2)}) collective-permute-start(bf16[2,4,1,96,1536]{4,3,2,1,0:T(8,128)(2,1)} %get-tuple-element.320), channel_id=1, source_target_pairs={{0,2},{2,0},{1,3},{3,1},{4,6},{6,4},{5,7},{7,5},{8,10},{10,8},{9,1... | collective-permute-start | bytes 7077896 | tf_op jit(solution)/shard_map/ppermute | solution.py:329
  778.0 153.1 %reduce-scatter.17.cloned.1.call-start = ((), (), s32[]{:S(2)}) async-start(), calls=%async_computation.13 | async-start | bytes 1474560 | tf_op jit(solution)/shard_map/reduce_scatter | solution.py:818
  785.5 83.3 %collective-permute-start.77 = (bf16[2,192,1536]{2,1,0:T(8,128)(2,1)}, bf16[2,192,1536]{2,1,0:T(8,128)(2,1)}, u32[]{:S(2)}, u32[]{:S(2)}) collective-permute-start(bf16[2,192,1536]{2,1,0:T(8,128)(2,1)} %pad_maximum_fusion.15), channel_id=1, source_target_pairs={{0,16},{16,0},{1,17},{17,1},{2,18},{18,2},{3,19},{19,3},{4,20},{20... | collective-permute-start | bytes 3538952 | tf_op jit(solution)/shard_map/ppermute | solution.py:329
  802.4 38.2 %collective-permute-start.56 = (bf16[2,1,96,1536]{3,2,1,0:T(8,128)(2,1)}, bf16[2,1,96,1536]{3,2,1,0:T(8,128)(2,1)}, u32[]{:S(2)}, u32[]{:S(2)}) collective-permute-start(bf16[2,1,96,1536]{3,2,1,0:T(8,128)(2,1)} %get-tuple-element.406), channel_id=1, source_target_pairs={{0,2},{2,0},{1,3},{3,1},{4,6},{6,4},{5,7},{7,5},{8,10},{10,8},{9,1... | collective-permute-start | bytes 1769480 | tf_op jit(solution)/shard_map/ppermute | solution.py:329
  810.0 67.0 %collective-permute-start.54 = (f32[1,256,1536]{2,1,0:T(8,128)}, f32[1,256,1536]{2,1,0:T(8,128)}, u32[]{:S(2)}, u32[]{:S(2)}) collective-permute-start(f32[1,256,1536]{2,1,0:T(8,128)} %get-tuple-element.327), channel_id=1, source_target_pairs={{0,1},{1,0},{2,3},{3,2},{4,5},{5,4},{6,7},{7,6},{8,9},{9,8},{10,11... | collective-permute-start | bytes 4718600 | tf_op jit(solution)/shard_map/ppermute | solution.py:329
  811.7 45.9 %collective-permute-start.53 = (bf16[1,256,1536]{2,1,0:T(8,128)(2,1)S(1)}, bf16[1,256,1536]{2,1,0:T(8,128)(2,1)S(1)}, u32[]{:S(2)}, u32[]{:S(2)}) collective-permute-start(bf16[1,256,1536]{2,1,0:T(8,128)(2,1)S(1)} %get-tuple-element.379), channel_id=1, source_target_pairs={{0,1},{1,0},{2,3},{3,2},{4,5},{5,4},{6,7},{7,6},{8,9},{9,8},{10,11... | collective-permute-start | bytes 2359304 | tf_op jit(solution)/shard_map/ppermute | solution.py:329
  856.6 41.3 %collective-permute-start.74 = (bf16[1,4,1,96,1536]{4,3,2,1,0:T(8,128)(2,1)}, bf16[1,4,1,96,1536]{4,3,2,1,0:T(8,128)(2,1)}, u32[]{:S(2)}, u32[]{:S(2)}) collective-permute-start(bf16[1,4,1,96,1536]{4,3,2,1,0:T(8,128)(2,1)} %get-tuple-element.338), channel_id=1, source_target_pairs={{0,16},{16,0},{1,17},{17,1},{2,18},{18,2},{3,19},{19,3},{4,20},{20... | collective-permute-start | bytes 3538952 | tf_op jit(solution)/shard_map/ppermute | solution.py:329
  (216 other events, 2038.8 us)
Sparse Core Ops, SparseCore 0:
  23.9 79.9 all-gather.14
  106.0 89.3 all-gather.16
  222.8 53.4 all-gather.12
  277.8 50.5 all-gather.20
  329.8 50.4 all-gather.10
  381.8 50.5 all-gather.18
  439.4 57.6 reduce-scatter.10
  529.8 58.1 reduce-scatter.6
  590.3 53.3 reduce-scatter.12
  645.9 53.3 reduce-scatter.8
  778.1 76.3 reduce-scatter.14
  900.5 30.4 reduce-scatter.16

commit v5 on v4

--- a/solution.py
+++ b/solution.py
@@ -687,7 +687,7 @@
     pre_txt, back_relays = together(pre_txt, back_relays)
     back_last = swap(plus(back_other[:1], back_relays[0]), "x"), swap(plus(back_own[3:4], back_relays[1]), "y")
     up_grad_txt = weight_grad(hidden_two_seqs, pre_txt, streams[1], None)
-    back_last, up_grad_txt = together(back_last, up_grad_txt)
+    back_last, (up_grad_txt, down_grad_img) = together(back_last, (up_grad_txt, down_grad_img))
     grad_hidden_two = sum_square(back_own, (back_last[0], back_first[0]), (back_first[1], back_last[1]))
     grad_up = [owner_rows(up_grad_img), owner_rows(up_grad_txt)]
     grad_down = [
@@ -762,7 +762,9 @@
 
     qkv_grad_img = qkv_grad(0, grad_pairs)
     hidden_first, qkv_grad_img = together(hidden_first, qkv_grad_img)
-    (grad_pairs, proj_received), hidden_first = together((grad_pairs, proj_received), hidden_first)
+    (grad_pairs, proj_received, grad_up), hidden_first = together((grad_pairs, proj_received, grad_up), hidden_first)
+    up_pair = split_swap(replicas(jnp.stack(grad_up)), 1, yi, "y")
+    proj_received, up_kept = together(proj_received, up_pair[0])
     grad_proj = plus(proj_kept, proj_received)
     grad_proj = jnp.concatenate([lax.dynamic_slice_in_dim(grad_proj, position[t], 1, 1) for t in range(4)], 1)
     proj_kept, proj_received = split_swap(grad_proj, 2, yi, "y")
@@ -771,20 +773,22 @@
     cols = grad_qkv.shape[2]
     grad_qkv = grad_qkv.reshape(2, shards, 2, 2, rows, cols).transpose(1, 3, 0, 2, 4, 5)
     grad_qkv = grad_qkv.reshape(2 * shards, 2, 2, rows, cols)
-    hidden_last, (grad_qkv, proj_kept) = together(hidden_last, (grad_qkv, proj_kept))
+    (hidden_last, up_received), (grad_qkv, proj_kept) = together((hidden_last, up_pair[1]), (grad_qkv, proj_kept))
+    up_mine = jnp.concatenate([up_kept, up_received], 1)
     grad_hidden = sum_square(
         hidden_back_own, (hidden_last[0], hidden_first[0]), (hidden_first[1], hidden_last[1])
     )
     grad_qkv = lax.psum_scatter(grad_qkv, ("z", "c"), scatter_dimension=0, tiled=True).reshape(2, 2, rows, cols)
 
-    (mlp_own, grad_up, grad_down), grad_hidden = together((mlp_own, grad_up, grad_down), grad_hidden)
+    (mlp_own, up_mine, grad_down, late_sums), grad_hidden = together(
+        (mlp_own, up_mine, grad_down, (sums_own, sums_other, sums_txt)), grad_hidden
+    )
+    sums_own, sums_other, sums_txt = late_sums
     mlp = sum_square(mlp_own, (mlp_x0, mlp_x1), (mlp_y2, mlp_y3)) + with_bias(downb_full)
     result = ((after + vector(5) * mlp) * live).astype(BF)
-    up_pair = split_swap(replicas(jnp.stack(grad_up)), 1, yi, "y")
     down = replicas(jnp.stack(grad_down))
     down_other = swap(down, "x")
-    grad_hidden_late, (up_kept, down) = together(grad_hidden, (up_pair[0], down))
-    up_pair = up_kept, up_pair[1]
+    grad_hidden_late, down = together(grad_hidden, down)
 
     grad_tokens = grad_after + back_normalize(grad_hidden * (1.0 + vector(1)), normed, spread_one)
 
@@ -805,8 +809,6 @@
         ],
         1,
     ).reshape(2, 6 * width)
-    up_pair, sums = together(up_pair, sums)
-    up_mine = jnp.concatenate(up_pair, 1)
     dmod = (sums + swap(sums, "y")).astype(BF)
     proj_received, dmod = together(proj_received, dmod)
     proj_kept, proj_received = split_swap(plus(proj_kept, proj_received), 0, xi, "x")

time: 963 us -> 967 us (level)
    ppermute x56, waiting for transfers between devices: 190 us -> 156 us  [swap(): return lax.ppermute(value, axis, FLIP)]
    ppermute x18, waiting for transfers between devices: 17 us -> 46.7 us  [shift_xor(): lax.ppermute(value, axis, [(i, i ^ bit) for i in range(lax.axis_size(axis...]
    unnamed x326 -> x310, local copies, waits for them, and re-layouts: 49.7 us -> 40.5 us
  transfers between devices with their start and end apart: 91 -> 91, of which waited for: 35 -> 35; matrix products, arithmetic and copies ran while one was open for 41% -> 41% of each run, Pallas kernels for 19% -> 17%
where the time goes in v5:
time: 967 us; the launch traced here: 958 us
  waiting for transfers between devices  224 us (23%)
  Pallas kernels  183 us (19%)
  other arithmetic  181 us (19%)
  local copies, waits for them, and re-layouts  155 us (16%)
  matrix products  102 us (11%)
  starting transfers between devices  87.6 us (9%)
  between operations  25.2 us (3%)
    ppermute x56, waiting for transfers between devices, swap(): return lax.ppermute(value, axis, FLIP)  156 us
    dot_general x8, matrix products, two_sums(): jnp.einsum('btd,bte->de', left, right, preferred_element_type=F32)  54 us
    ppermute x56, starting transfers between devices, swap(): return lax.ppermute(value, axis, FLIP)  53.4 us
    pallas_call x2, Pallas kernels, attend_backward(): pl.pallas_call(lambda *refs: attend_backward_kernel(*refs, heads=heads, s...  52.4 us
    ppermute x18, waiting for transfers between devices, shift_xor(): lax.ppermute(value, axis, [(i, i ^ bit) for i in range(lax.axis_size(axis...  46.7 us
    pallas_call x3, Pallas kernels, feed_forward_hidden(): pl.pallas_call(lambda *refs: hidden_kernel(*refs, count=count), grid=(ff...  43.1 us
    unnamed x310, local copies, waits for them, and re-layouts  40.5 us
    pallas_call x3, Pallas kernels, feed_forward_output(): pl.pallas_call(lambda *refs: output_kernel(*refs, count=count), grid=(wid...  33.8 us
  transfers between devices with their start and end apart: 91, of which 35 were waited for; matrix products, arithmetic and copies ran while one was open for 41% of the time, Pallas kernels for 17%

profile of v5, /device:TPU:0, one launch (start us, length us, event | category | flops | bytes accessed | tf_op | source)
XLA Modules:
  0.0 957.6 jit_solution(14167249368630993109)
XLA Ops:
  12.5 10.2 %collective-permute-done.18 = bf16[2,96,1152]{2,1,0:T(8,128)(2,1)S(1)} collective-permute-done((bf16[2,96,1152]{2,1,0:T(8,128)(2,1)S(1)}, bf16[2,96,1152]{2,1,0:T(8,128)(2,1)S(1)}, u32[]{:S(2)}, u32[]{:S(2)}) %collective-permute-start.18) | collective-permute-done | bytes 442400 | tf_op jit(solution)/shard_map/ppermute | solution.py:329
  30.0 10.6 %collective-permute-done.22 = bf16[2,96,1536]{2,1,0:T(8,128)(2,1)} collective-permute-done((bf16[2,96,1536]{2,1,0:T(8,128)(2,1)}, bf16[2,96,1536]{2,1,0:T(8,128)(2,1)}, u32[]{:S(2)}, u32[]{:S(2)}) %collective-permute-start.22) | collective-permute-done | bytes 589856 | tf_op jit(solution)/shard_map/ppermute | solution.py:329
  120.8 27.4 %collective-permute-done.13 = bf16[2,256,1536]{2,1,0:T(8,128)(2,1)} collective-permute-done((bf16[2,256,1536]{2,1,0:T(8,128)(2,1)}, bf16[2,256,1536]{2,1,0:T(8,128)(2,1)}, u32[]{:S(2)}, u32[]{:S(2)}) %collective-permute-start.13) | collective-permute-done | bytes 1572896 | tf_op jit(solution)/shard_map/ppermute | solution.py:329
  149.6 29.4 %collective-permute-done.11 = bf16[2,256,1536]{2,1,0:T(8,128)(2,1)} collective-permute-done((bf16[2,256,1536]{2,1,0:T(8,128)(2,1)}, bf16[2,256,1536]{2,1,0:T(8,128)(2,1)}, u32[]{:S(2)}, u32[]{:S(2)}) %collective-permute-start.11) | collective-permute-done | bytes 1572896 | tf_op jit(solution)/shard_map/ppermute | solution.py:329
  188.8 8.5 collective-permute-done.15
  235.3 16.6 %attend_forward.2 = (bf16[4,256,384]{2,1,0:T(8,128)(2,1)S(1)}, f32[6,1024]{1,0:T(8,128)S(1)}) custom-call(bf16[4,224,1152]{2,1,0:T(8,128)(2,1)S(1)} %copy-done.31, bf16[4,32,1152]{2,1,0:T(8,128)(2,1)S(1)} %copy-done.13), custom_call_target="tpu_custom_call" | custom-call | flops 14495514624 | bytes 4718592 | tf_op jit(solution)/shard_map/attend_forward/pallas_call | solution.py:117
  258.5 16.6 %attend_forward.3 = (bf16[4,256,384]{2,1,0:T(8,128)(2,1)S(1)}, f32[6,1024]{1,0:T(8,128)S(1)}) custom-call(bf16[4,224,1152]{2,1,0:T(8,128)(2,1)S(1)} %fusion.14.refs_0_, bf16[4,32,1152]{2,1,0:T(8,128)(2,1)S(1)} %fusion.34.refs_1_), custom_call_target="tpu_custom_call" | custom-call | flops 14495514624 | bytes 4718592 | tf_op jit(solution)/shard_map/attend_forward/pallas_call | solution.py:117
  288.0 8.8 collective-permute-done.21
  330.9 23.5 %collective-permute-done.26 = bf16[2,256,1536]{2,1,0:T(8,128)(2,1)} collective-permute-done((bf16[2,256,1536]{2,1,0:T(8,128)(2,1)}, bf16[2,256,1536]{2,1,0:T(8,128)(2,1)}, u32[]{:S(2)}, u32[]{:S(2)}) %collective-permute-start.26) | collective-permute-done | bytes 1572896 | tf_op jit(solution)/shard_map/ppermute | solution.py:329
  388.8 16.6 %feed_forward_hidden.4 = (bf16[4,224,1536]{2,1,0:T(8,128)(2,1)S(1)}, bf16[4,224,1536]{2,1,0:T(8,128)(2,1)S(1)}, f32[1,1536]{1,0:T(1,128)S(1)}) custom-call(bf16[4,256,1536]{2,1,0:T(8,128)(2,1)} %constant_dynamic-update-slice_fusion.4.refs_0_, bf16[4,256,1536]{2,1,0:T(8,128)(2,1)} %multiply_convert_fusion.1.refs_2_.refs_1_, bf16[1536,1536]{1,0:T(8,128)(2,1)} %bitcast.271, ...), custom_call_target="tpu_custom_call" | custom-call | flops 16911433728 | bytes 20447232 | tf_op jit(solution)/shard_map/feed_forward_hidden/pallas_call | solution.py:200
  405.4 18.4 %feed_forward_hidden.5 = (bf16[4,224,1536]{2,1,0:T(8,128)(2,1)S(1)}, bf16[4,224,1536]{2,1,0:T(8,128)(2,1)S(1)}, f32[1,1536]{1,0:T(1,128)S(1)}) custom-call(bf16[4,256,1536]{2,1,0:T(8,128)(2,1)} %constant_dynamic-update-slice_fusion.6.refs_1_.refs_0_, bf16[4,256,1536]{2,1,0:T(8,128)(2,1)} %multiply_convert_fusion.refs_3_.refs_1_, ...), custom_call_target="tpu_custom_call" | custom-call | flops 16911433728 | bytes 20447232 | tf_op jit(solution)/shard_map/feed_forward_hidden/pallas_call | solution.py:200
  423.9 13.5 %feed_forward_output.4 = (bf16[4,256,1536]{2,1,0:T(8,128)(2,1)}, bf16[4,256,1536]{2,1,0:T(8,128)(2,1)}) custom-call(bf16[4,224,1536]{2,1,0:T(8,128)(2,1)S(1)} %get-tuple-element.182.refs_0_, bf16[4,224,1536]{2,1,0:T(8,128)(2,1)S(1)} %get-tuple-element.196.refs_1_, bf16[1536,1536]{1,0:T(8,128)(2,1)} %bitcast.273, bf16[1536,1536]{1,0:T(8,128)(2,1)} %bitcast.320), custom_call_target="tpu_custom_call" | custom-call | flops 16911433728 | bytes 20447232 | tf_op jit(solution)/shard_map/feed_forward_output/pallas_call | solution.py:231
  437.4 12.3 %feed_forward_output.3 = (bf16[4,256,1536]{2,1,0:T(8,128)(2,1)}, bf16[4,256,1536]{2,1,0:T(8,128)(2,1)}) custom-call(bf16[4,224,1536]{2,1,0:T(8,128)(2,1)S(1)} %get-tuple-element.179.refs_0_, bf16[4,224,1536]{2,1,0:T(8,128)(2,1)S(1)} %get-tuple-element.195.refs_1_, bf16[1536,1536]{1,0:T(8,128)(2,1)} %bitcast.274, bf16[1536,1536]{1,0:T(8,128)(2,1)} %bitcast.321), custom_call_target="tpu_custom_call" | custom-call | flops 16911433728 | bytes 20447232 | tf_op jit(solution)/shard_map/feed_forward_output/pallas_call | solution.py:231
  449.8 8.1 feed_forward_hidden.3
  458.0 8.0 feed_forward_output.5
  466.0 10.7 %fusion.27 = f32[1536,1536,1]{1,0,2:T(8,128)} fusion(bf16[4,224,1536]{2,1,0:T(8,128)(2,1)S(1)} %copy-done.30, bf16[4,256,1536]{2,1,0:T(8,128)(2,1)} %constant_dynamic-update-slice_fusion.4.refs_0_), kind=kOutput, calls=%fused_computation.82 | convolution fusion | flops 4227858432 | bytes 14942208 | tf_op jit(solution)/shard_map/btd,bte->de/dot_general | solution.py:671
  489.9 8.9 fusion.2
  499.6 10.8 %collective-permute-done.33 = bf16[1,256,1536]{2,1,0:T(8,128)(2,1)} collective-permute-done((bf16[1,256,1536]{2,1,0:T(8,128)(2,1)}, bf16[1,256,1536]{2,1,0:T(8,128)(2,1)}, u32[]{:S(2)}, u32[]{:S(2)}) %collective-permute-start.33) | collective-permute-done | bytes 786464 | tf_op jit(solution)/shard_map/ppermute | solution.py:329
  512.9 7.9 fusion.24
  528.0 7.4 fusion.1
  537.5 5.6 weight_grad.3
  614.1 26.3 %attend_backward.2 = (bf16[4,224,1152]{2,1,0:T(8,128)(2,1)S(1)}, bf16[4,32,1152]{2,1,0:T(8,128)(2,1)S(1)}, f32[2,1152]{1,0:T(2,128)S(1)}) custom-call(bf16[4,224,1152]{2,1,0:T(8,128)(2,1)S(1)} %copy-done.34, bf16[4,32,1152]{2,1,0:T(8,128)(2,1)S(1)} %copy-done.16, f32[6,1024]{1,0:T(8,128)S(1)} %copy-done.38, bf16[4,256,384]{2,1,0:T(8,128)(2,1)S(1)} %pad_maximum_fusion.19.refs_3_), custom_call_target="tpu_custom_call" | custom-call | flops 36238786560 | bytes 4718592 | tf_op jit(solution)/shard_map/attend_backward/pallas_call | solution.py:131
  641.4 7.0 convolution_convert_fusion.1
  665.1 26.1 %attend_backward.3 = (bf16[4,224,1152]{2,1,0:T(8,128)(2,1)S(1)}, bf16[4,32,1152]{2,1,0:T(8,128)(2,1)S(1)}, f32[2,1152]{1,0:T(2,128)S(1)}) custom-call(bf16[4,224,1152]{2,1,0:T(8,128)(2,1)S(1)} %copy-done.32, bf16[4,32,1152]{2,1,0:T(8,128)(2,1)S(1)} %copy-done.14, f32[6,1024]{1,0:T(8,128)S(1)} %copy-done.36, bf16[4,256,384]{2,1,0:T(8,128)(2,1)S(1)} %pad_maximum_fusion.18.refs_3_), custom_call_target="tpu_custom_call" | custom-call | flops 36238786560 | bytes 4718592 | tf_op jit(solution)/shard_map/attend_backward/pallas_call | solution.py:131
  714.1 6.8 convolution_bitcast_fusion.4
  720.9 5.9 fusion.5
  769.9 6.5 fusion.22
  806.5 7.0 collective-permute-done.70
  814.5 6.2 collective-permute-start.71
  829.8 8.6 collective-permute-done.72
  863.7 13.0 %collective-permute-done.60 = bf16[4,2,9216]{2,1,0:T(2,128)(2,1)S(1)} collective-permute-done((bf16[4,2,9216]{2,1,0:T(2,128)(2,1)S(1)}, bf16[4,2,9216]{2,1,0:T(2,128)(2,1)S(1)}, u32[]{:S(2)}, u32[]{:S(2)}) %collective-permute-start.60) | collective-permute-done | bytes 147488 | tf_op jit(solution)/shard_map/ppermute | solution.py:333
  937.0 8.4 collective-permute-done.68.others_ref
  (766 shorter events, 530.4 us)
Async XLA Ops:
  7.2 199.2 %all-gather.15.cloned.1.call-start = ((), (), s32[]{:S(2)}) async-start(), calls=%async_computation.14 | async-start | bytes 7962624 | tf_op jit(solution)/shard_map/all_gather | solution.py:514
  23.8 276.6 %all-gather.17.cloned.1.call-start = ((), (), s32[]{:S(2)}) async-start(), calls=%async_computation.15 | async-start | bytes 10616832 | tf_op jit(solution)/shard_map/all_gather | solution.py:571
  43.1 335.2 %all-gather.13.cloned.1.call-start = ((), (), s32[]{:S(2)}) async-start(), calls=%async_computation.7 | async-start | bytes 5308416 | tf_op jit(solution)/shard_map/all_gather | solution.py:598
  46.9 56.9 %collective-permute-start = (bf16[1,256,1536]{2,1,0:T(8,128)(2,1)}, bf16[1,256,1536]{2,1,0:T(8,128)(2,1)}, u32[]{:S(2)}, u32[]{:S(2)}) collective-permute-start(bf16[1,256,1536]{2,1,0:T(8,128)(2,1)} %get-tuple-element.409), channel_id=1, source_target_pairs={{0,1},{1,0},{2,3},{3,2},{4,5},{5,4},{6,7},{7,6},{8,9},{9,8},{10,11... | collective-permute-start | bytes 2359304 | tf_op jit(solution)/shard_map/ppermute | solution.py:329
  56.1 57.3 %collective-permute-start.10 = (bf16[1,256,1536]{2,1,0:T(8,128)(2,1)}, bf16[1,256,1536]{2,1,0:T(8,128)(2,1)}, u32[]{:S(2)}, u32[]{:S(2)}) collective-permute-start(bf16[1,256,1536]{2,1,0:T(8,128)(2,1)} %get-tuple-element.411), channel_id=1, source_target_pairs={{0,1},{1,0},{2,3},{3,2},{4,5},{5,4},{6,7},{7,6},{8,9},{9,8},{10,11... | collective-permute-start | bytes 2359304 | tf_op jit(solution)/shard_map/ppermute | solution.py:329
  110.5 37.7 %collective-permute-start.13 = (bf16[2,256,1536]{2,1,0:T(8,128)(2,1)}, bf16[2,256,1536]{2,1,0:T(8,128)(2,1)}, u32[]{:S(2)}, u32[]{:S(2)}) collective-permute-start(bf16[2,256,1536]{2,1,0:T(8,128)(2,1)} %fusion.16), channel_id=1, source_target_pairs={{0,16},{16,0},{1,17},{17,1},{2,18},{18,2},{3,19},{19,3},{4,20},{20... | collective-permute-start | bytes 4718600 | tf_op jit(solution)/shard_map/ppermute | solution.py:329
  111.9 37.6 %collective-permute-start.14 = (bf16[2,256,1536]{2,1,0:T(8,128)(2,1)}, bf16[2,256,1536]{2,1,0:T(8,128)(2,1)}, u32[]{:S(2)}, u32[]{:S(2)}) collective-permute-start(bf16[2,256,1536]{2,1,0:T(8,128)(2,1)} %fusion.16), channel_id=1, source_target_pairs={{0,2},{2,0},{1,3},{3,1},{4,6},{6,4},{5,7},{7,5},{8,10},{10,8},{9,1... | collective-permute-start | bytes 4718600 | tf_op jit(solution)/shard_map/ppermute | solution.py:329
  116.0 63.0 %collective-permute-start.11 = (bf16[2,256,1536]{2,1,0:T(8,128)(2,1)}, bf16[2,256,1536]{2,1,0:T(8,128)(2,1)}, u32[]{:S(2)}, u32[]{:S(2)}) collective-permute-start(bf16[2,256,1536]{2,1,0:T(8,128)(2,1)} %pad_maximum_fusion.9), channel_id=1, source_target_pairs={{0,16},{16,0},{1,17},{17,1},{2,18},{18,2},{3,19},{19,3},{4,20},{20... | collective-permute-start | bytes 4718600 | tf_op jit(solution)/shard_map/ppermute | solution.py:329
  116.6 63.3 %collective-permute-start.12 = (bf16[2,256,1536]{2,1,0:T(8,128)(2,1)}, bf16[2,256,1536]{2,1,0:T(8,128)(2,1)}, u32[]{:S(2)}, u32[]{:S(2)}) collective-permute-start(bf16[2,256,1536]{2,1,0:T(8,128)(2,1)} %pad_maximum_fusion.9), channel_id=1, source_target_pairs={{0,2},{2,0},{1,3},{3,1},{4,6},{6,4},{5,7},{7,5},{8,10},{10,8},{9,1... | collective-permute-start | bytes 4718600 | tf_op jit(solution)/shard_map/ppermute | solution.py:329
  222.7 160.5 %all-gather.11.cloned.1.call-start = ((), (), s32[]{:S(2)}) async-start(), calls=%async_computation.6 | async-start | bytes 5308416 | tf_op jit(solution)/shard_map/all_gather | solution.py:598
  223.2 164.9 %all-gather.21.cloned.1.call-start = ((), (), s32[]{:S(2)}) async-start(), calls=%async_computation.17 | async-start | bytes 5308416 | tf_op jit(solution)/shard_map/all_gather | solution.py:601
  232.2 217.6 %all-gather.19.cloned.1.call-start = ((), (), s32[]{:S(2)}) async-start(), calls=%async_computation.16 | async-start | bytes 5308416 | tf_op jit(solution)/shard_map/all_gather | solution.py:601
  282.4 37.2 %collective-permute-start.23 = (bf16[1,256,1536]{2,1,0:T(8,128)(2,1)}, bf16[1,256,1536]{2,1,0:T(8,128)(2,1)}, u32[]{:S(2)}, u32[]{:S(2)}) collective-permute-start(bf16[1,256,1536]{2,1,0:T(8,128)(2,1)} %slice.730), channel_id=1, source_target_pairs={{0,2},{2,0},{1,3},{3,1},{4,6},{6,4},{5,7},{7,5},{8,10},{10,8},{9,1... | collective-permute-start | bytes 2359304 | tf_op jit(solution)/shard_map/ppermute | solution.py:329
  319.6 40.4 %collective-permute-start.25 = (bf16[2,256,1536]{2,1,0:T(8,128)(2,1)}, bf16[2,256,1536]{2,1,0:T(8,128)(2,1)}, u32[]{:S(2)}, u32[]{:S(2)}) collective-permute-start(bf16[2,256,1536]{2,1,0:T(8,128)(2,1)} %add_convert_fusion.2), channel_id=1, source_target_pairs={{0,2},{2,0},{1,3},{3,1},{4,6},{6,4},{5,7},{7,5},{8,10},{10,8},{9,1... | collective-permute-start | bytes 4718600 | tf_op jit(solution)/shard_map/ppermute | solution.py:329
  322.3 407.9 %reduce-scatter.7.cloned.1.call-start = ((), (), s32[]{:S(2)}) async-start(), calls=%async_computation.8 | async-start | bytes 5308416 | tf_op jit(solution)/shard_map/reduce_scatter | solution.py:678
  512.9 217.4 %reduce-scatter.9.cloned.1.call-start = ((), (), s32[]{:S(2)}) async-start(), calls=%async_computation.9 | async-start | bytes 5308416 | tf_op jit(solution)/shard_map/reduce_scatter | solution.py:678
  548.1 221.8 %reduce-scatter.13.cloned.1.call-start = ((), (), s32[]{:S(2)}) async-start(), calls=%async_computation.11 | async-start | bytes 5308416 | tf_op jit(solution)/shard_map/reduce_scatter | solution.py:694
  548.9 221.0 %reduce-scatter.11.cloned.1.call-start = ((), (), s32[]{:S(2)}) async-start(), calls=%async_computation.10 | async-start | bytes 5308416 | tf_op jit(solution)/shard_map/reduce_scatter | solution.py:694
  598.7 282.8 %reduce-scatter.15.cloned.1.call-start = ((), (), s32[]{:S(2)}) async-start(), calls=%async_computation.12 | async-start | bytes 7962624 | tf_op jit(solution)/shard_map/reduce_scatter | solution.py:781
  658.6 37.7 %collective-permute-start.47 = (bf16[1,256,1536]{2,1,0:T(8,128)(2,1)}, bf16[1,256,1536]{2,1,0:T(8,128)(2,1)S(1)}, u32[]{:S(2)}, u32[]{:S(2)}) collective-permute-start(bf16[1,256,1536]{2,1,0:T(8,128)(2,1)} %add_convert_fusion.6), channel_id=1, source_target_pairs={{0,2},{2,0},{1,3},{3,1},{4,6},{6,4},{5,7},{7,5},{8,10},{10,8},{9,1... | collective-permute-start | bytes 2359304 | tf_op jit(solution)/shard_map/ppermute | solution.py:329
  660.9 35.3 %collective-permute-start.46 = (bf16[1,256,1536]{2,1,0:T(8,128)(2,1)}, bf16[1,256,1536]{2,1,0:T(8,128)(2,1)S(1)}, u32[]{:S(2)}, u32[]{:S(2)}) collective-permute-start(bf16[1,256,1536]{2,1,0:T(8,128)(2,1)} %add_convert_fusion.7), channel_id=1, source_target_pairs={{0,16},{16,0},{1,17},{17,1},{2,18},{18,2},{3,19},{19,3},{4,20},{20... | collective-permute-start | bytes 2359304 | tf_op jit(solution)/shard_map/ppermute | solution.py:329
  661.2 35.1 %collective-permute-start.44 = (bf16[1,256,1536]{2,1,0:T(8,128)(2,1)}, bf16[1,256,1536]{2,1,0:T(8,128)(2,1)}, u32[]{:S(2)}, u32[]{:S(2)}) collective-permute-start(bf16[1,256,1536]{2,1,0:T(8,128)(2,1)} %get-tuple-element.337), channel_id=1, source_target_pairs={{0,2},{2,0},{1,3},{3,1},{4,6},{6,4},{5,7},{7,5},{8,10},{10,8},{9,1... | collective-permute-start | bytes 2359304 | tf_op jit(solution)/shard_map/ppermute | solution.py:329
  662.1 34.9 %collective-permute-start.45 = (bf16[1,256,1536]{2,1,0:T(8,128)(2,1)}, bf16[1,256,1536]{2,1,0:T(8,128)(2,1)}, u32[]{:S(2)}, u32[]{:S(2)}) collective-permute-start(bf16[1,256,1536]{2,1,0:T(8,128)(2,1)} %get-tuple-element.336), channel_id=1, source_target_pairs={{0,16},{16,0},{1,17},{17,1},{2,18},{18,2},{3,19},{19,3},{4,20},{20... | collective-permute-start | bytes 2359304 | tf_op jit(solution)/shard_map/ppermute | solution.py:329
  664.7 65.5 %collective-permute-start.49 = (bf16[1,256,1536]{2,1,0:T(8,128)(2,1)}, bf16[1,256,1536]{2,1,0:T(8,128)(2,1)}, u32[]{:S(2)}, u32[]{:S(2)}) collective-permute-start(bf16[1,256,1536]{2,1,0:T(8,128)(2,1)} %slice.817), channel_id=1, source_target_pairs={{0,16},{16,0},{1,17},{17,1},{2,18},{18,2},{3,19},{19,3},{4,20},{20... | collective-permute-start | bytes 2359304 | tf_op jit(solution)/shard_map/ppermute | solution.py:329
  708.1 48.6 %collective-permute-start.52 = (bf16[1,256,1536]{2,1,0:T(8,128)(2,1)}, bf16[1,256,1536]{2,1,0:T(8,128)(2,1)}, u32[]{:S(2)}, u32[]{:S(2)}) collective-permute-start(bf16[1,256,1536]{2,1,0:T(8,128)(2,1)} %add_convert_fusion.4), channel_id=1, source_target_pairs={{0,2},{2,0},{1,3},{3,1},{4,6},{6,4},{5,7},{7,5},{8,10},{10,8},{9,1... | collective-permute-start | bytes 2359304 | tf_op jit(solution)/shard_map/ppermute | solution.py:329
  711.1 45.5 %collective-permute-start.51 = (bf16[1,256,1536]{2,1,0:T(8,128)(2,1)}, bf16[1,256,1536]{2,1,0:T(8,128)(2,1)}, u32[]{:S(2)}, u32[]{:S(2)}) collective-permute-start(bf16[1,256,1536]{2,1,0:T(8,128)(2,1)} %add_convert_fusion.5), channel_id=1, source_target_pairs={{0,16},{16,0},{1,17},{17,1},{2,18},{18,2},{3,19},{19,3},{4,20},{20... | collective-permute-start | bytes 2359304 | tf_op jit(solution)/shard_map/ppermute | solution.py:329
  755.8 93.2 %collective-permute-start.56 = (bf16[2,4,1,96,1536]{4,3,2,1,0:T(8,128)(2,1)}, bf16[2,4,1,96,1536]{4,3,2,1,0:T(8,128)(2,1)}, u32[]{:S(2)}, u32[]{:S(2)}) collective-permute-start(bf16[2,4,1,96,1536]{4,3,2,1,0:T(8,128)(2,1)} %get-tuple-element.328), channel_id=1, source_target_pairs={{0,2},{2,0},{1,3},{3,1},{4,6},{6,4},{5,7},{7,5},{8,10},{10,8},{9,1... | collective-permute-start | bytes 7077896 | tf_op jit(solution)/shard_map/ppermute | solution.py:329
  778.9 70.1 %collective-permute-start.77 = (bf16[2,192,1536]{2,1,0:T(8,128)(2,1)}, bf16[2,192,1536]{2,1,0:T(8,128)(2,1)}, u32[]{:S(2)}, u32[]{:S(2)}) collective-permute-start(bf16[2,192,1536]{2,1,0:T(8,128)(2,1)} %pad_maximum_fusion.16), channel_id=1, source_target_pairs={{0,16},{16,0},{1,17},{17,1},{2,18},{18,2},{3,19},{19,3},{4,20},{20... | collective-permute-start | bytes 3538952 | tf_op jit(solution)/shard_map/ppermute | solution.py:329
  788.4 141.8 %reduce-scatter.17.cloned.1.call-start = ((), (), s32[]{:S(2)}) async-start(), calls=%async_computation.13 | async-start | bytes 1474560 | tf_op jit(solution)/shard_map/reduce_scatter | solution.py:820
  824.7 61.1 %collective-permute-start.55 = (f32[1,256,1536]{2,1,0:T(8,128)}, f32[1,256,1536]{2,1,0:T(8,128)}, u32[]{:S(2)}, u32[]{:S(2)}) collective-permute-start(f32[1,256,1536]{2,1,0:T(8,128)} %get-tuple-element.335), channel_id=1, source_target_pairs={{0,1},{1,0},{2,3},{3,2},{4,5},{5,4},{6,7},{7,6},{8,9},{9,8},{10,11... | collective-permute-start | bytes 4718600 | tf_op jit(solution)/shard_map/ppermute | solution.py:329
  843.8 47.0 %collective-permute-start.76 = (bf16[2,2,96,1536]{3,2,1,0:T(8,128)(2,1)}, bf16[2,2,96,1536]{3,2,1,0:T(8,128)(2,1)}, u32[]{:S(2)}, u32[]{:S(2)}) collective-permute-start(bf16[2,2,96,1536]{3,2,1,0:T(8,128)(2,1)} %pad_maximum_fusion.15.mine_ref), channel_id=1, source_target_pairs={{0,16},{16,0},{1,17},{17,1},{2,18},{18,2},{3,19},{19,3},{4,20},{20... | collective-permute-start | bytes 3538952 | tf_op jit(solution)/shard_map/ppermute | solution.py:329
  852.4 50.4 %collective-permute-start.78 = (bf16[2,192,1536]{2,1,0:T(8,128)(2,1)}, bf16[2,192,1536]{2,1,0:T(8,128)(2,1)}, u32[]{:S(2)}, u32[]{:S(2)}) collective-permute-start(bf16[2,192,1536]{2,1,0:T(8,128)(2,1)} %get-tuple-element.345), channel_id=1, source_target_pairs={{0,1},{1,0},{2,3},{3,2},{4,5},{5,4},{6,7},{7,6},{8,9},{9,8},{10,11... | collective-permute-start | bytes 3538952 | tf_op jit(solution)/shard_map/ppermute | solution.py:329
  (208 other events, 1831.4 us)
Sparse Core Ops, SparseCore 0:
  23.9 79.9 all-gather.14
  106.0 89.3 all-gather.16
  222.8 53.5 all-gather.12
  277.8 50.4 all-gather.10
  329.8 50.5 all-gather.20
  381.9 50.5 all-gather.18
  513.0 58.5 reduce-scatter.6
  574.5 53.3 reduce-scatter.8
  630.2 53.3 reduce-scatter.12
  685.7 53.3 reduce-scatter.10
  788.5 92.9 reduce-scatter.14
  900.2 30.0 reduce-scatter.16
